TPU v7x, 256 devices: a whole 4x4x8 slice. The times are simulated.
256 devices in a mesh: wide: 64 (over x, z, core), narrow: 4 (over y).
Axes of the slice: x: 4, y: 4, z: 8, core: 2. Of those that a mesh axis runs over, the one named last changes fastest.
Arguments:
- activations: bfloat16 [512, 8192], P('wide', 'narrow'), may hold values from -6 to 6
- up_weight: bfloat16 [8192, 28672], P('narrow', 'wide'), may hold values from -0.0625 to 0.0625
- block_mask: int32 [128, 448], P('narrow', 'wide'), may hold values from 0 to 1, as said below
- out_grad: bfloat16 [512, 28672], P('narrow', 'wide'), may hold values from -6 to 6
Outputs:
- output: bfloat16 [512, 28672], P('narrow', 'wide')
- input_grad: bfloat16 [512, 8192], P('wide', 'narrow')
- weight_grad: bfloat16 [8192, 28672], P('narrow', 'wide')
Inputs may be any that keep to these rules, and one draw needn't show every extreme that they name: block_mask holds 0 or 1; the share of kept blocks differs from one block column to another.
All inputs are finite; a program needn't handle non-finite values.
Results may differ from a plain program's by a relative error of at most 0.012.
Values may be sent and summed in bfloat16 or wider, within the bound.
No kernel may reach another device: no remote copies, remote signals or barrier semaphores. Data moves between devices by JAX's collectives and lax.ppermute only.
A program may use at most 64 MiB of HBM per device.

v0:
```python
import jax
import jax.numpy as jnp
from jax import lax
from jax.sharding import Mesh
from jax.sharding import PartitionSpec as P

WIDE = ("wide_0", "wide_1", "wide_2")


def sent_to_all(array, axis):
    copies = jnp.broadcast_to(array, (lax.axis_size(axis), *array.shape))
    return lax.all_to_all(copies, axis, split_axis=0, concat_axis=0, tiled=True)


def in_order(blocks, dim):
    blocks = jnp.moveaxis(blocks, 0, dim)
    dims = blocks.shape
    return blocks.reshape(*dims[:dim], dims[dim] * dims[dim + 1], *dims[dim + 2 :])


def whole_of(array, axes, dim):
    far, near = axes
    blocks = sent_to_all(sent_to_all(array, far), near)
    return in_order(blocks.swapaxes(0, 1).reshape(-1, *array.shape), dim)


def in_blocks(array, dim, devices):
    dims = array.shape
    blocks = array.reshape(*dims[:dim], devices, dims[dim] // devices, *dims[dim + 1 :])
    return jnp.moveaxis(blocks, dim, 0)


def sum_at_owner(array, axis, dim):
    blocks = in_blocks(array, dim, lax.axis_size(axis))
    arrived = lax.all_to_all(blocks, axis, split_axis=0, concat_axis=0, tiled=True)
    return arrived.astype(jnp.float32).sum(axis=0)


def collect(array, axis, dim):
    return in_order(sent_to_all(array, axis), dim)


def sent_and_summed(array, axis, dim):
    blocks = in_blocks(array, dim, lax.axis_size(axis))
    arrived = lax.all_to_all(blocks, axis, split_axis=0, concat_axis=0, tiled=True)
    return arrived.sum(axis=0)


def sum_by_axis(array, axes, dim):
    far, near = axes
    blocks = in_blocks(array, dim, lax.axis_size(far))
    nearer = sent_and_summed(blocks, near, dim + 1)
    arrived = lax.all_to_all(nearer, far, split_axis=0, concat_axis=0, tiled=True)
    return arrived.sum(axis=0)


def apply_mask(weight, blocks):
    rows_b, cols_b = blocks.shape
    side_rows = weight.shape[0] // rows_b
    side_cols = weight.shape[1] // cols_b
    shaped = weight.reshape(rows_b, side_rows, cols_b, side_cols)
    return (shaped * blocks[:, None, :, None].astype(weight.dtype)).reshape(weight.shape)


def on_device(activations, up_weight, block_mask, out_grad):
    masked = apply_mask(up_weight, block_mask)
    gathered = whole_of(activations, (("wide_0", "wide_1"), "wide_2"), 0)
    partial_sum = jnp.dot(gathered, masked, preferred_element_type=jnp.float32)
    output = sum_at_owner(partial_sum.astype(jnp.bfloat16), "narrow", 0).astype(jnp.bfloat16)
    grad_all = collect(out_grad, "narrow", 0)
    input_grad = sum_by_axis(
        lax.dot_general(
            grad_all, masked, (((1,), (1,)), ((), ())), preferred_element_type=jnp.float32
        ),
        (("wide_0", "wide_1"), "wide_2"),
        0,
    ).astype(jnp.bfloat16)
    full_grad = lax.dot_general(
        gathered, grad_all, (((0,), (0,)), ((), ())), preferred_element_type=jnp.float32
    )
    weight_grad = apply_mask(full_grad, block_mask).astype(jnp.bfloat16)
    return (output, input_grad, weight_grad)


def solution(mesh):
    torus = Mesh(
        mesh.devices.reshape(4, 8, 2, mesh.shape["narrow"]),
        ("wide_0", "wide_1", "wide_2", "narrow"),
    )
    return jax.shard_map(
        on_device,
        mesh=torus,
        in_specs=(P(WIDE, "narrow"), P("narrow", WIDE), P("narrow", WIDE), P("narrow", WIDE)),
        out_specs=(P("narrow", WIDE), P(WIDE, "narrow"), P("narrow", WIDE)),
        check_vma=False,
    )
```

profile of v0, /device:TPU:1, one launch (start us, length us, event | category | flops | bytes accessed | tf_op | source)
XLA Modules:
  0.0 141.2 jit_solution(1990724783127503556)
XLA Ops:
  0.6 1.0 broadcast_in_dim.13
  1.6 12.4 %all_to_all.30 = bf16[4,128,448]{1,2,0:T(8,128)(2,1)S(1)} all-to-all(bf16[4,128,448]{1,2,0:T(8,128)(2,1)S(1)} %broadcast_in_dim.13), channel_id=1, replica_groups=mesh['wide_0'=4,'wide_1'=8,'wide_2'=2,'narrow'=4] {'narrow'}, dimensions={0} | all-to-all | bytes 917504 | tf_op jit(solution)/shard_map/all_to_all | solution.py:12
  14.0 1.8 %broadcast_in_dim.11 = bf16[32,8,2048]{2,1,0:T(8,128)(2,1)} broadcast(bf16[8,2048]{1,0:T(8,128)(2,1)} %param.4), dimensions={1,2} | broadcast | bytes 1081344 | tf_op jit(solution)/shard_map/broadcast_in_dim | solution.py:11
  15.9 11.0 %all-to-all-start = ((bf16[32,8,2048]{2,1,0:T(8,128)(2,1)}), bf16[32,8,2048]{2,1,0:T(8,128)(2,1)S(1)}, u32[]{:S(2)}, u32[]{:S(2)}) async-start(bf16[32,8,2048]{2,1,0:T(8,128)(2,1)} %broadcast_in_dim.11), calls=%async_computation | async-start | bytes 2097152 | tf_op jit(solution)/shard_map/all_to_all | solution.py:12
  26.9 2.3 %mul.19 = bf16[32,64,7,64]{1,0,3,2:T(8,128)(2,1)} broadcast(bf16[32,7]{0,1:T(8,128)(2,1)S(1)} %get-tuple-element.4), dimensions={0,2} | broadcast | bytes 1835456 | tf_op jit(solution)/shard_map/mul | solution.py:62
  29.3 5.3 %mul.20 = bf16[2048,448]{0,1:T(8,128)(2,1)S(1)} reshape(bf16[32,64,7,64]{1,0,3,2:T(8,128)(2,1)} %mul.19) | data formatting | bytes 3670016 | tf_op jit(solution)/shard_map/mul | solution.py:62
  34.6 2.8 %fusion.1 = f32[2048,512]{0,1:T(8,128)S(1)} fusion(bf16[2048,448]{0,1:T(8,128)(2,1)} %param.5, bf16[2048,448]{0,1:T(8,128)(2,1)S(1)} %mul.20, bf16[4,128,448]{1,2,0:T(8,128)(2,1)S(1)} %all_to_all.30), kind=kOutput, calls=%fused_computation.4 | convolution fusion | flops 940441600 | bytes 8323072 | tf_op jit(solution)/shard_map/dot_general | solution.py:72
  37.4 2.3 %copy.39 = f32[32,2,8,2048]{3,2,0,1:T(8,128)} copy(f32[32,2,8,2048]{3,2,1,0:T(8,128)S(1)} %bitcast.47) | data formatting | bytes 8388608 | tf_op jit(solution)/shard_map/reshape;reshape | solution.py:29
  39.7 11.4 %all-to-all-done = bf16[32,8,2048]{2,1,0:T(8,128)(2,1)S(1)} async-done(((bf16[32,8,2048]{2,1,0:T(8,128)(2,1)}), bf16[32,8,2048]{2,1,0:T(8,128)(2,1)S(1)}, u32[]{:S(2)}, u32[]{:S(2)}) %all-to-all-start) | async-done | bytes 1048608 | tf_op jit(solution)/shard_map/all_to_all | solution.py:12
  51.4 11.2 %all_to_all.31 = bf16[2,32,8,2048]{3,2,1,0:T(8,128)(2,1)} all-to-all(bf16[2,32,8,2048]{3,2,1,0:T(8,128)(2,1)S(1)} %broadcast_in_dim.12), channel_id=1, replica_groups=mesh['wide_0'=4,'wide_1'=8,'wide_2'=2,'narrow'=4] {'wide_2'}, dimensions={0} | all-to-all | bytes 4194304 | tf_op jit(solution)/shard_map/all_to_all | solution.py:12
  62.6 5.9 %all-to-all-start.4 = ((f32[2,32,8,2048]{3,2,1,0:T(8,128)}), f32[2,32,8,2048]{3,2,1,0:T(8,128)}, u32[]{:S(2)}, u32[]{:S(2)}) async-start(f32[2,32,8,2048]{3,2,1,0:T(8,128)} %bitcast.48), calls=%async_computation.4 | async-start | bytes 8388608 | tf_op jit(solution)/shard_map/all_to_all | solution.py:45
  68.5 1.9 %copy.25 = bf16[2,32,8,2048]{3,2,0,1:T(8,128)(2,1)S(1)} copy(bf16[2,32,8,2048]{3,2,1,0:T(8,128)(2,1)} %all_to_all.31) | data formatting | bytes 4194304 | tf_op jit(solution)/shard_map/all_to_all | solution.py:12
  70.7 1.2 fusion
  71.8 0.8 copy.40
  72.7 3.5 %all-to-all-start.2 = ((bf16[4,128,448]{1,2,0:T(8,128)(2,1)}), bf16[4,128,448]{1,2,0:T(8,128)(2,1)S(1)}, u32[]{:S(2)}, u32[]{:S(2)}) async-start(bf16[4,128,448]{1,2,0:T(8,128)(2,1)} %bitcast.46), calls=%async_computation.2 | async-start | bytes 917504 | tf_op jit(solution)/shard_map/all_to_all | solution.py:35
  76.1 4.1 %reduce_sum.31 = f32[32,8,2048]{2,1,0:T(8,128)} reduce(f32[2,32,8,2048]{3,2,1,0:T(8,128)} %all-to-all-done.4, f32[]{:T(128)} %constant.3.clone.1), dimensions={0}, to_apply=%region_1.0 | reduce | flops 524288 | bytes 6291460 | tf_op jit(solution)/shard_map/reduce_sum | solution.py:46
  80.2 4.4 %all-to-all-done.2 = bf16[4,128,448]{1,2,0:T(8,128)(2,1)S(1)} async-done(((bf16[4,128,448]{1,2,0:T(8,128)(2,1)}), bf16[4,128,448]{1,2,0:T(8,128)(2,1)S(1)}, u32[]{:S(2)}, u32[]{:S(2)}) %all-to-all-start.2) | async-done | bytes 458784 | tf_op jit(solution)/shard_map/all_to_all | solution.py:35
  84.6 5.0 %all-to-all-start.5 = ((f32[32,8,2048]{2,1,0:T(8,128)}), f32[32,8,2048]{2,1,0:T(8,128)}, u32[]{:S(2)}, u32[]{:S(2)}) async-start(f32[32,8,2048]{2,1,0:T(8,128)} %reduce_sum.31), calls=%async_computation.5 | async-start | bytes 4194304 | tf_op jit(solution)/shard_map/all_to_all | solution.py:53
  90.6 2.6 %copy.29 = bf16[2048,512]{1,0:T(8,128)(2,1)} copy(bf16[2048,512]{0,1:T(8,128)(2,1)S(1)} %bitcast.50) | data formatting | bytes 4194304 | tf_op jit(solution)/shard_map/dot_general | solution.py:78
  93.2 5.8 %multiply_convert_fusion = bf16[32,64,7,64]{3,1,2,0:T(8,128)(2,1)} fusion(f32[32,7]{1,0:T(8,128)S(1)} %copy.30, bf16[32,64,512,1]{2,1,3,0:T(8,128)(2,1)} %bitcast.51, bf16[7,64,512,1]{2,1,0,3:T(8,128)(2,1)S(1)} %bitcast.52), kind=kOutput, calls=%fused_computation | convolution fusion | flops 941359104 | bytes 4391808 | tf_op jit(solution)/shard_map/dot_general | solution.py:78
  98.9 7.0 %copy.31 = bf16[32,64,7,64]{1,0,3,2:T(8,128)(2,1)} copy(bf16[32,64,7,64]{3,1,2,0:T(8,128)(2,1)} %multiply_convert_fusion) | data formatting | bytes 3670016 | tf_op jit(solution)/shard_map/convert_element_type | solution.py:81
  106.0 6.2 %convert_element_type.31 = bf16[2048,448]{0,1:T(8,128)(2,1)} reshape(bf16[32,64,7,64]{1,0,3,2:T(8,128)(2,1)} %copy.31) | data formatting | bytes 3670016 | tf_op jit(solution)/shard_map/convert_element_type | solution.py:81
  112.9 26.0 %all-to-all-done.5 = f32[32,8,2048]{2,1,0:T(8,128)} async-done(((f32[32,8,2048]{2,1,0:T(8,128)}), f32[32,8,2048]{2,1,0:T(8,128)}, u32[]{:S(2)}, u32[]{:S(2)}) %all-to-all-start.5) | async-done | bytes 2097184 | tf_op jit(solution)/shard_map/all_to_all | solution.py:53
  138.9 2.3 %reduce_sum.32 = bf16[8,2048]{1,0:T(8,128)(2,1)} reduce(f32[32,8,2048]{2,1,0:T(8,128)} %all-to-all-done.5, f32[]{:T(128)} %constant.3.clone.1), dimensions={0}, to_apply=%region_2.0 | reduce | flops 507904 | bytes 2129924 | tf_op jit(solution)/shard_map/reduce_sum | solution.py:54
  (16 shorter events, 2.1 us)
Async XLA Ops:
  1.6 25.3 %copy-start.4 = (s32[32,7]{0,1:T(8,128)S(1)}, s32[32,7]{0,1:T(8,128)}, u32[]{:S(2)}) copy-start(s32[32,7]{0,1:T(8,128)} %param.6) | copy-start | bytes 2692
  15.9 35.2 %all-to-all-start = ((bf16[32,8,2048]{2,1,0:T(8,128)(2,1)}), bf16[32,8,2048]{2,1,0:T(8,128)(2,1)S(1)}, u32[]{:S(2)}, u32[]{:S(2)}) async-start(bf16[32,8,2048]{2,1,0:T(8,128)(2,1)} %broadcast_in_dim.11), calls=%async_computation | async-start | bytes 2097152 | tf_op jit(solution)/shard_map/all_to_all | solution.py:12
  62.6 10.1 %all-to-all-start.4 = ((f32[2,32,8,2048]{3,2,1,0:T(8,128)}), f32[2,32,8,2048]{3,2,1,0:T(8,128)}, u32[]{:S(2)}, u32[]{:S(2)}) async-start(f32[2,32,8,2048]{3,2,1,0:T(8,128)} %bitcast.48), calls=%async_computation.4 | async-start | bytes 8388608 | tf_op jit(solution)/shard_map/all_to_all | solution.py:45
  68.5 2.1 %copy-start.2 = (bf16[2048,448]{0,1:T(8,128)(2,1)S(1)}, bf16[2048,448]{0,1:T(8,128)(2,1)}, u32[]{:S(2)}) copy-start(bf16[2048,448]{0,1:T(8,128)(2,1)} %param.5) | copy-start | bytes 5505028
  70.4 1.4 %copy-start = (bf16[2,32,8,2048]{3,2,0,1:T(8,128)(2,1)}, bf16[2,32,8,2048]{3,2,0,1:T(8,128)(2,1)S(1)}, u32[]{:S(2)}) copy-start(bf16[2,32,8,2048]{3,2,0,1:T(8,128)(2,1)S(1)} %copy.25) | copy-start | bytes 6291460
  72.7 12.0 %all-to-all-start.2 = ((bf16[4,128,448]{1,2,0:T(8,128)(2,1)}), bf16[4,128,448]{1,2,0:T(8,128)(2,1)S(1)}, u32[]{:S(2)}, u32[]{:S(2)}) async-start(bf16[4,128,448]{1,2,0:T(8,128)(2,1)} %bitcast.46), calls=%async_computation.2 | async-start | bytes 917504 | tf_op jit(solution)/shard_map/all_to_all | solution.py:35
  80.2 10.4 %copy-start.1 = (bf16[2,32,8,2048]{3,2,0,1:T(8,128)(2,1)S(1)}, bf16[2,32,8,2048]{3,2,0,1:T(8,128)(2,1)}, u32[]{:S(2)}) copy-start(bf16[2,32,8,2048]{3,2,0,1:T(8,128)(2,1)} %copy-done) | copy-start | bytes 6291460
  84.6 54.3 %all-to-all-start.5 = ((f32[32,8,2048]{2,1,0:T(8,128)}), f32[32,8,2048]{2,1,0:T(8,128)}, u32[]{:S(2)}, u32[]{:S(2)}) async-start(f32[32,8,2048]{2,1,0:T(8,128)} %reduce_sum.31), calls=%async_computation.5 | async-start | bytes 4194304 | tf_op jit(solution)/shard_map/all_to_all | solution.py:53
  90.6 2.6 %copy-start.3 = (bf16[512,448]{0,1:T(8,128)(2,1)S(1)}, bf16[512,448]{0,1:T(8,128)(2,1)}, u32[]{:S(2)}) copy-start(bf16[512,448]{0,1:T(8,128)(2,1)} %copy_bitcast_fusion.1) | copy-start | bytes 1376260
where the time goes:
time: 142 us; the launch traced here: 141 us
  waiting for transfers between devices  41.9 us (30%)
  local copies, waits for them, and re-layouts  32.7 us (23%)
  starting transfers between devices  25.5 us (18%)
  blocking collectives  23.6 us (17%)
  matrix products  9.71 us (7%)
  other arithmetic  7.1 us (5%)
    all_to_all x1, waiting for transfers between devices, sum_by_axis(): lax.all_to_all(nearer, far, split_axis=0, concat_axis=0, tiled=True)  26 us
    all_to_all x2, blocking collectives, sent_to_all(): return lax.all_to_all(copies, axis, split_axis=0, concat_axis=0, tiled=True)  23.6 us
    convert_element_type x2, local copies, waits for them, and re-layouts, on_device(): weight_grad = apply_mask(full_grad, block_mask).astype(jnp.bfloat16)  13.2 us
    all_to_all x1, waiting for transfers between devices, sent_to_all(): return lax.all_to_all(copies, axis, split_axis=0, concat_axis=0, tiled=True)  11.4 us
    all_to_all x1, starting transfers between devices, sent_to_all(): return lax.all_to_all(copies, axis, split_axis=0, concat_axis=0, tiled=True)  11 us
    mul x2, local copies, waits for them, and re-layouts, apply_mask(): shaped * blocks[:, None, :, None].astype(weight.dtype)  7.65 us
    all_to_all x1, starting transfers between devices, sent_and_summed(): lax.all_to_all(blocks, axis, split_axis=0, concat_axis=0, tiled=True)  5.93 us
    dot_general x1, matrix products, on_device(): lax.dot_general(gathered, grad_all, (((0,), (0,)), ((), ())), preferred_e...  5.76 us
  transfers between devices with their start and end apart: 4, of which 3 were waited for; matrix products, arithmetic and copies ran while one was open for 31% of the time, Pallas kernels for 0%

commit v1 on v0

v1 whole, which is shorter than its diff:
```python
import jax
import jax.numpy as jnp
from jax import lax
from jax.experimental import pallas as pl
from jax.experimental.pallas import tpu as pltpu
from jax.sharding import Mesh
from jax.sharding import PartitionSpec as P

WIDE = ("x", "z", "core")
BF = jnp.bfloat16
F32 = jnp.float32


def cost(flops, moved):
    return pl.CostEstimate(flops=flops, bytes_accessed=moved, transcendentals=0)


def spread(mask, rows_b, cols):
    cols_b = mask.shape[1]
    side = cols // cols_b
    block = lax.broadcasted_iota(jnp.int32, (cols_b, cols), 0)
    at = lax.broadcasted_iota(jnp.int32, (cols_b, cols), 1)
    first = block * side
    pick = jnp.logical_and(at >= first, at < first + side).astype(F32)
    return jnp.dot(mask.astype(F32), pick, preferred_element_type=F32)


def mask_kernel(w_ref, m_ref, o_ref):
    rows, cols = w_ref.shape
    rows_b = m_ref.shape[0]
    side = rows // rows_b
    wide = spread(m_ref[...], rows_b, cols)
    for i in range(rows_b):
        span = pl.ds(i * side, side)
        o_ref[span, :] = w_ref[span, :] * wide[i : i + 1, :].astype(BF)


def masked_weight(wt, mt):
    return pl.pallas_call(
        mask_kernel,
        out_shape=jax.ShapeDtypeStruct(wt.shape, BF),
        in_specs=[pl.BlockSpec(memory_space=pltpu.VMEM)] * 2,
        out_specs=pl.BlockSpec(memory_space=pltpu.VMEM),
        cost_estimate=cost(wt.size * 2, wt.size * 4),
        name="mask_weight",
    )(wt, mt)


def dgrad_kernel(core_ref, dy_ref, w_ref, keep_ref, send_ref):
    total = lax.dot_general(
        dy_ref[0], w_ref[...], (((0,), (0,)), ((), ())), preferred_element_type=F32
    )
    rows, cols = total.shape
    split = total.reshape(rows // 16, 2, 8, cols)
    low, high = split[:, 0], split[:, 1]
    second = core_ref[0] == 1
    keep_ref[0] = jnp.where(second, high, low).reshape(rows // 2, cols).astype(BF)
    send_ref[0] = jnp.where(second, low, high).reshape(rows // 2, cols).astype(BF)


def dgrad(core, dyg, masked):
    n, hidden, rows = dyg.shape
    cols = masked.shape[1]
    half = jax.ShapeDtypeStruct((n, rows // 2, cols), BF)
    block = pl.BlockSpec((1, rows // 2, cols), lambda i, c: (i, 0, 0))
    return pl.pallas_call(
        dgrad_kernel,
        out_shape=(half, half),
        grid_spec=pltpu.PrefetchScalarGridSpec(
            num_scalar_prefetch=1,
            grid=(n,),
            in_specs=[
                pl.BlockSpec((1, hidden, rows), lambda i, c: (i, 0, 0)),
                pl.BlockSpec((hidden, cols), lambda i, c: (0, 0)),
            ],
            out_specs=(block, block),
        ),
        cost_estimate=cost(2 * n * rows * hidden * cols, 6 << 20),
        name="dgrad",
    )(core, dyg, masked)


def fwd_kernel(core_ref, mine_ref, other_ref, w_ref, out_ref, full_ref):
    mine, other = mine_ref[0].astype(F32), other_ref[0].astype(F32)
    second = core_ref[0] == 1
    low = jnp.where(second, other, mine)
    high = jnp.where(second, mine, other)
    groups, eight, cols = low.shape
    rows = jnp.stack([low, high], axis=1).reshape(groups * 16, cols).astype(BF)
    full_ref[0] = rows
    out_ref[0] = lax.dot_general(
        w_ref[...], rows, (((1,), (1,)), ((), ())), preferred_element_type=F32
    ).astype(BF)


def forward(core, mine, other, masked):
    n, groups, eight, cols = mine.shape
    hidden = masked.shape[0]
    rows = groups * 16
    block = pl.BlockSpec((1, groups, eight, cols), lambda i, c: (i, 0, 0, 0))
    return pl.pallas_call(
        fwd_kernel,
        out_shape=(
            jax.ShapeDtypeStruct((n, hidden, rows), BF),
            jax.ShapeDtypeStruct((n, rows, cols), BF),
        ),
        grid_spec=pltpu.PrefetchScalarGridSpec(
            num_scalar_prefetch=1,
            grid=(n,),
            in_specs=[block, block, pl.BlockSpec((hidden, cols), lambda i, c: (0, 0))],
            out_specs=(
                pl.BlockSpec((1, hidden, rows), lambda i, c: (i, 0, 0)),
                pl.BlockSpec((1, rows, cols), lambda i, c: (i, 0, 0)),
            ),
        ),
        cost_estimate=cost(2 * n * rows * hidden * cols, 6 << 20),
        name="forward",
    )(core, mine, other, masked)


def wgrad_kernel(dy_ref, a_ref, m_ref, o_ref):
    n, hidden, rows = dy_ref.shape
    cols = a_ref.shape[2]
    total = jnp.dot(dy_ref[0], a_ref[0], preferred_element_type=F32)
    for i in range(1, n):
        total += jnp.dot(dy_ref[i], a_ref[i], preferred_element_type=F32)
    rows_b = m_ref.shape[1]
    side = hidden // rows_b
    wide = spread(m_ref[0], rows_b, cols)
    for i in range(rows_b):
        o_ref[i * side : (i + 1) * side, :] = (
            total[i * side : (i + 1) * side] * wide[i : i + 1, :]
        ).astype(BF)


def wgrad(dyg, full, mt):
    n, hidden, rows = dyg.shape
    cols = full.shape[2]
    steps = 4
    tile = cols // steps
    rows_b, cols_b = mt.shape
    parts = jnp.stack(jnp.split(mt, steps, axis=1))
    return pl.pallas_call(
        wgrad_kernel,
        out_shape=jax.ShapeDtypeStruct((hidden, cols), BF),
        grid=(steps,),
        in_specs=[
            pl.BlockSpec((n, hidden, rows), lambda i: (0, 0, 0)),
            pl.BlockSpec((n, rows, tile), lambda i: (0, 0, i)),
            pl.BlockSpec((1, rows_b, cols_b // steps), lambda i: (i, 0, 0)),
        ],
        out_specs=pl.BlockSpec((hidden, tile), lambda i: (0, i)),
        cost_estimate=cost(2 * n * rows * hidden * cols, 6 << 20),
        name="wgrad",
    )(dyg, full, parts)


def exchange(blocks, axis):
    return lax.all_to_all(blocks, axis, split_axis=0, concat_axis=0, tiled=True)


def copies(array, axis):
    return jnp.broadcast_to(array, (lax.axis_size(axis), *array.shape))


def swap(array):
    return lax.ppermute(array, "core", [(0, 1), (1, 0)])


def summed(blocks):
    return blocks.astype(F32).sum(axis=0).astype(BF)


def on_device(activations, up_weight, block_mask, out_grad):
    core = lax.axis_index("core").astype(jnp.int32).reshape(1)
    wt, mt, dyt = up_weight.T, block_mask.T, out_grad.T
    masked = masked_weight(wt, mt)
    dyg = exchange(copies(dyt, "narrow"), "narrow")
    near = exchange(copies(activations, "z"), "z")

    keep, send = dgrad(core, dyg, masked)
    paired = (keep.astype(F32) + swap(send).astype(F32)).astype(BF)
    along_x = summed(exchange(paired, "x"))
    along_z = exchange(along_x.reshape(8, 8, -1), "z")
    input_grad = summed(along_z)

    mine = exchange(copies(near, "x"), "x")
    other = swap(mine)
    partial, full = forward(core, mine, other, masked)
    output = summed(exchange(partial, "narrow")).T
    weight_grad = wgrad(dyg, full, mt).T
    return (output, input_grad, weight_grad)


def solution(mesh):
    torus = Mesh(
        mesh.devices.reshape(4, 8, 2, mesh.shape["narrow"]),
        ("x", "z", "core", "narrow"),
    )
    return jax.shard_map(
        on_device,
        mesh=torus,
        in_specs=(P(WIDE, "narrow"), P("narrow", WIDE), P("narrow", WIDE), P("narrow", WIDE)),
        out_specs=(P("narrow", WIDE), P(WIDE, "narrow"), P("narrow", WIDE)),
        check_vma=False,
    )
```

time: 142 us -> 104 us (0.73)
  local copies, waits for them, and re-layouts: 32.7 us -> 2.62 us
  waiting for transfers between devices: 41.9 us -> 19.2 us
  Pallas kernels: 0 us -> 18.9 us
  matrix products: 9.71 us -> 0 us
  blocking collectives: 23.6 us -> 28.8 us
  other arithmetic: 7.1 us -> 4.25 us
  starting transfers between devices: 25.5 us -> 28.1 us
    all_to_all x4, waiting for transfers between devices: 41.9 us -> 19.2 us  [exchange(): return lax.all_to_all(blocks, axis, split_axis=0, concat_axis=0, tiled=True)]
    pallas_call x0 -> x4, Pallas kernels: none -> 18.9 us  [the longest x1 5.45 us: forward(): pl.pallas_call(fwd_kernel, out_shape=(jax.ShapeDtypeStruct((n, hidden, ro...]
    convert_element_type x3 -> x0, local copies, waits for them, and re-layouts: 13.3 us -> none  [the longest x2 13.2 us: on_device(): weight_grad = apply_mask(full_grad, block_mask).astype(jnp.bfloat16)]
    dot_general x3 -> x0, matrix products: 9.71 us -> none  [the longest x1 5.76 us: on_device(): lax.dot_general(gathered, grad_all, (((0,), (0,)), ((), ())), preferred_e...]
    mul x2 -> x0, local copies, waits for them, and re-layouts: 7.65 us -> none  [apply_mask(): shaped * blocks[:, None, :, None].astype(weight.dtype)]
    ppermute x0 -> x2, starting transfers between devices: none -> 5.89 us  [swap(): return lax.ppermute(array, 'core', [(0, 1), (1, 0)])]
    all_to_all x2, blocking collectives: 23.6 us -> 28.8 us  [exchange(): return lax.all_to_all(blocks, axis, split_axis=0, concat_axis=0, tiled=True)]
    reduce_sum x3, other arithmetic: 7.09 us -> 2.28 us  [summed(): return blocks.astype(F32).sum(axis=0).astype(BF)]
  transfers between devices with their start and end apart: 4 -> 6, of which waited for: 3 -> 3; matrix products, arithmetic and copies ran while one was open for 31% -> 4% of each run, Pallas kernels for 0% -> 18%
where the time goes in v1:
time: 104 us; the launch traced here: 103 us
  blocking collectives  28.8 us (28%)
  starting transfers between devices  28.1 us (27%)
  waiting for transfers between devices  19.2 us (18%)
  Pallas kernels  18.9 us (18%)
  other arithmetic  4.25 us (4%)
  local copies, waits for them, and re-layouts  2.62 us (3%)
    all_to_all x2, blocking collectives, exchange(): return lax.all_to_all(blocks, axis, split_axis=0, concat_axis=0, tiled=True)  28.8 us
    all_to_all x4, starting transfers between devices, exchange(): return lax.all_to_all(blocks, axis, split_axis=0, concat_axis=0, tiled=True)  22.2 us
    all_to_all x4, waiting for transfers between devices, exchange(): return lax.all_to_all(blocks, axis, split_axis=0, concat_axis=0, tiled=True)  19.2 us
    ppermute x2, starting transfers between devices, swap(): return lax.ppermute(array, 'core', [(0, 1), (1, 0)])  5.89 us
    pallas_call x1, Pallas kernels, forward(): pl.pallas_call(fwd_kernel, out_shape=(jax.ShapeDtypeStruct((n, hidden, ro...  5.45 us
    pallas_call x1, Pallas kernels, wgrad(): pl.pallas_call(wgrad_kernel, out_shape=jax.ShapeDtypeStruct((hidden, cols...  5.33 us
    pallas_call x1, Pallas kernels, dgrad(): pl.pallas_call(dgrad_kernel, out_shape=(half, half), grid_spec=pltpu.Pref...  4.98 us
    pallas_call x1, Pallas kernels, masked_weight(): pl.pallas_call(mask_kernel, out_shape=jax.ShapeDtypeStruct(wt.shape, BF),...  3.14 us
  transfers between devices with their start and end apart: 6, of which 3 were waited for; matrix products, arithmetic and copies ran while one was open for 4% of the time, Pallas kernels for 18%

profile of v1, /device:TPU:1, one launch (start us, length us, event | category | flops | bytes accessed | tf_op | source)
XLA Modules:
  0.0 102.5 jit_solution(13660217296872706701)
XLA Ops:
  0.6 1.0 broadcast_in_dim.11
  1.6 12.4 %all_to_all.30.dy_ref = bf16[4,448,128]{2,1,0:T(8,128)(2,1)} all-to-all(bf16[4,448,128]{2,1,0:T(8,128)(2,1)S(1)} %broadcast_in_dim.11), channel_id=1, replica_groups=mesh['x'=4,'z'=8,'core'=2,'narrow'=4] {'narrow'}, dimensions={0} | all-to-all | bytes 917504 | tf_op jit(solution)/shard_map/all_to_all | solution.py:159
  14.0 1.5 %broadcast_in_dim.9 = bf16[8,8,2048]{2,1,0:T(8,128)(2,1)} broadcast(bf16[8,2048]{1,0:T(8,128)(2,1)} %param.4), dimensions={1,2} | broadcast | bytes 294912 | tf_op jit(solution)/shard_map/broadcast_in_dim | solution.py:163
  15.5 8.3 %all-to-all-start = ((bf16[8,8,2048]{2,1,0:T(8,128)(2,1)}), bf16[8,8,2048]{2,1,0:T(8,128)(2,1)S(1)}, u32[]{:S(2)}, u32[]{:S(2)}) async-start(bf16[8,8,2048]{2,1,0:T(8,128)(2,1)} %broadcast_in_dim.9), calls=%async_computation | async-start | bytes 524288 | tf_op jit(solution)/shard_map/all_to_all | solution.py:159
  23.8 3.1 %mask_weight.1.w_ref = bf16[448,2048]{1,0:T(8,128)(2,1)} custom-call(bf16[448,2048]{1,0:T(8,128)(2,1)} %bitcast.15, s32[7,32]{1,0:T(8,128)} %bitcast.19), custom_call_target="tpu_custom_call" | custom-call | flops 1835008 | bytes 3670016 | tf_op jit(solution)/shard_map/mask_weight/pallas_call | solution.py:39
  26.9 5.0 %dgrad.1 = (bf16[4,64,2048]{2,1,0:T(8,128)(2,1)}, bf16[4,64,2048]{2,1,0:T(8,128)(2,1)}) custom-call(s32[1]{0:T(128)} %bitcast.core_ref, bf16[4,448,128]{2,1,0:T(8,128)(2,1)} %all_to_all.30.dy_ref, bf16[448,2048]{1,0:T(8,128)(2,1)} %mask_weight.1.w_ref), custom_call_target="tpu_custom_call" | custom-call | flops 939524096 | bytes 6291456 | tf_op jit(solution)/shard_map/dgrad/pallas_call | solution.py:66
  31.9 2.4 %collective-permute-start.1 = (bf16[4,64,2048]{2,1,0:T(8,128)(2,1)}, bf16[4,64,2048]{2,1,0:T(8,128)(2,1)S(1)}, u32[]{:S(2)}, u32[]{:S(2)}) collective-permute-start(bf16[4,64,2048]{2,1,0:T(8,128)(2,1)} %get-tuple-element.9), channel_id=1, source_target_pairs={{0,4},{4,0},{1,5},{5,1},{2,6},{6,2},{3,7},{7,3},{8,12},{12,8},{9,1... | collective-permute-start | bytes 3145736 | tf_op jit(solution)/shard_map/ppermute | solution.py:167
  34.3 0.1 broadcast_in_dim.10
  34.4 16.4 %all_to_all.31.mine_ref = bf16[4,8,8,2048]{3,2,1,0:T(8,128)(2,1)S(1)} all-to-all(bf16[4,8,8,2048]{3,2,1,0:T(8,128)(2,1)S(1)} %broadcast_in_dim.10), channel_id=1, replica_groups=mesh['x'=4,'z'=8,'core'=2,'narrow'=4] {'x'}, dimensions={0} | all-to-all | bytes 2097152 | tf_op jit(solution)/shard_map/all_to_all | solution.py:159
  50.8 3.5 %collective-permute-start = (bf16[4,8,8,2048]{3,2,1,0:T(8,128)(2,1)S(1)}, bf16[4,8,8,2048]{3,2,1,0:T(8,128)(2,1)}, u32[]{:S(2)}, u32[]{:S(2)}) collective-permute-start(bf16[4,8,8,2048]{3,2,1,0:T(8,128)(2,1)S(1)} %all_to_all.31.mine_ref), channel_id=1, source_target_pairs={{0,4},{4,0},{1,5},{5,1},{2,6},{6,2},{3,7},{7,3},{8,12},{12,8},{9,1... | collective-permute-start | bytes 3145736 | tf_op jit(solution)/shard_map/ppermute | solution.py:167
  54.3 1.4 %add_convert_fusion = bf16[4,64,2048]{2,1,0:T(8,128)(2,1)} fusion(bf16[4,64,2048]{2,1,0:T(8,128)(2,1)S(1)} %collective-permute-done.1, bf16[4,64,2048]{2,1,0:T(8,128)(2,1)S(1)} %copy-done.1), kind=kLoop, calls=%fused_computation | loop fusion | flops 2097152 | bytes 3145728 | tf_op jit(solution)/shard_map/convert_element_type | solution.py:182
  55.6 3.5 %all-to-all-start.4 = ((bf16[4,64,2048]{2,1,0:T(8,128)(2,1)}), bf16[4,64,2048]{2,1,0:T(8,128)(2,1)S(1)}, u32[]{:S(2)}, u32[]{:S(2)}) async-start(bf16[4,64,2048]{2,1,0:T(8,128)(2,1)} %add_convert_fusion), calls=%async_computation.4 | async-start | bytes 2097152 | tf_op jit(solution)/shard_map/all_to_all | solution.py:159
  59.2 5.5 %forward.1 = (bf16[4,448,128]{2,1,0:T(8,128)(2,1)}, bf16[4,128,2048]{2,1,0:T(8,128)(2,1)}) custom-call(s32[1]{0:T(128)} %bitcast.core_ref, bf16[4,8,8,2048]{3,2,1,0:T(8,128)(2,1)} %copy-done, bf16[4,8,8,2048]{3,2,1,0:T(8,128)(2,1)} %collective-permute-done.other_ref, bf16[448,2048]{1,0:T(8,128)(2,1)} %mask_weight.1.w_ref), custom_call_target="tpu_custom_call" | custom-call | flops 939524096 | bytes 6291456 | tf_op jit(solution)/shard_map/forward/pallas_call | solution.py:101
  64.6 9.7 %all-to-all-done.4 = bf16[4,64,2048]{2,1,0:T(8,128)(2,1)S(1)} async-done(((bf16[4,64,2048]{2,1,0:T(8,128)(2,1)}), bf16[4,64,2048]{2,1,0:T(8,128)(2,1)S(1)}, u32[]{:S(2)}, u32[]{:S(2)}) %all-to-all-start.4) | async-done | bytes 1048608 | tf_op jit(solution)/shard_map/all_to_all | solution.py:159
  74.3 3.5 %all-to-all-start.2 = ((bf16[4,448,128]{2,1,0:T(8,128)(2,1)}), bf16[4,448,128]{2,1,0:T(8,128)(2,1)S(1)}, u32[]{:S(2)}, u32[]{:S(2)}) async-start(bf16[4,448,128]{2,1,0:T(8,128)(2,1)} %get-tuple-element.7), calls=%async_computation.2 | async-start | bytes 917504 | tf_op jit(solution)/shard_map/all_to_all | solution.py:159
  77.8 0.9 reduce_sum.37
  78.7 6.8 %all-to-all-done.2 = bf16[4,448,128]{2,1,0:T(8,128)(2,1)S(1)} async-done(((bf16[4,448,128]{2,1,0:T(8,128)(2,1)}), bf16[4,448,128]{2,1,0:T(8,128)(2,1)S(1)}, u32[]{:S(2)}, u32[]{:S(2)}) %all-to-all-start.2) | async-done | bytes 458784 | tf_op jit(solution)/shard_map/all_to_all | solution.py:159
  85.5 6.9 %all-to-all-start.5 = ((bf16[8,8,2048]{2,1,0:T(8,128)(2,1)}), bf16[8,8,2048]{2,1,0:T(8,128)(2,1)S(1)}, u32[]{:S(2)}, u32[]{:S(2)}) async-start(bf16[8,8,2048]{2,1,0:T(8,128)(2,1)} %bitcast.5), calls=%async_computation.5 | async-start | bytes 524288 | tf_op jit(solution)/shard_map/all_to_all | solution.py:159
  92.4 0.1 slice_bitcast_fusion.3
  92.5 0.6 pad_add_fusion.m_ref
  93.1 5.3 %wgrad.1 = bf16[448,2048]{1,0:T(8,128)(2,1)} custom-call(bf16[4,448,128]{2,1,0:T(8,128)(2,1)} %all_to_all.30.dy_ref, bf16[4,128,2048]{2,1,0:T(8,128)(2,1)} %get-tuple-element.10.a_ref, s32[4,7,8]{2,1,0:T(8,128)} %pad_add_fusion.m_ref), custom_call_target="tpu_custom_call" | custom-call | flops 939524096 | bytes 6291456 | tf_op jit(solution)/shard_map/wgrad/pallas_call | solution.py:143
  98.4 0.7 reduce_sum.36
  99.1 2.7 %all-to-all-done.5 = bf16[8,8,2048]{2,1,0:T(8,128)(2,1)S(1)} async-done(((bf16[8,8,2048]{2,1,0:T(8,128)(2,1)}), bf16[8,8,2048]{2,1,0:T(8,128)(2,1)S(1)}, u32[]{:S(2)}, u32[]{:S(2)}) %all-to-all-start.5) | async-done | bytes 262176 | tf_op jit(solution)/shard_map/all_to_all | solution.py:159
  101.9 0.7 reduce_sum.38
  (9 shorter events, 0.0 us)
Async XLA Ops:
  15.5 18.8 %all-to-all-start = ((bf16[8,8,2048]{2,1,0:T(8,128)(2,1)}), bf16[8,8,2048]{2,1,0:T(8,128)(2,1)S(1)}, u32[]{:S(2)}, u32[]{:S(2)}) async-start(bf16[8,8,2048]{2,1,0:T(8,128)(2,1)} %broadcast_in_dim.9), calls=%async_computation | async-start | bytes 524288 | tf_op jit(solution)/shard_map/all_to_all | solution.py:159
  31.9 22.4 %copy-start.1 = (bf16[4,64,2048]{2,1,0:T(8,128)(2,1)S(1)}, bf16[4,64,2048]{2,1,0:T(8,128)(2,1)}, u32[]{:S(2)}) copy-start(bf16[4,64,2048]{2,1,0:T(8,128)(2,1)} %get-tuple-element.8) | copy-start | bytes 3145732
  31.9 22.4 %collective-permute-start.1 = (bf16[4,64,2048]{2,1,0:T(8,128)(2,1)}, bf16[4,64,2048]{2,1,0:T(8,128)(2,1)S(1)}, u32[]{:S(2)}, u32[]{:S(2)}) collective-permute-start(bf16[4,64,2048]{2,1,0:T(8,128)(2,1)} %get-tuple-element.9), channel_id=1, source_target_pairs={{0,4},{4,0},{1,5},{5,1},{2,6},{6,2},{3,7},{7,3},{8,12},{12,8},{9,1... | collective-permute-start | bytes 3145736 | tf_op jit(solution)/shard_map/ppermute | solution.py:167
  50.8 4.9 %copy-start = (bf16[4,8,8,2048]{3,2,1,0:T(8,128)(2,1)}, bf16[4,8,8,2048]{3,2,1,0:T(8,128)(2,1)S(1)}, u32[]{:S(2)}) copy-start(bf16[4,8,8,2048]{3,2,1,0:T(8,128)(2,1)S(1)} %all_to_all.31.mine_ref) | copy-start | bytes 3145732
  50.8 8.4 %collective-permute-start = (bf16[4,8,8,2048]{3,2,1,0:T(8,128)(2,1)S(1)}, bf16[4,8,8,2048]{3,2,1,0:T(8,128)(2,1)}, u32[]{:S(2)}, u32[]{:S(2)}) collective-permute-start(bf16[4,8,8,2048]{3,2,1,0:T(8,128)(2,1)S(1)} %all_to_all.31.mine_ref), channel_id=1, source_target_pairs={{0,4},{4,0},{1,5},{5,1},{2,6},{6,2},{3,7},{7,3},{8,12},{12,8},{9,1... | collective-permute-start | bytes 3145736 | tf_op jit(solution)/shard_map/ppermute | solution.py:167
  55.6 18.7 %all-to-all-start.4 = ((bf16[4,64,2048]{2,1,0:T(8,128)(2,1)}), bf16[4,64,2048]{2,1,0:T(8,128)(2,1)S(1)}, u32[]{:S(2)}, u32[]{:S(2)}) async-start(bf16[4,64,2048]{2,1,0:T(8,128)(2,1)} %add_convert_fusion), calls=%async_computation.4 | async-start | bytes 2097152 | tf_op jit(solution)/shard_map/all_to_all | solution.py:159
  64.6 27.8 %copy-start.2 = (s32[32,7]{0,1:T(8,128)S(1)}, s32[32,7]{0,1:T(8,128)}, u32[]{:S(2)}) copy-start(s32[32,7]{0,1:T(8,128)} %param.6) | copy-start | bytes 2692
  74.3 11.1 %all-to-all-start.2 = ((bf16[4,448,128]{2,1,0:T(8,128)(2,1)}), bf16[4,448,128]{2,1,0:T(8,128)(2,1)S(1)}, u32[]{:S(2)}, u32[]{:S(2)}) async-start(bf16[4,448,128]{2,1,0:T(8,128)(2,1)} %get-tuple-element.7), calls=%async_computation.2 | async-start | bytes 917504 | tf_op jit(solution)/shard_map/all_to_all | solution.py:159
  85.5 16.4 %all-to-all-start.5 = ((bf16[8,8,2048]{2,1,0:T(8,128)(2,1)}), bf16[8,8,2048]{2,1,0:T(8,128)(2,1)S(1)}, u32[]{:S(2)}, u32[]{:S(2)}) async-start(bf16[8,8,2048]{2,1,0:T(8,128)(2,1)} %bitcast.5), calls=%async_computation.5 | async-start | bytes 524288 | tf_op jit(solution)/shard_map/all_to_all | solution.py:159

commit v2 on v0

v2 whole, which is shorter than its diff:
```python
import jax
import jax.numpy as jnp
from jax import lax
from jax.experimental import pallas as pl
from jax.experimental.pallas import tpu as pltpu
from jax.sharding import Mesh
from jax.sharding import PartitionSpec as P

WIDE = ("x", "z", "core")
BF = jnp.bfloat16
F32 = jnp.float32
VMEM = pl.BlockSpec(memory_space=pltpu.VMEM)
SMEM = pl.BlockSpec(memory_space=pltpu.SMEM)


def cost(flops, moved):
    return pl.CostEstimate(flops=flops, bytes_accessed=moved, transcendentals=0)


def grant(mib):
    return pltpu.CompilerParams(vmem_limit_bytes=mib << 20)


def shaped(*dims, kind=BF):
    return jax.ShapeDtypeStruct(dims, kind)


def mask_kernel(w_ref, m_ref, o_ref, wide_ref):
    rows, cols = w_ref.shape
    rows_b, cols_b = m_ref.shape
    side = cols // cols_b
    block = lax.broadcasted_iota(jnp.int32, (cols_b, cols), 0)
    at = lax.broadcasted_iota(jnp.int32, (cols_b, cols), 1)
    first = block * side
    pick = jnp.logical_and(at >= first, at < first + side).astype(F32)
    wide = jnp.dot(m_ref[...].astype(F32), pick, preferred_element_type=F32)
    wide_ref[...] = wide
    side = rows // rows_b
    for i in range(rows_b):
        span = pl.ds(i * side, side)
        o_ref[span, :] = w_ref[span, :] * wide[i : i + 1, :].astype(BF)


def masked_weight(wt, mt):
    return pl.pallas_call(
        mask_kernel,
        out_shape=(shaped(*wt.shape), shaped(mt.shape[0], wt.shape[1], kind=F32)),
        in_specs=[VMEM] * 2,
        out_specs=(VMEM, VMEM),
        cost_estimate=cost(wt.size * 2, wt.size * 4),
        compiler_params=grant(8),
        name="mask_weight",
    )(wt, mt)


def own_first(core, tokens, back=False):
    old = lax.broadcasted_iota(jnp.int32, (tokens, tokens), 1 if back else 0)
    new = lax.broadcasted_iota(jnp.int32, (tokens, tokens), 0 if back else 1)
    half = tokens // 2
    other = (new >= half).astype(jnp.int32)
    within = new - other * half
    group = jnp.right_shift(within, 3)
    src = group * 16 + jnp.bitwise_xor(other, core) * 8 + (within - group * 8)
    return (src == old).astype(BF)


def dgrad_kernel(at_ref, d0, d1, d2, d3, w_ref, keep_ref, send_ref, dy_ref):
    x, y, core = at_ref[0], at_ref[1], at_ref[2]
    tokens = d0.shape[1]
    half = tokens // 2
    order = own_first(core, tokens)
    for k, d in enumerate((d0, d1, d2, d3)):
        rel = lax.rem(y + k - x + 4, 4)
        lanes = jnp.dot(d[...], order, preferred_element_type=F32).astype(BF)
        dy_ref[:, pl.ds(pl.multiple_of(rel * tokens, tokens), tokens)] = lanes
        total = lax.dot_general(
            lanes, w_ref[...], (((0,), (0,)), ((), ())), preferred_element_type=F32
        ).astype(BF)
        keep_ref[rel] = total[:half]
        send_ref[rel] = total[half:]


def dgrad(at, blocks, masked):
    hidden, tokens = blocks[0].shape
    cols = masked.shape[1]
    half = shaped(4, tokens // 2, cols)
    return pl.pallas_call(
        dgrad_kernel,
        out_shape=(half, half, shaped(hidden, 4 * tokens)),
        in_specs=[SMEM] + [VMEM] * 5,
        out_specs=(VMEM,) * 3,
        cost_estimate=cost(8 * tokens * hidden * cols, 4 << 20),
        compiler_params=grant(16),
        name="dgrad",
    )(at, *blocks, masked)


def fwd_kernel(at_ref, *refs):
    mine, other = refs[:5], refs[5:10]
    w_ref, o0, o1, o2, o3, full_ref, acc_ref = refs[10:]
    x, y = at_ref[0], at_ref[1]
    half = mine[0].shape[0]
    quarter = half // 2
    for h, group in enumerate((mine, other)):
        for k in range(3):
            full_ref[pl.ds((0, 2, 6)[k] * half + h * half, half), :] = group[k][...]
        full_ref[pl.ds(4 * half + h * half, quarter), :] = group[3][...]
        full_ref[pl.ds(4 * half + h * half + quarter, quarter), :] = group[4][...]
    acc_ref[...] = lax.dot_general(
        w_ref[...], full_ref[...], (((1,), (1,)), ((), ())), preferred_element_type=F32
    ).astype(BF)
    tokens = 2 * half
    for k, out in enumerate((o0, o1, o2, o3)):
        rel = lax.rem(y + k - x + 4, 4)
        out[...] = acc_ref[:, pl.ds(pl.multiple_of(rel * tokens, tokens), tokens)]


def forward(at, mine, other, masked):
    half = mine[0].shape[0]
    hidden, cols = masked.shape
    out = shaped(hidden, 2 * half)
    return pl.pallas_call(
        fwd_kernel,
        out_shape=(out,) * 4 + (shaped(8 * half, cols),),
        in_specs=[SMEM] + [VMEM] * 11,
        out_specs=(VMEM,) * 5,
        scratch_shapes=[pltpu.VMEM((hidden, 8 * half), BF)],
        cost_estimate=cost(16 * half * hidden * cols, 6 << 20),
        compiler_params=grant(16),
        name="forward",
    )(at, *mine, *other, masked)


def wgrad_kernel(dy_ref, a_ref, wide_ref, o_ref):
    total = jnp.dot(dy_ref[...], a_ref[...], preferred_element_type=F32)
    rows_b = wide_ref.shape[0]
    side = total.shape[0] // rows_b
    for i in range(rows_b):
        span = slice(i * side, (i + 1) * side)
        o_ref[span, :] = (total[span] * wide_ref[i : i + 1, :]).astype(BF)


def wgrad(dy, full, wide):
    hidden, rows = dy.shape
    cols = full.shape[1]
    steps = 4
    tile = cols // steps
    return pl.pallas_call(
        wgrad_kernel,
        out_shape=shaped(hidden, cols),
        grid=(steps,),
        in_specs=[
            pl.BlockSpec((hidden, rows), lambda i: (0, 0)),
            pl.BlockSpec((rows, tile), lambda i: (0, i)),
            pl.BlockSpec((wide.shape[0], tile), lambda i: (0, i)),
        ],
        out_specs=pl.BlockSpec((hidden, tile), lambda i: (0, i)),
        cost_estimate=cost(2 * rows * hidden * cols, 6 << 20),
        compiler_params=grant(14),
        name="wgrad",
    )(dy, full, wide)


def finish_kernel(at_ref, r0, r1, r2, r3, o_ref):
    total = (r0[...].astype(F32) + r1[...].astype(F32)) + (
        r2[...].astype(F32) + r3[...].astype(F32)
    )
    back = own_first(at_ref[2], r0.shape[1], back=True)
    o_ref[...] = jnp.dot(total.astype(BF), back, preferred_element_type=F32).astype(BF)


def finish(at, parts):
    return pl.pallas_call(
        finish_kernel,
        out_shape=shaped(*parts[0].shape),
        in_specs=[SMEM] + [VMEM] * 4,
        out_specs=VMEM,
        cost_estimate=cost(parts[0].size * 256, 1 << 20),
        compiler_params=grant(6),
        name="finish",
    )(at, *parts)


def exchange(blocks, axis):
    return lax.all_to_all(blocks, axis, split_axis=0, concat_axis=0, tiled=True)


def copies(array, axis):
    return jnp.broadcast_to(array, (lax.axis_size(axis), *array.shape))


def to(array, axis, step):
    n = lax.axis_size(axis)
    return lax.ppermute(array, axis, [(i, (i + step) % n) for i in range(n)])


def added(*terms):
    return sum(t.astype(F32) for t in terms).astype(BF)


def on_device(activations, up_weight, block_mask, out_grad):
    at = jnp.stack([lax.axis_index(n).astype(jnp.int32) for n in ("x", "narrow", "core")])
    wt, mt, dyt = up_weight.T, block_mask.T, out_grad.T
    masked, wide = masked_weight(wt, mt)

    blocks = [to(dyt, "narrow", -1), to(dyt, "narrow", 1)]
    blocks = (dyt, blocks[0], to(dyt, "narrow", 2), blocks[1])
    near = exchange(copies(activations, "z"), "z").reshape(-1, activations.shape[1])

    keep, send, dy = dgrad(at, blocks, masked)
    got = to(send, "core", 1)
    half = keep.shape[1] // 2
    ahead = to(added(keep[2, :half], got[2, :half]), "x", 1)
    behind = to(added(keep[2, half:], got[2, half:]), "x", -1)
    none = jnp.zeros_like(ahead)
    right = added(keep[1], got[1], jnp.concatenate([ahead, none]))
    left = added(keep[3], got[3], jnp.concatenate([none, behind]))
    along_x = added(keep[0], got[0], to(right, "x", 1), to(left, "x", -1))
    along_z = exchange(along_x.reshape(8, 8, -1), "z")
    input_grad = along_z.astype(F32).sum(axis=0).astype(BF)

    after, before = to(near, "x", -1), to(near, "x", 1)
    far_low, far_high = to(before[:half], "x", 1), to(after[half:], "x", -1)
    mine = (near, after, before, far_low, far_high)
    other = tuple(to(m, "core", 1) for m in mine)
    o0, o1, o2, o3, full = forward(at, mine, other, masked)
    parts = (o0, to(o1, "narrow", 1), to(o2, "narrow", 2), to(o3, "narrow", -1))
    output = finish(at, parts).T
    weight_grad = wgrad(dy, full, wide).T
    return (output, input_grad, weight_grad)


def solution(mesh):
    torus = Mesh(
        mesh.devices.reshape(4, 8, 2, mesh.shape["narrow"]),
        ("x", "z", "core", "narrow"),
    )
    return jax.shard_map(
        on_device,
        mesh=torus,
        in_specs=(P(WIDE, "narrow"), P("narrow", WIDE), P("narrow", WIDE), P("narrow", WIDE)),
        out_specs=(P("narrow", WIDE), P(WIDE, "narrow"), P("narrow", WIDE)),
        check_vma=False,
    )
```

time: 142 us -> 77.2 us (0.54)
  waiting for transfers between devices: 41.9 us -> 12.3 us
  local copies, waits for them, and re-layouts: 32.7 us -> 6.6 us
  blocking collectives: 23.6 us -> 0 us
  starting transfers between devices: 25.5 us -> 39.6 us
  Pallas kernels: 0 us -> 10.9 us
  matrix products: 9.71 us -> 0 us
    all_to_all x4 -> x2, waiting for transfers between devices: 41.9 us -> 7.95 us  [exchange(): return lax.all_to_all(blocks, axis, split_axis=0, concat_axis=0, tiled=True)]
    ppermute x0 -> x20, starting transfers between devices: none -> 27.6 us  [to(): return lax.ppermute(array, axis, [(i, (i + step) % n) for i in range(n)])]
    all_to_all x2 -> x0, blocking collectives: 23.6 us -> none  [sent_to_all(): return lax.all_to_all(copies, axis, split_axis=0, concat_axis=0, tiled=True)]
    all_to_all x4 -> x2, starting transfers between devices: 25.5 us -> 12 us  [exchange(): return lax.all_to_all(blocks, axis, split_axis=0, concat_axis=0, tiled=True)]
    convert_element_type x3 -> x0, local copies, waits for them, and re-layouts: 13.3 us -> none  [the longest x2 13.2 us: on_device(): weight_grad = apply_mask(full_grad, block_mask).astype(jnp.bfloat16)]
    pallas_call x0 -> x5, Pallas kernels: none -> 10.9 us  [the longest x1 3.59 us: dgrad(): pl.pallas_call(dgrad_kernel, out_shape=(half, half, shaped(hidden, 4 * to...]
    dot_general x3 -> x0, matrix products: 9.71 us -> none  [the longest x1 5.76 us: on_device(): lax.dot_general(gathered, grad_all, (((0,), (0,)), ((), ())), preferred_e...]
    mul x2 -> x0, local copies, waits for them, and re-layouts: 7.65 us -> none  [apply_mask(): shaped * blocks[:, None, :, None].astype(weight.dtype)]
  transfers between devices with their start and end apart: 4 -> 22, of which waited for: 3 -> 7; matrix products, arithmetic and copies ran while one was open for 31% -> 10% of each run, Pallas kernels for 0% -> 10%
where the time goes in v2:
time: 77.2 us; the launch traced here: 76.7 us
  starting transfers between devices  39.6 us (51%)
  waiting for transfers between devices  12.3 us (16%)
  Pallas kernels  10.9 us (14%)
  local copies, waits for them, and re-layouts  6.6 us (9%)
  other arithmetic  6.51 us (8%)
    ppermute x20, starting transfers between devices, to(): return lax.ppermute(array, axis, [(i, (i + step) % n) for i in range(n)])  27.6 us
    all_to_all x2, starting transfers between devices, exchange(): return lax.all_to_all(blocks, axis, split_axis=0, concat_axis=0, tiled=True)  12 us
    all_to_all x2, waiting for transfers between devices, exchange(): return lax.all_to_all(blocks, axis, split_axis=0, concat_axis=0, tiled=True)  7.95 us
    ppermute x20, waiting for transfers between devices, to(): return lax.ppermute(array, axis, [(i, (i + step) % n) for i in range(n)])  4.38 us
    unnamed x16, local copies, waits for them, and re-layouts  3.63 us
    pallas_call x1, Pallas kernels, dgrad(): pl.pallas_call(dgrad_kernel, out_shape=(half, half, shaped(hidden, 4 * to...  3.59 us
    convert_element_type x2, other arithmetic, added(): return sum((t.astype(F32) for t in terms)).astype(BF)  3.02 us
    pallas_call x1, Pallas kernels, wgrad(): pl.pallas_call(wgrad_kernel, out_shape=shaped(hidden, cols), grid=(steps,...  2.9 us
  transfers between devices with their start and end apart: 22, of which 7 were waited for; matrix products, arithmetic and copies ran while one was open for 10% of the time, Pallas kernels for 10%

profile of v2, /device:TPU:1, one launch (start us, length us, event | category | flops | bytes accessed | tf_op | source)
XLA Modules:
  0.0 76.7 jit_solution(16836557234622998025)
XLA Ops:
  0.6 2.2 %collective-permute-start.14 = (bf16[448,128]{1,0:T(8,128)(2,1)}, bf16[448,128]{1,0:T(8,128)(2,1)S(1)}, u32[]{:S(2)}, u32[]{:S(2)}) collective-permute-start(bf16[448,128]{1,0:T(8,128)(2,1)} %bitcast.37), channel_id=1, source_target_pairs={{0,1},{1,2},{2,3},{3,0},{4,5},{5,6},{6,7},{7,4},{8,9},{9,10},{10,1... | collective-permute-start | bytes 344072 | tf_op jit(solution)/shard_map/ppermute | solution.py:194
  2.8 2.6 %collective-permute-start.13 = (bf16[448,128]{1,0:T(8,128)(2,1)}, bf16[448,128]{1,0:T(8,128)(2,1)S(1)}, u32[]{:S(2)}, u32[]{:S(2)}) collective-permute-start(bf16[448,128]{1,0:T(8,128)(2,1)} %bitcast.38), channel_id=1, source_target_pairs={{0,2},{1,3},{2,0},{3,1},{4,6},{5,7},{6,4},{7,5},{8,10},{9,11},{10,... | collective-permute-start | bytes 344072 | tf_op jit(solution)/shard_map/ppermute | solution.py:194
  6.5 1.5 %copy-done = bf16[2048,448]{0,1:T(8,128)(2,1)S(1)} copy-done((bf16[2048,448]{0,1:T(8,128)(2,1)S(1)}, bf16[2048,448]{0,1:T(8,128)(2,1)}, u32[]{:S(2)}) %copy-start) | copy-done | bytes 1835032
  10.7 3.6 %dgrad.1 = (bf16[4,64,2048]{2,1,0:T(8,128)(2,1)S(1)}, bf16[4,64,2048]{2,1,0:T(8,128)(2,1)}, bf16[448,512]{1,0:T(8,128)(2,1)S(1)}) custom-call(s32[3]{0:T(128)S(1)} %pad_add_fusion.at_ref, bf16[448,128]{1,0:T(8,128)(2,1)S(1)} %bitcast.40, bf16[448,128]{1,0:T(8,128)(2,1)S(1)} %collective-permute-done.12.d1, bf16[448,128]{1,0:T(8,128)(2,1)S(1)} %collective-permute-done.13.d2, ...), custom_call_target="tpu_custom_call" | custom-call | flops 939524096 | bytes 4194304 | tf_op jit(solution)/shard_map/dgrad/pallas_call | solution.py:87
  15.1 1.8 %collective-permute-start.15 = (bf16[4,64,2048]{2,1,0:T(8,128)(2,1)}, bf16[4,64,2048]{2,1,0:T(8,128)(2,1)}, u32[]{:S(2)}, u32[]{:S(2)}) collective-permute-start(bf16[4,64,2048]{2,1,0:T(8,128)(2,1)} %get-tuple-element.19), channel_id=1, source_target_pairs={{0,4},{4,0},{1,5},{5,1},{2,6},{6,2},{3,7},{7,3},{8,12},{12,8},{9,1... | collective-permute-start | bytes 3145736 | tf_op jit(solution)/shard_map/ppermute | solution.py:194
  17.6 7.9 %all-to-all-start = ((bf16[8,8,2048]{2,1,0:T(8,128)(2,1)}), bf16[8,8,2048]{2,1,0:T(8,128)(2,1)S(1)}, u32[]{:S(2)}, u32[]{:S(2)}) async-start(bf16[8,8,2048]{2,1,0:T(8,128)(2,1)} %broadcast_in_dim.4), calls=%async_computation | async-start | bytes 524288 | tf_op jit(solution)/shard_map/all_to_all | solution.py:185
  25.5 1.7 %fusion.5 = (bf16[32,2048]{1,0:T(8,128)(2,1)}, bf16[32,2048]{1,0:T(8,128)(2,1)}) fusion(bf16[4,64,2048]{2,1,0:T(8,128)(2,1)} %collective-permute-done.15, bf16[4,64,2048]{2,1,0:T(8,128)(2,1)S(1)} %get-tuple-element.18), kind=kLoop, calls=%fused_computation.10 | loop fusion | flops 524288 | bytes 786432 | tf_op jit(solution)/shard_map/convert_element_type | solution.py:198
  28.5 1.5 %collective-permute-start.18 = (bf16[32,2048]{1,0:T(8,128)(2,1)}, bf16[32,2048]{1,0:T(8,128)(2,1)}, u32[]{:S(2)}, u32[]{:S(2)}) collective-permute-start(bf16[32,2048]{1,0:T(8,128)(2,1)} %get-tuple-element.26), channel_id=1, source_target_pairs={{0,192},{64,0},{128,64},{192,128},{1,193},{65,1},{129,65},{193,129... | collective-permute-start | bytes 393224 | tf_op jit(solution)/shard_map/ppermute | solution.py:194
  30.0 7.9 %all-to-all-done = bf16[8,8,2048]{2,1,0:T(8,128)(2,1)S(1)} async-done(((bf16[8,8,2048]{2,1,0:T(8,128)(2,1)}), bf16[8,8,2048]{2,1,0:T(8,128)(2,1)S(1)}, u32[]{:S(2)}, u32[]{:S(2)}) %all-to-all-start) | async-done | bytes 262176 | tf_op jit(solution)/shard_map/all_to_all | solution.py:185
  39.1 1.5 %collective-permute-start = (bf16[64,2048]{1,0:T(8,128)(2,1)S(1)}, bf16[64,2048]{1,0:T(8,128)(2,1)}, u32[]{:S(2)}, u32[]{:S(2)}) collective-permute-start(bf16[64,2048]{1,0:T(8,128)(2,1)S(1)} %bitcast.33), channel_id=1, source_target_pairs={{0,192},{64,0},{128,64},{192,128},{1,193},{65,1},{129,65},{193,129... | collective-permute-start | bytes 786440 | tf_op jit(solution)/shard_map/ppermute | solution.py:194
  40.6 1.3 %fusion.1 = (bf16[64,2048]{1,0:T(8,128)(2,1)S(1)}, bf16[64,2048]{1,0:T(8,128)(2,1)S(1)}) fusion(bf16[4,64,2048]{2,1,0:T(8,128)(2,1)} %collective-permute-done.15, bf16[32,2048]{1,0:T(8,128)(2,1)S(1)} %collective-permute-done.16, bf16[4,64,2048]{2,1,0:T(8,128)(2,1)S(1)} %get-tuple-element.18, bf16[32,2048]{1,0:T(8,128)(2,1)} %collective-permute-done.18), kind=kLoop, calls=%fused_computation.3 | loop fusion | flops 1572864 | bytes 1835008 | tf_op jit(solution)/shard_map/convert_element_type | solution.py:198
  42.0 2.7 %collective-permute-start.19 = (bf16[64,2048]{1,0:T(8,128)(2,1)S(1)}, bf16[64,2048]{1,0:T(8,128)(2,1)S(1)}, u32[]{:S(2)}, u32[]{:S(2)}) collective-permute-start(bf16[64,2048]{1,0:T(8,128)(2,1)S(1)} %get-tuple-element.24), channel_id=1, source_target_pairs={{0,192},{64,0},{128,64},{192,128},{1,193},{65,1},{129,65},{193,129... | collective-permute-start | bytes 786440 | tf_op jit(solution)/shard_map/ppermute | solution.py:194
  44.6 1.6 %collective-permute-start.4 = (bf16[64,2048]{1,0:T(8,128)(2,1)S(1)}, bf16[64,2048]{1,0:T(8,128)(2,1)}, u32[]{:S(2)}, u32[]{:S(2)}) collective-permute-start(bf16[64,2048]{1,0:T(8,128)(2,1)S(1)} %bitcast.34), channel_id=1, source_target_pairs={{0,4},{4,0},{1,5},{5,1},{2,6},{6,2},{3,7},{7,3},{8,12},{12,8},{9,1... | collective-permute-start | bytes 786440 | tf_op jit(solution)/shard_map/ppermute | solution.py:194
  47.3 1.6 %slice.49 = bf16[32,2048]{1,0:T(8,128)(2,1)} slice(bf16[64,2048]{1,0:T(8,128)(2,1)} %collective-permute-done.refs_1_), slice={[32:64], [0:2048]} | slice | bytes 262144 | tf_op jit(solution)/shard_map/slice | solution.py:223
  48.9 2.6 %collective-permute-start.3 = (bf16[32,2048]{1,0:T(8,128)(2,1)}, bf16[32,2048]{1,0:T(8,128)(2,1)}, u32[]{:S(2)}, u32[]{:S(2)}) collective-permute-start(bf16[32,2048]{1,0:T(8,128)(2,1)} %slice.49), channel_id=1, source_target_pairs={{0,192},{64,0},{128,64},{192,128},{1,193},{65,1},{129,65},{193,129... | collective-permute-start | bytes 393224 | tf_op jit(solution)/shard_map/ppermute | solution.py:194
  52.1 2.2 %collective-permute-start.6 = (bf16[64,2048]{1,0:T(8,128)(2,1)S(1)}, bf16[64,2048]{1,0:T(8,128)(2,1)}, u32[]{:S(2)}, u32[]{:S(2)}) collective-permute-start(bf16[64,2048]{1,0:T(8,128)(2,1)S(1)} %collective-permute-done.1.refs_2_), channel_id=1, source_target_pairs={{0,4},{4,0},{1,5},{5,1},{2,6},{6,2},{3,7},{7,3},{8,12},{12,8},{9,1... | collective-permute-start | bytes 786440 | tf_op jit(solution)/shard_map/ppermute | solution.py:194
  54.7 1.8 %fusion.4 = bf16[8,8,2048]{2,1,0:T(8,128)(2,1)} fusion(bf16[64,2048]{1,0:T(8,128)(2,1)S(1)} %collective-permute-done.19, bf16[64,2048]{1,0:T(8,128)(2,1)S(1)} %collective-permute-done.17, bf16[4,64,2048]{2,1,0:T(8,128)(2,1)} %collective-permute-done.15, bf16[4,64,2048]{2,1,0:T(8,128)(2,1)S(1)} %get-tuple-element.18), kind=kLoop, calls=%fused_computation.7 | loop fusion | flops 1048576 | bytes 1310720 | tf_op jit(solution)/shard_map/reshape | solution.py:219
  56.5 4.1 %all-to-all-start.1 = ((bf16[8,8,2048]{2,1,0:T(8,128)(2,1)}), bf16[8,8,2048]{2,1,0:T(8,128)(2,1)}, u32[]{:S(2)}, u32[]{:S(2)}) async-start(bf16[8,8,2048]{2,1,0:T(8,128)(2,1)} %fusion.4), calls=%async_computation.1 | async-start | bytes 524288 | tf_op jit(solution)/shard_map/all_to_all | solution.py:185
  62.4 2.6 %forward.1 = (bf16[448,128]{1,0:T(8,128)(2,1)S(1)}, bf16[448,128]{1,0:T(8,128)(2,1)S(1)}, bf16[448,128]{1,0:T(8,128)(2,1)S(1)}, bf16[448,128]{1,0:T(8,128)(2,1)S(1)}, bf16[512,2048]{1,0:T(8,128)(2,1)S(1)}) custom-call(s32[3]{0:T(128)S(1)} %pad_add_fusion.at_ref, bf16[64,2048]{1,0:T(8,128)(2,1)S(1)} %bitcast.35, ...), custom_call_target="tpu_custom_call" | custom-call | flops 939524096 | bytes 6291456 | tf_op jit(solution)/shard_map/forward/pallas_call | solution.py:122
  66.1 2.2 %collective-permute-start.10 = (bf16[448,128]{1,0:T(8,128)(2,1)S(1)}, bf16[448,128]{1,0:T(8,128)(2,1)S(1)}, u32[]{:S(2)}, u32[]{:S(2)}) collective-permute-start(bf16[448,128]{1,0:T(8,128)(2,1)S(1)} %get-tuple-element.16), channel_id=1, source_target_pairs={{0,2},{1,3},{2,0},{3,1},{4,6},{5,7},{6,4},{7,5},{8,10},{9,11},{10,... | collective-permute-start | bytes 344072 | tf_op jit(solution)/shard_map/ppermute | solution.py:194
  69.5 2.9 %wgrad.1 = bf16[448,2048]{1,0:T(8,128)(2,1)} custom-call(bf16[448,512]{1,0:T(8,128)(2,1)S(1)} %copy-done.2, bf16[512,2048]{1,0:T(8,128)(2,1)S(1)} %get-tuple-element.21.a_ref, f32[7,2048]{1,0:T(8,128)S(1)} %copy-done.4), custom_call_target="tpu_custom_call" | custom-call | flops 939524096 | bytes 6291456 | tf_op jit(solution)/shard_map/wgrad/pallas_call | solution.py:148
  72.4 1.3 %collective-permute-done.10.r2 = bf16[448,128]{1,0:T(8,128)(2,1)S(1)} collective-permute-done((bf16[448,128]{1,0:T(8,128)(2,1)S(1)}, bf16[448,128]{1,0:T(8,128)(2,1)S(1)}, u32[]{:S(2)}, u32[]{:S(2)}) %collective-permute-start.10) | collective-permute-done | bytes 114720 | tf_op jit(solution)/shard_map/ppermute | solution.py:194
  73.7 1.4 %finish.1 = bf16[448,128]{1,0:T(8,128)(2,1)} custom-call(s32[3]{0:T(128)S(1)} %pad_add_fusion.at_ref, bf16[448,128]{1,0:T(8,128)(2,1)S(1)} %get-tuple-element.14.r0, bf16[448,128]{1,0:T(8,128)(2,1)S(1)} %collective-permute-done.9.r1, bf16[448,128]{1,0:T(8,128)(2,1)S(1)} %collective-permute-done.10.r2, bf16[448,128]{1,0:T(8,128)(2,1)S(1)} %collective-permute-done.11.r3), custom_call_target="tpu_custom_call" | custom-call | flops 14680064 | bytes 1048576 | tf_op jit(solution)/shard_map/finish/pallas_call | solution.py:173
  75.1 1.6 %reduce_sum.12 = bf16[8,2048]{1,0:T(8,128)(2,1)} reduce(bf16[8,8,2048]{2,1,0:T(8,128)(2,1)} %all-to-all-done.1, bf16[]{:T(256)} %constant.16.clone.1), dimensions={0}, to_apply=%region_0.0 | reduce | flops 114688 | bytes 294914 | tf_op jit(solution)/shard_map/reduce_sum | solution.py:220
  (49 shorter events, 14.1 us)
Async XLA Ops:
  0.6 9.2 %collective-permute-start.14 = (bf16[448,128]{1,0:T(8,128)(2,1)}, bf16[448,128]{1,0:T(8,128)(2,1)S(1)}, u32[]{:S(2)}, u32[]{:S(2)}) collective-permute-start(bf16[448,128]{1,0:T(8,128)(2,1)} %bitcast.37), channel_id=1, source_target_pairs={{0,1},{1,2},{2,3},{3,0},{4,5},{5,6},{6,7},{7,4},{8,9},{9,10},{10,1... | collective-permute-start | bytes 344072 | tf_op jit(solution)/shard_map/ppermute | solution.py:194
  2.8 7.9 %collective-permute-start.13 = (bf16[448,128]{1,0:T(8,128)(2,1)}, bf16[448,128]{1,0:T(8,128)(2,1)S(1)}, u32[]{:S(2)}, u32[]{:S(2)}) collective-permute-start(bf16[448,128]{1,0:T(8,128)(2,1)} %bitcast.38), channel_id=1, source_target_pairs={{0,2},{1,3},{2,0},{3,1},{4,6},{5,7},{6,4},{7,5},{8,10},{9,11},{10,... | collective-permute-start | bytes 344072 | tf_op jit(solution)/shard_map/ppermute | solution.py:194
  5.4 5.2 %collective-permute-start.12 = (bf16[448,128]{1,0:T(8,128)(2,1)}, bf16[448,128]{1,0:T(8,128)(2,1)S(1)}, u32[]{:S(2)}, u32[]{:S(2)}) collective-permute-start(bf16[448,128]{1,0:T(8,128)(2,1)} %bitcast.39), channel_id=1, source_target_pairs={{0,3},{1,0},{2,1},{3,2},{4,7},{5,4},{6,5},{7,6},{8,11},{9,8},{10,9... | collective-permute-start | bytes 344072 | tf_op jit(solution)/shard_map/ppermute | solution.py:194
  15.1 10.5 %collective-permute-start.15 = (bf16[4,64,2048]{2,1,0:T(8,128)(2,1)}, bf16[4,64,2048]{2,1,0:T(8,128)(2,1)}, u32[]{:S(2)}, u32[]{:S(2)}) collective-permute-start(bf16[4,64,2048]{2,1,0:T(8,128)(2,1)} %get-tuple-element.19), channel_id=1, source_target_pairs={{0,4},{4,0},{1,5},{5,1},{2,6},{6,2},{3,7},{7,3},{8,12},{12,8},{9,1... | collective-permute-start | bytes 3145736 | tf_op jit(solution)/shard_map/ppermute | solution.py:194
  17.6 20.3 %all-to-all-start = ((bf16[8,8,2048]{2,1,0:T(8,128)(2,1)}), bf16[8,8,2048]{2,1,0:T(8,128)(2,1)S(1)}, u32[]{:S(2)}, u32[]{:S(2)}) async-start(bf16[8,8,2048]{2,1,0:T(8,128)(2,1)} %broadcast_in_dim.4), calls=%async_computation | async-start | bytes 524288 | tf_op jit(solution)/shard_map/all_to_all | solution.py:185
  27.3 13.3 %collective-permute-start.16 = (bf16[32,2048]{1,0:T(8,128)(2,1)}, bf16[32,2048]{1,0:T(8,128)(2,1)S(1)}, u32[]{:S(2)}, u32[]{:S(2)}) collective-permute-start(bf16[32,2048]{1,0:T(8,128)(2,1)} %get-tuple-element.25), channel_id=1, source_target_pairs={{0,64},{64,128},{128,192},{192,0},{1,65},{65,129},{129,193},{193,1... | collective-permute-start | bytes 393224 | tf_op jit(solution)/shard_map/ppermute | solution.py:194
  28.5 12.1 %collective-permute-start.18 = (bf16[32,2048]{1,0:T(8,128)(2,1)}, bf16[32,2048]{1,0:T(8,128)(2,1)}, u32[]{:S(2)}, u32[]{:S(2)}) collective-permute-start(bf16[32,2048]{1,0:T(8,128)(2,1)} %get-tuple-element.26), channel_id=1, source_target_pairs={{0,192},{64,0},{128,64},{192,128},{1,193},{65,1},{129,65},{193,129... | collective-permute-start | bytes 393224 | tf_op jit(solution)/shard_map/ppermute | solution.py:194
  37.9 8.6 %collective-permute-start.1 = (bf16[64,2048]{1,0:T(8,128)(2,1)S(1)}, bf16[64,2048]{1,0:T(8,128)(2,1)S(1)}, u32[]{:S(2)}, u32[]{:S(2)}) collective-permute-start(bf16[64,2048]{1,0:T(8,128)(2,1)S(1)} %bitcast.32), channel_id=1, source_target_pairs={{0,64},{64,128},{128,192},{192,0},{1,65},{65,129},{129,193},{193,1... | collective-permute-start | bytes 786440 | tf_op jit(solution)/shard_map/ppermute | solution.py:194
  39.1 8.2 %collective-permute-start = (bf16[64,2048]{1,0:T(8,128)(2,1)S(1)}, bf16[64,2048]{1,0:T(8,128)(2,1)}, u32[]{:S(2)}, u32[]{:S(2)}) collective-permute-start(bf16[64,2048]{1,0:T(8,128)(2,1)S(1)} %bitcast.33), channel_id=1, source_target_pairs={{0,192},{64,0},{128,64},{192,128},{1,193},{65,1},{129,65},{193,129... | collective-permute-start | bytes 786440 | tf_op jit(solution)/shard_map/ppermute | solution.py:194
  41.9 10.3 %collective-permute-start.17 = (bf16[64,2048]{1,0:T(8,128)(2,1)S(1)}, bf16[64,2048]{1,0:T(8,128)(2,1)S(1)}, u32[]{:S(2)}, u32[]{:S(2)}) collective-permute-start(bf16[64,2048]{1,0:T(8,128)(2,1)S(1)} %get-tuple-element.23), channel_id=1, source_target_pairs={{0,64},{64,128},{128,192},{192,0},{1,65},{65,129},{129,193},{193,1... | collective-permute-start | bytes 786440 | tf_op jit(solution)/shard_map/ppermute | solution.py:194
  42.0 12.4 %collective-permute-start.19 = (bf16[64,2048]{1,0:T(8,128)(2,1)S(1)}, bf16[64,2048]{1,0:T(8,128)(2,1)S(1)}, u32[]{:S(2)}, u32[]{:S(2)}) collective-permute-start(bf16[64,2048]{1,0:T(8,128)(2,1)S(1)} %get-tuple-element.24), channel_id=1, source_target_pairs={{0,192},{64,0},{128,64},{192,128},{1,193},{65,1},{129,65},{193,129... | collective-permute-start | bytes 786440 | tf_op jit(solution)/shard_map/ppermute | solution.py:194
  44.6 16.5 %collective-permute-start.4 = (bf16[64,2048]{1,0:T(8,128)(2,1)S(1)}, bf16[64,2048]{1,0:T(8,128)(2,1)}, u32[]{:S(2)}, u32[]{:S(2)}) collective-permute-start(bf16[64,2048]{1,0:T(8,128)(2,1)S(1)} %bitcast.34), channel_id=1, source_target_pairs={{0,4},{4,0},{1,5},{5,1},{2,6},{6,2},{3,7},{7,3},{8,12},{12,8},{9,1... | collective-permute-start | bytes 786440 | tf_op jit(solution)/shard_map/ppermute | solution.py:194
  47.2 13.4 %collective-permute-start.2 = (bf16[32,2048]{1,0:T(8,128)(2,1)}, bf16[32,2048]{1,0:T(8,128)(2,1)S(1)}, u32[]{:S(2)}, u32[]{:S(2)}) collective-permute-start(bf16[32,2048]{1,0:T(8,128)(2,1)} %slice.48), channel_id=1, source_target_pairs={{0,64},{64,128},{128,192},{192,0},{1,65},{65,129},{129,193},{193,1... | collective-permute-start | bytes 393224 | tf_op jit(solution)/shard_map/ppermute | solution.py:194
  48.9 12.0 %collective-permute-start.3 = (bf16[32,2048]{1,0:T(8,128)(2,1)}, bf16[32,2048]{1,0:T(8,128)(2,1)}, u32[]{:S(2)}, u32[]{:S(2)}) collective-permute-start(bf16[32,2048]{1,0:T(8,128)(2,1)} %slice.49), channel_id=1, source_target_pairs={{0,192},{64,0},{128,64},{192,128},{1,193},{65,1},{129,65},{193,129... | collective-permute-start | bytes 393224 | tf_op jit(solution)/shard_map/ppermute | solution.py:194
  52.1 10.3 %collective-permute-start.6 = (bf16[64,2048]{1,0:T(8,128)(2,1)S(1)}, bf16[64,2048]{1,0:T(8,128)(2,1)}, u32[]{:S(2)}, u32[]{:S(2)}) collective-permute-start(bf16[64,2048]{1,0:T(8,128)(2,1)S(1)} %collective-permute-done.1.refs_2_), channel_id=1, source_target_pairs={{0,4},{4,0},{1,5},{5,1},{2,6},{6,2},{3,7},{7,3},{8,12},{12,8},{9,1... | collective-permute-start | bytes 786440 | tf_op jit(solution)/shard_map/ppermute | solution.py:194
  54.4 8.1 %collective-permute-start.5 = (bf16[64,2048]{1,0:T(8,128)(2,1)}, bf16[64,2048]{1,0:T(8,128)(2,1)}, u32[]{:S(2)}, u32[]{:S(2)}) collective-permute-start(bf16[64,2048]{1,0:T(8,128)(2,1)} %collective-permute-done.refs_1_), channel_id=1, source_target_pairs={{0,4},{4,0},{1,5},{5,1},{2,6},{6,2},{3,7},{7,3},{8,12},{12,8},{9,1... | collective-permute-start | bytes 786440 | tf_op jit(solution)/shard_map/ppermute | solution.py:194
  56.5 18.6 %all-to-all-start.1 = ((bf16[8,8,2048]{2,1,0:T(8,128)(2,1)}), bf16[8,8,2048]{2,1,0:T(8,128)(2,1)}, u32[]{:S(2)}, u32[]{:S(2)}) async-start(bf16[8,8,2048]{2,1,0:T(8,128)(2,1)} %fusion.4), calls=%async_computation.1 | async-start | bytes 524288 | tf_op jit(solution)/shard_map/all_to_all | solution.py:185
  60.5 9.0 %copy-start.2 = (bf16[448,512]{1,0:T(8,128)(2,1)S(1)}, bf16[448,512]{1,0:T(8,128)(2,1)}, u32[]{:S(2)}) copy-start(bf16[448,512]{1,0:T(8,128)(2,1)} %copy-done.1) | copy-start | bytes 1376260
  60.5 9.0 %copy-start.4 = (f32[7,2048]{1,0:T(8,128)S(1)}, f32[7,2048]{1,0:T(8,128)}, u32[]{:S(2)}) copy-start(f32[7,2048]{1,0:T(8,128)} %copy-done.3) | copy-start | bytes 172036
  60.6 1.4 %collective-permute-start.7 = (bf16[32,2048]{1,0:T(8,128)(2,1)S(1)}, bf16[32,2048]{1,0:T(8,128)(2,1)S(1)}, u32[]{:S(2)}, u32[]{:S(2)}) collective-permute-start(bf16[32,2048]{1,0:T(8,128)(2,1)S(1)} %collective-permute-done.2.refs_3_), channel_id=1, source_target_pairs={{0,4},{4,0},{1,5},{5,1},{2,6},{6,2},{3,7},{7,3},{8,12},{12,8},{9,1... | collective-permute-start | bytes 393224 | tf_op jit(solution)/shard_map/ppermute | solution.py:194
  60.9 1.6 %collective-permute-start.8 = (bf16[32,2048]{1,0:T(8,128)(2,1)}, bf16[32,2048]{1,0:T(8,128)(2,1)S(1)}, u32[]{:S(2)}, u32[]{:S(2)}) collective-permute-start(bf16[32,2048]{1,0:T(8,128)(2,1)} %collective-permute-done.3.refs_4_), channel_id=1, source_target_pairs={{0,4},{4,0},{1,5},{5,1},{2,6},{6,2},{3,7},{7,3},{8,12},{12,8},{9,1... | collective-permute-start | bytes 393224 | tf_op jit(solution)/shard_map/ppermute | solution.py:194
  65.0 7.4 %collective-permute-start.9 = (bf16[448,128]{1,0:T(8,128)(2,1)S(1)}, bf16[448,128]{1,0:T(8,128)(2,1)S(1)}, u32[]{:S(2)}, u32[]{:S(2)}) collective-permute-start(bf16[448,128]{1,0:T(8,128)(2,1)S(1)} %get-tuple-element.15), channel_id=1, source_target_pairs={{0,1},{1,2},{2,3},{3,0},{4,5},{5,6},{6,7},{7,4},{8,9},{9,10},{10,1... | collective-permute-start | bytes 344072 | tf_op jit(solution)/shard_map/ppermute | solution.py:194
  66.1 7.6 %collective-permute-start.10 = (bf16[448,128]{1,0:T(8,128)(2,1)S(1)}, bf16[448,128]{1,0:T(8,128)(2,1)S(1)}, u32[]{:S(2)}, u32[]{:S(2)}) collective-permute-start(bf16[448,128]{1,0:T(8,128)(2,1)S(1)} %get-tuple-element.16), channel_id=1, source_target_pairs={{0,2},{1,3},{2,0},{3,1},{4,6},{5,7},{6,4},{7,5},{8,10},{9,11},{10,... | collective-permute-start | bytes 344072 | tf_op jit(solution)/shard_map/ppermute | solution.py:194
  68.2 5.4 %collective-permute-start.11 = (bf16[448,128]{1,0:T(8,128)(2,1)S(1)}, bf16[448,128]{1,0:T(8,128)(2,1)S(1)}, u32[]{:S(2)}, u32[]{:S(2)}) collective-permute-start(bf16[448,128]{1,0:T(8,128)(2,1)S(1)} %get-tuple-element.17), channel_id=1, source_target_pairs={{0,3},{1,0},{2,1},{3,2},{4,7},{5,4},{6,5},{7,6},{8,11},{9,8},{10,9... | collective-permute-start | bytes 344072 | tf_op jit(solution)/shard_map/ppermute | solution.py:194
  (6 other events, 12.7 us)

commit v3 on v2

v3 whole, which is shorter than its diff:
```python
import jax
import jax.numpy as jnp
from jax import lax
from jax.experimental import pallas as pl
from jax.experimental.pallas import tpu as pltpu
from jax.sharding import Mesh
from jax.sharding import PartitionSpec as P

WIDE = ("x", "z", "core")
BF = jnp.bfloat16
F32 = jnp.float32
VMEM = pl.BlockSpec(memory_space=pltpu.VMEM)
HBM = pl.BlockSpec(memory_space=pltpu.HBM)
SMEM = pl.BlockSpec(memory_space=pltpu.SMEM)


def cost(flops, moved):
    return pl.CostEstimate(flops=flops, bytes_accessed=moved, transcendentals=0)


def grant(mib):
    return pltpu.CompilerParams(vmem_limit_bytes=mib << 20)


def in_hbm(array):
    return pltpu.with_memory_space_constraint(array, pltpu.HBM)


def shaped(*dims, kind=BF):
    return jax.ShapeDtypeStruct(dims, kind)


def spread(mask, cols):
    cols_b = mask.shape[1]
    side = cols // cols_b
    block = lax.broadcasted_iota(jnp.int32, (cols_b, cols), 0)
    at = lax.broadcasted_iota(jnp.int32, (cols_b, cols), 1)
    first = block * side
    pick = jnp.logical_and(at >= first, at < first + side).astype(F32)
    return jnp.dot(mask.astype(F32), pick, preferred_element_type=F32)


def own_first(core, tokens):
    new = lax.broadcasted_iota(jnp.int32, (tokens, tokens), 0)
    old = lax.broadcasted_iota(jnp.int32, (tokens, tokens), 1)
    half = tokens // 2
    other = (new >= half).astype(jnp.int32)
    within = new - other * half
    group = jnp.right_shift(within, 3)
    src = group * 16 + jnp.bitwise_xor(other, core) * 8 + (within - group * 8)
    return (src == old).astype(BF)


def dgrad_kernel(at_ref, m_ref, d0, d1, d2, d3, w_hbm, keep_ref, send_ref, dy_ref, masked_ref, wide_ref, d_ref, w_ref, d_sems, sems):
    x, y, core = at_ref[0], at_ref[1], at_ref[2]
    hidden, tokens = d0.shape
    cols = w_ref.shape[1]
    loads = [
        pltpu.make_async_copy(d, d_ref.at[k], d_sems.at[k]) for k, d in enumerate((d0, d1, d2, d3))
    ]
    for load in loads:
        load.start()
    rows_b = m_ref.shape[0]
    side = hidden // rows_b

    def fetch(i):
        span = pl.ds(i * side, side)
        return pltpu.make_async_copy(w_hbm.at[span], w_ref.at[span], sems.at[i])

    for i in range(rows_b):
        fetch(i).start()
    half = tokens // 2
    order = own_first(core, tokens)
    wide = spread(m_ref[...], cols)
    wide_ref[...] = wide
    for k, load in enumerate(loads):
        block = lax.rem(y + k, 4)
        load.wait()
        rows = lax.dot_general(
            order, d_ref[k], (((1,), (1,)), ((), ())), preferred_element_type=F32
        ).astype(BF)
        dy_ref[pl.ds(pl.multiple_of(block * half, half), half), :] = rows[:half]
        dy_ref[pl.ds(pl.multiple_of((block + 4) * half, half), half), :] = rows[half:]
    for i in range(rows_b):
        fetch(i).wait()
        span = pl.ds(i * side, side)
        masked_ref[span, :] = w_ref[span, :] * wide[i : i + 1, :].astype(BF)
    steps = 4
    tile = cols // steps
    for j in range(steps):
        span = pl.ds(j * tile, tile)
        total = jnp.dot(dy_ref[...], masked_ref[:, span], preferred_element_type=F32).astype(BF)
        for b in range(4):
            rel = lax.rem(b - x + 4, 4)
            keep_ref[rel, :, span] = total[b * half : (b + 1) * half]
            send_ref[rel, :, span] = total[(b + 4) * half : (b + 5) * half]


def dgrad(at, blocks, mt, wt):
    hidden, tokens = blocks[0].shape
    cols = wt.shape[1]
    half = shaped(4, tokens // 2, cols)
    return pl.pallas_call(
        dgrad_kernel,
        out_shape=(
            half,
            half,
            shaped(4 * tokens, hidden),
            shaped(hidden, cols),
            shaped(mt.shape[0], cols, kind=F32),
        ),
        in_specs=[SMEM, VMEM] + [HBM] * 5,
        out_specs=(VMEM,) * 5,
        scratch_shapes=[
            pltpu.VMEM((4, hidden, tokens), BF),
            pltpu.VMEM((hidden, cols), BF),
            pltpu.SemaphoreType.DMA((4,)),
            pltpu.SemaphoreType.DMA((mt.shape[0],)),
        ],
        cost_estimate=cost(8 * tokens * hidden * cols, 4 << 20),
        compiler_params=grant(20),
        name="dgrad",
    )(at, mt, *blocks, wt)


def fwd_kernel(at_ref, mine_ref, other_ref, w_ref, o0, o1, o2, o3, sum_ref, acc_ref):
    step = pl.program_id(0)
    rows = mine_ref.shape[0]

    @pl.when(step == 0)
    def _():
        sum_ref[...] = jnp.zeros_like(sum_ref)

    for h, ref in enumerate((mine_ref, other_ref)):
        sum_ref[:, h * rows : (h + 1) * rows] += lax.dot_general(
            w_ref[...], ref[...], (((1,), (1,)), ((), ())), preferred_element_type=F32
        )

    @pl.when(step == pl.num_programs(0) - 1)
    def _():
        y = at_ref[1]
        half = rows // 4
        tokens = 2 * half
        for b in range(4):
            own = sum_ref[:, b * half : (b + 1) * half]
            far = sum_ref[:, rows + b * half : rows + (b + 1) * half]
            acc_ref[:, b * tokens : (b + 1) * tokens] = jnp.concatenate([own, far], axis=1).astype(BF)
        for k, out in enumerate((o0, o1, o2, o3)):
            block = lax.rem(y + k, 4)
            out[...] = acc_ref[:, pl.ds(pl.multiple_of(block * tokens, tokens), tokens)]


def forward(at, mine, other, masked):
    rows, cols = mine.shape
    hidden = masked.shape[0]
    out = shaped(hidden, rows // 2)
    steps = 4
    tile = cols // steps
    tokens = pl.BlockSpec((rows, tile), lambda i: (0, i))
    whole = pl.BlockSpec((hidden, rows // 2), lambda i: (0, 0))
    return pl.pallas_call(
        fwd_kernel,
        out_shape=(out,) * 4,
        grid=(steps,),
        in_specs=[SMEM, tokens, tokens, pl.BlockSpec((hidden, tile), lambda i: (0, i))],
        out_specs=(whole,) * 4,
        scratch_shapes=[pltpu.VMEM((hidden, 2 * rows), F32), pltpu.VMEM((hidden, 2 * rows), BF)],
        cost_estimate=cost(4 * rows * hidden * cols, 6 << 20),
        compiler_params=grant(14),
        name="forward",
    )(at, mine, other, masked)


def wgrad_kernel(dy_ref, mine_ref, other_ref, wide_ref, o_ref, dyt_ref):
    @pl.when(pl.program_id(0) == 0)
    def _():
        dyt_ref[...] = dy_ref[...].T

    rows = mine_ref.shape[0]
    total = jnp.dot(dyt_ref[:, :rows], mine_ref[...], preferred_element_type=F32)
    total += jnp.dot(dyt_ref[:, rows:], other_ref[...], preferred_element_type=F32)
    rows_b = wide_ref.shape[0]
    side = total.shape[0] // rows_b
    for i in range(rows_b):
        span = slice(i * side, (i + 1) * side)
        o_ref[span, :] = (total[span] * wide_ref[i : i + 1, :]).astype(BF)


def wgrad(dy, mine, other, wide):
    rows, hidden = dy.shape
    cols = mine.shape[1]
    steps = 4
    tile = cols // steps
    return pl.pallas_call(
        wgrad_kernel,
        out_shape=shaped(hidden, cols),
        grid=(steps,),
        in_specs=[
            pl.BlockSpec((rows, hidden), lambda i: (0, 0)),
            pl.BlockSpec((rows // 2, tile), lambda i: (0, i)),
            pl.BlockSpec((rows // 2, tile), lambda i: (0, i)),
            pl.BlockSpec((wide.shape[0], tile), lambda i: (0, i)),
        ],
        out_specs=pl.BlockSpec((hidden, tile), lambda i: (0, i)),
        scratch_shapes=[pltpu.VMEM((hidden, rows), BF)],
        cost_estimate=cost(2 * rows * hidden * cols, 6 << 20),
        compiler_params=grant(14),
        name="wgrad",
    )(dy, mine, other, wide)


def finish_kernel(at_ref, r0, r1, r2, r3, o_ref):
    total = (r0[...].astype(F32) + r1[...].astype(F32)) + (
        r2[...].astype(F32) + r3[...].astype(F32)
    )
    back = own_first(at_ref[2], r0.shape[1])
    o_ref[...] = jnp.dot(total.astype(BF), back, preferred_element_type=F32).astype(BF)


def finish(at, parts):
    return pl.pallas_call(
        finish_kernel,
        out_shape=shaped(*parts[0].shape),
        in_specs=[SMEM] + [VMEM] * 4,
        out_specs=VMEM,
        cost_estimate=cost(parts[0].size * 256, 1 << 20),
        compiler_params=grant(6),
        name="finish",
    )(at, *parts)


def exchange(blocks, axis):
    return lax.all_to_all(blocks, axis, split_axis=0, concat_axis=0, tiled=True)


def copies(array, axis):
    return jnp.broadcast_to(array, (lax.psum(1, axis), *array.shape))


def to(array, axis, step):
    n = lax.axis_size(axis)
    return lax.ppermute(array, axis, [(i, (i + step) % n) for i in range(n)])


def added(*terms):
    return sum(t.astype(F32) for t in terms).astype(BF)


def on_device(activations, up_weight, block_mask, out_grad):
    at = jnp.stack([lax.axis_index(n).astype(jnp.int32) for n in ("x", "narrow", "core")])
    wt, mt, dyt = up_weight.T, block_mask.T, out_grad.T

    blocks = (dyt, to(dyt, "narrow", -1), to(dyt, "narrow", 2), to(dyt, "narrow", 1))
    mine = exchange(copies(activations, ("x", "z")), ("x", "z")).reshape(-1, activations.shape[1])

    keep, send, dy, masked, wide = dgrad(at, [in_hbm(b) for b in blocks], mt, in_hbm(wt))
    got = to(send, "core", 1)
    half = keep.shape[1] // 2
    ahead = to(added(keep[2, :half], got[2, :half]), "x", 1)
    behind = to(added(keep[2, half:], got[2, half:]), "x", -1)
    none = jnp.zeros_like(ahead)
    right = added(keep[1], got[1], jnp.concatenate([ahead, none]))
    left = added(keep[3], got[3], jnp.concatenate([none, behind]))
    along_x = added(keep[0], got[0], to(right, "x", 1), to(left, "x", -1))
    along_z = exchange(along_x.reshape(8, 8, -1), "z")
    input_grad = along_z.astype(F32).sum(axis=0).astype(BF)

    other = to(mine, "core", 1)
    o0, o1, o2, o3 = forward(at, mine, other, masked)
    parts = (o0, to(o1, "narrow", 1), to(o2, "narrow", 2), to(o3, "narrow", -1))
    output = finish(at, parts).T
    weight_grad = wgrad(dy, mine, other, wide).T
    return (output, input_grad, weight_grad)


def solution(mesh):
    torus = Mesh(
        mesh.devices.reshape(4, 8, 2, mesh.shape["narrow"]),
        ("x", "z", "core", "narrow"),
    )
    return jax.shard_map(
        on_device,
        mesh=torus,
        in_specs=(P(WIDE, "narrow"), P("narrow", WIDE), P("narrow", WIDE), P("narrow", WIDE)),
        out_specs=(P("narrow", WIDE), P(WIDE, "narrow"), P("narrow", WIDE)),
        check_vma=False,
    )
```

time: 77.2 us -> 85.8 us (1.11)
  waiting for transfers between devices: 12.3 us -> 28.7 us
  starting transfers between devices: 39.6 us -> 31.3 us
  Pallas kernels: 10.9 us -> 12.1 us
    ppermute x20 -> x12, starting transfers between devices: 27.6 us -> 16.2 us  [to(): return lax.ppermute(array, axis, [(i, (i + step) % n) for i in range(n)])]
    ppermute x20 -> x12, waiting for transfers between devices: 4.38 us -> 14.5 us  [to(): return lax.ppermute(array, axis, [(i, (i + step) % n) for i in range(n)])]
    all_to_all x2, waiting for transfers between devices: 7.95 us -> 14.1 us  [exchange(): return lax.all_to_all(blocks, axis, split_axis=0, concat_axis=0, tiled=True)]
    all_to_all x2, starting transfers between devices: 12 us -> 15.1 us  [exchange(): return lax.all_to_all(blocks, axis, split_axis=0, concat_axis=0, tiled=True)]
    slice x2 -> x0, local copies, waits for them, and re-layouts: 2.23 us -> none  [on_device(): far_low, far_high = (to(before[:half], 'x', 1), to(after[half:], 'x', -1))]
    unnamed x16 -> x18, local copies, waits for them, and re-layouts: 3.63 us -> 4.85 us
    pallas_call x3 -> x2, Pallas kernels: 6.61 us -> 7.64 us  [the longest x1 4.07 us: dgrad(): pl.pallas_call(dgrad_kernel, out_shape=(half, half, shaped(4 * tokens, hi...]
  transfers between devices with their start and end apart: 22 -> 14, of which waited for: 7 -> 7; matrix products, arithmetic and copies ran while one was open for 10% -> 9% of each run, Pallas kernels for 10% -> 8%
where the time goes in v3:
time: 85.8 us; the launch traced here: 85.3 us
  starting transfers between devices  31.3 us (36%)
  waiting for transfers between devices  28.7 us (33%)
  Pallas kernels  12.1 us (14%)
  other arithmetic  6.62 us (8%)
  local copies, waits for them, and re-layouts  5.94 us (7%)
    ppermute x12, starting transfers between devices, to(): return lax.ppermute(array, axis, [(i, (i + step) % n) for i in range(n)])  16.2 us
    all_to_all x2, starting transfers between devices, exchange(): return lax.all_to_all(blocks, axis, split_axis=0, concat_axis=0, tiled=True)  15.1 us
    ppermute x12, waiting for transfers between devices, to(): return lax.ppermute(array, axis, [(i, (i + step) % n) for i in range(n)])  14.5 us
    all_to_all x2, waiting for transfers between devices, exchange(): return lax.all_to_all(blocks, axis, split_axis=0, concat_axis=0, tiled=True)  14.1 us
    unnamed x18, local copies, waits for them, and re-layouts  4.85 us
    pallas_call x1, Pallas kernels, dgrad(): pl.pallas_call(dgrad_kernel, out_shape=(half, half, shaped(4 * tokens, hi...  4.07 us
    pallas_call x1, Pallas kernels, forward(): pl.pallas_call(fwd_kernel, out_shape=(out,) * 4, grid=(steps,), in_specs=...  3.58 us
    pallas_call x1, Pallas kernels, wgrad(): pl.pallas_call(wgrad_kernel, out_shape=shaped(hidden, cols), grid=(steps,...  3.09 us
  transfers between devices with their start and end apart: 14, of which 7 were waited for; matrix products, arithmetic and copies ran while one was open for 9% of the time, Pallas kernels for 8%

profile of v3, /device:TPU:1, one launch (start us, length us, event | category | flops | bytes accessed | tf_op | source)
XLA Modules:
  0.0 85.3 jit_solution(14401685501906009166)
XLA Ops:
  0.6 3.6 %collective-permute-start.1 = (bf16[448,128]{1,0:T(8,128)(2,1)}, bf16[448,128]{1,0:T(8,128)(2,1)S(1)}, u32[]{:S(2)}, u32[]{:S(2)}) collective-permute-start(bf16[448,128]{1,0:T(8,128)(2,1)} %bitcast.38), channel_id=1, source_target_pairs={{0,3},{1,0},{2,1},{3,2},{4,7},{5,4},{6,5},{7,6},{8,11},{9,8},{10,9... | collective-permute-start | bytes 344072 | tf_op jit(solution)/shard_map/ppermute | solution.py:242
  5.4 2.2 %collective-permute-done.1.d1 = bf16[448,128]{1,0:T(8,128)(2,1)S(1)} collective-permute-done((bf16[448,128]{1,0:T(8,128)(2,1)}, bf16[448,128]{1,0:T(8,128)(2,1)S(1)}, u32[]{:S(2)}, u32[]{:S(2)}) %collective-permute-start.1) | collective-permute-done | bytes 114720 | tf_op jit(solution)/shard_map/ppermute | solution.py:242
  7.6 2.2 %collective-permute-done.2.d2 = bf16[448,128]{1,0:T(8,128)(2,1)S(1)} collective-permute-done((bf16[448,128]{1,0:T(8,128)(2,1)}, bf16[448,128]{1,0:T(8,128)(2,1)S(1)}, u32[]{:S(2)}, u32[]{:S(2)}) %collective-permute-start.2) | collective-permute-done | bytes 114720 | tf_op jit(solution)/shard_map/ppermute | solution.py:242
  9.7 3.5 %collective-permute-done.3.d3 = bf16[448,128]{1,0:T(8,128)(2,1)S(1)} collective-permute-done((bf16[448,128]{1,0:T(8,128)(2,1)}, bf16[448,128]{1,0:T(8,128)(2,1)S(1)}, u32[]{:S(2)}, u32[]{:S(2)}) %collective-permute-start.3) | collective-permute-done | bytes 114720 | tf_op jit(solution)/shard_map/ppermute | solution.py:242
  14.6 4.1 %dgrad.1 = (bf16[4,64,2048]{2,1,0:T(8,128)(2,1)S(1)}, bf16[4,64,2048]{2,1,0:T(8,128)(2,1)S(1)}, bf16[512,448]{1,0:T(8,128)(2,1)S(1)}, bf16[448,2048]{1,0:T(8,128)(2,1)S(1)}, f32[7,2048]{1,0:T(8,128)S(1)}) custom-call(s32[3]{0:T(128)S(1)} %pad_add_fusion.at_ref, s32[7,32]{1,0:T(8,128)S(1)} %bitcast.34, bf16[448,128]{1,0:T(8,128)(2,1)} %bitcast.41, ...), custom_call_target="tpu_custom_call" | custom-call | flops 939524096 | bytes 4194304 | tf_op jit(solution)/shard_map/dgrad/pallas_call | solution.py:103
  18.7 1.2 %copy-done = bf16[448,2048]{1,0:T(8,128)(2,1)} copy-done((bf16[448,2048]{1,0:T(8,128)(2,1)}, bf16[448,2048]{1,0:T(8,128)(2,1)S(1)}, u32[]{:S(2)}) %copy-start) | copy-done | bytes 1835032
  21.4 1.1 %broadcast_in_dim.4 = bf16[32,8,2048]{2,1,0:T(8,128)(2,1)} broadcast(bf16[8,2048]{1,0:T(8,128)(2,1)S(1)} %copy-done.5), dimensions={1,2} | broadcast | bytes 1081344 | tf_op jit(solution)/shard_map/broadcast_in_dim | solution.py:237
  22.5 11.0 %all-to-all-start = ((bf16[32,8,2048]{2,1,0:T(8,128)(2,1)}), bf16[32,8,2048]{2,1,0:T(8,128)(2,1)S(1)}, u32[]{:S(2)}, u32[]{:S(2)}) async-start(bf16[32,8,2048]{2,1,0:T(8,128)(2,1)} %broadcast_in_dim.4), calls=%async_computation | async-start | bytes 2097152 | tf_op jit(solution)/shard_map/all_to_all | solution.py:233
  34.6 2.6 %collective-permute-start.10 = (bf16[32,2048]{1,0:T(8,128)(2,1)S(1)}, bf16[32,2048]{1,0:T(8,128)(2,1)S(1)}, u32[]{:S(2)}, u32[]{:S(2)}) collective-permute-start(bf16[32,2048]{1,0:T(8,128)(2,1)S(1)} %get-tuple-element.24), channel_id=1, source_target_pairs={{0,192},{64,0},{128,64},{192,128},{1,193},{65,1},{129,65},{193,129... | collective-permute-start | bytes 393224 | tf_op jit(solution)/shard_map/ppermute | solution.py:242
  37.2 3.6 %collective-permute-done.10 = bf16[32,2048]{1,0:T(8,128)(2,1)S(1)} collective-permute-done((bf16[32,2048]{1,0:T(8,128)(2,1)S(1)}, bf16[32,2048]{1,0:T(8,128)(2,1)S(1)}, u32[]{:S(2)}, u32[]{:S(2)}) %collective-permute-start.10) | collective-permute-done | bytes 131104 | tf_op jit(solution)/shard_map/ppermute | solution.py:242
  40.7 3.1 %collective-permute-done.8 = bf16[32,2048]{1,0:T(8,128)(2,1)S(1)} collective-permute-done((bf16[32,2048]{1,0:T(8,128)(2,1)S(1)}, bf16[32,2048]{1,0:T(8,128)(2,1)S(1)}, u32[]{:S(2)}, u32[]{:S(2)}) %collective-permute-start.8) | collective-permute-done | bytes 131104 | tf_op jit(solution)/shard_map/ppermute | solution.py:242
  43.8 2.0 %fusion.1 = (bf16[64,2048]{1,0:T(8,128)(2,1)}, bf16[64,2048]{1,0:T(8,128)(2,1)}) fusion(bf16[4,64,2048]{2,1,0:T(8,128)(2,1)} %collective-permute-done.7, bf16[32,2048]{1,0:T(8,128)(2,1)S(1)} %collective-permute-done.8, bf16[4,64,2048]{2,1,0:T(8,128)(2,1)S(1)} %get-tuple-element.17, bf16[32,2048]{1,0:T(8,128)(2,1)S(1)} %collective-permute-done.10), kind=kLoop, calls=%fused_computation.3 | loop fusion | flops 1572864 | bytes 1835008 | tf_op jit(solution)/shard_map/convert_element_type | solution.py:246
  47.3 11.7 %all-to-all-done = bf16[32,8,2048]{2,1,0:T(8,128)(2,1)S(1)} async-done(((bf16[32,8,2048]{2,1,0:T(8,128)(2,1)}), bf16[32,8,2048]{2,1,0:T(8,128)(2,1)S(1)}, u32[]{:S(2)}, u32[]{:S(2)}) %all-to-all-start) | async-done | bytes 1048608 | tf_op jit(solution)/shard_map/all_to_all | solution.py:233
  59.0 4.1 %collective-permute-start = (bf16[256,2048]{1,0:T(8,128)(2,1)S(1)}, bf16[256,2048]{1,0:T(8,128)(2,1)S(1)}, u32[]{:S(2)}, u32[]{:S(2)}) collective-permute-start(bf16[256,2048]{1,0:T(8,128)(2,1)S(1)} %bitcast.31), channel_id=1, source_target_pairs={{0,4},{4,0},{1,5},{5,1},{2,6},{6,2},{3,7},{7,3},{8,12},{12,8},{9,1... | collective-permute-start | bytes 3145736 | tf_op jit(solution)/shard_map/ppermute | solution.py:242
  63.0 1.9 %fusion.4 = bf16[8,8,2048]{2,1,0:T(8,128)(2,1)} fusion(bf16[64,2048]{1,0:T(8,128)(2,1)S(1)} %collective-permute-done.11, bf16[64,2048]{1,0:T(8,128)(2,1)} %collective-permute-done.9, bf16[4,64,2048]{2,1,0:T(8,128)(2,1)} %collective-permute-done.7, bf16[4,64,2048]{2,1,0:T(8,128)(2,1)S(1)} %get-tuple-element.17), kind=kLoop, calls=%fused_computation.7 | loop fusion | flops 1048576 | bytes 1310720 | tf_op jit(solution)/shard_map/reshape | solution.py:265
  64.9 4.1 %all-to-all-start.1 = ((bf16[8,8,2048]{2,1,0:T(8,128)(2,1)}), bf16[8,8,2048]{2,1,0:T(8,128)(2,1)}, u32[]{:S(2)}, u32[]{:S(2)}) async-start(bf16[8,8,2048]{2,1,0:T(8,128)(2,1)} %fusion.4), calls=%async_computation.1 | async-start | bytes 524288 | tf_op jit(solution)/shard_map/all_to_all | solution.py:233
  69.0 1.5 %copy-done.1 = bf16[448,2048]{1,0:T(8,128)(2,1)S(1)} copy-done((bf16[448,2048]{1,0:T(8,128)(2,1)S(1)}, bf16[448,2048]{1,0:T(8,128)(2,1)}, u32[]{:S(2)}) %copy-start.1) | copy-done | bytes 1835032
  70.5 3.6 %forward.1 = (bf16[448,128]{1,0:T(8,128)(2,1)S(1)}, bf16[448,128]{1,0:T(8,128)(2,1)}, bf16[448,128]{1,0:T(8,128)(2,1)S(1)}, bf16[448,128]{1,0:T(8,128)(2,1)S(1)}) custom-call(s32[3]{0:T(128)S(1)} %pad_add_fusion.at_ref, bf16[256,2048]{1,0:T(8,128)(2,1)S(1)} %bitcast.32, bf16[256,2048]{1,0:T(8,128)(2,1)S(1)} %collective-permute-done.other_ref, ...), custom_call_target="tpu_custom_call" | custom-call | flops 939524096 | bytes 6291456 | tf_op jit(solution)/shard_map/forward/pallas_call | solution.py:161
  74.1 1.5 %collective-permute-start.5 = (bf16[448,128]{1,0:T(8,128)(2,1)S(1)}, bf16[448,128]{1,0:T(8,128)(2,1)S(1)}, u32[]{:S(2)}, u32[]{:S(2)}) collective-permute-start(bf16[448,128]{1,0:T(8,128)(2,1)S(1)} %get-tuple-element.15), channel_id=1, source_target_pairs={{0,2},{1,3},{2,0},{3,1},{4,6},{5,7},{6,4},{7,5},{8,10},{9,11},{10,... | collective-permute-start | bytes 344072 | tf_op jit(solution)/shard_map/ppermute | solution.py:242
  75.6 1.2 %collective-permute-start.6 = (bf16[448,128]{1,0:T(8,128)(2,1)S(1)}, bf16[448,128]{1,0:T(8,128)(2,1)S(1)}, u32[]{:S(2)}, u32[]{:S(2)}) collective-permute-start(bf16[448,128]{1,0:T(8,128)(2,1)S(1)} %get-tuple-element.16), channel_id=1, source_target_pairs={{0,3},{1,0},{2,1},{3,2},{4,7},{5,4},{6,5},{7,6},{8,11},{9,8},{10,9... | collective-permute-start | bytes 344072 | tf_op jit(solution)/shard_map/ppermute | solution.py:242
  76.8 2.5 %all-to-all-done.1 = bf16[8,8,2048]{2,1,0:T(8,128)(2,1)} async-done(((bf16[8,8,2048]{2,1,0:T(8,128)(2,1)}), bf16[8,8,2048]{2,1,0:T(8,128)(2,1)}, u32[]{:S(2)}, u32[]{:S(2)}) %all-to-all-start.1) | async-done | bytes 262176 | tf_op jit(solution)/shard_map/all_to_all | solution.py:233
  79.2 1.6 %reduce_sum.12 = bf16[8,2048]{1,0:T(8,128)(2,1)} reduce(bf16[8,8,2048]{2,1,0:T(8,128)(2,1)} %all-to-all-done.1, bf16[]{:T(256)} %constant.16.clone.1), dimensions={0}, to_apply=%region_0.0 | reduce | flops 114688 | bytes 294914 | tf_op jit(solution)/shard_map/reduce_sum | solution.py:266
  80.8 3.1 %wgrad.1 = bf16[448,2048]{1,0:T(8,128)(2,1)} custom-call(bf16[512,448]{1,0:T(8,128)(2,1)S(1)} %copy-done.3, bf16[256,2048]{1,0:T(8,128)(2,1)S(1)} %bitcast.33, bf16[256,2048]{1,0:T(8,128)(2,1)S(1)} %collective-permute-done.other_ref, f32[7,2048]{1,0:T(8,128)S(1)} %get-tuple-element.20.wide_ref), custom_call_target="tpu_custom_call" | custom-call | flops 939524096 | bytes 6291456 | tf_op jit(solution)/shard_map/wgrad/pallas_call | solution.py:194
  83.9 1.4 %finish.1 = bf16[448,128]{1,0:T(8,128)(2,1)} custom-call(s32[3]{0:T(128)S(1)} %pad_add_fusion.at_ref, bf16[448,128]{1,0:T(8,128)(2,1)S(1)} %get-tuple-element.13.r0, bf16[448,128]{1,0:T(8,128)(2,1)S(1)} %collective-permute-done.4.r1, bf16[448,128]{1,0:T(8,128)(2,1)S(1)} %collective-permute-done.5.r2, bf16[448,128]{1,0:T(8,128)(2,1)S(1)} %collective-permute-done.6.r3), custom_call_target="tpu_custom_call" | custom-call | flops 14680064 | bytes 1048576 | tf_op jit(solution)/shard_map/finish/pallas_call | solution.py:221
  (32 shorter events, 6.5 us)
Async XLA Ops:
  0.6 6.9 %collective-permute-start.1 = (bf16[448,128]{1,0:T(8,128)(2,1)}, bf16[448,128]{1,0:T(8,128)(2,1)S(1)}, u32[]{:S(2)}, u32[]{:S(2)}) collective-permute-start(bf16[448,128]{1,0:T(8,128)(2,1)} %bitcast.38), channel_id=1, source_target_pairs={{0,3},{1,0},{2,1},{3,2},{4,7},{5,4},{6,5},{7,6},{8,11},{9,8},{10,9... | collective-permute-start | bytes 344072 | tf_op jit(solution)/shard_map/ppermute | solution.py:242
  4.3 5.5 %collective-permute-start.2 = (bf16[448,128]{1,0:T(8,128)(2,1)}, bf16[448,128]{1,0:T(8,128)(2,1)S(1)}, u32[]{:S(2)}, u32[]{:S(2)}) collective-permute-start(bf16[448,128]{1,0:T(8,128)(2,1)} %bitcast.39), channel_id=1, source_target_pairs={{0,2},{1,3},{2,0},{3,1},{4,6},{5,7},{6,4},{7,5},{8,10},{9,11},{10,... | collective-permute-start | bytes 344072 | tf_op jit(solution)/shard_map/ppermute | solution.py:242
  4.6 8.6 %collective-permute-start.3 = (bf16[448,128]{1,0:T(8,128)(2,1)}, bf16[448,128]{1,0:T(8,128)(2,1)S(1)}, u32[]{:S(2)}, u32[]{:S(2)}) collective-permute-start(bf16[448,128]{1,0:T(8,128)(2,1)} %bitcast.40), channel_id=1, source_target_pairs={{0,1},{1,2},{2,3},{3,0},{4,5},{5,6},{6,7},{7,4},{8,9},{9,10},{10,1... | collective-permute-start | bytes 344072 | tf_op jit(solution)/shard_map/ppermute | solution.py:242
  7.6 5.7 %copy-start.6 = (bf16[448,128]{1,0:T(8,128)(2,1)}, bf16[448,128]{1,0:T(8,128)(2,1)S(1)}, u32[]{:S(2)}) copy-start(bf16[448,128]{1,0:T(8,128)(2,1)S(1)} %collective-permute-done.1.d1) | copy-start | bytes 344068
  9.7 3.5 %copy-start.7 = (bf16[448,128]{1,0:T(8,128)(2,1)}, bf16[448,128]{1,0:T(8,128)(2,1)S(1)}, u32[]{:S(2)}) copy-start(bf16[448,128]{1,0:T(8,128)(2,1)S(1)} %collective-permute-done.2.d2) | copy-start | bytes 344068
  13.2 0.6 copy-start.8
  13.9 0.7 copy-start.4
  14.6 6.9 %copy-start.5 = (bf16[8,2048]{1,0:T(8,128)(2,1)S(1)}, bf16[8,2048]{1,0:T(8,128)(2,1)}, u32[]{:S(2)}) copy-start(bf16[8,2048]{1,0:T(8,128)(2,1)} %param.4) | copy-start | bytes 98308
  18.6 1.2 %copy-start = (bf16[448,2048]{1,0:T(8,128)(2,1)}, bf16[448,2048]{1,0:T(8,128)(2,1)S(1)}, u32[]{:S(2)}) copy-start(bf16[448,2048]{1,0:T(8,128)(2,1)S(1)} %get-tuple-element.12.w_ref) | copy-start | bytes 5505028
  19.9 0.8 copy-start.2
  20.7 12.9 %collective-permute-start.7 = (bf16[4,64,2048]{2,1,0:T(8,128)(2,1)S(1)}, bf16[4,64,2048]{2,1,0:T(8,128)(2,1)}, u32[]{:S(2)}, u32[]{:S(2)}) collective-permute-start(bf16[4,64,2048]{2,1,0:T(8,128)(2,1)S(1)} %get-tuple-element.18), channel_id=1, source_target_pairs={{0,4},{4,0},{1,5},{5,1},{2,6},{6,2},{3,7},{7,3},{8,12},{12,8},{9,1... | collective-permute-start | bytes 3145736 | tf_op jit(solution)/shard_map/ppermute | solution.py:242
  22.5 36.5 %all-to-all-start = ((bf16[32,8,2048]{2,1,0:T(8,128)(2,1)}), bf16[32,8,2048]{2,1,0:T(8,128)(2,1)S(1)}, u32[]{:S(2)}, u32[]{:S(2)}) async-start(bf16[32,8,2048]{2,1,0:T(8,128)(2,1)} %broadcast_in_dim.4), calls=%async_computation | async-start | bytes 2097152 | tf_op jit(solution)/shard_map/all_to_all | solution.py:233
  34.6 6.1 %collective-permute-start.10 = (bf16[32,2048]{1,0:T(8,128)(2,1)S(1)}, bf16[32,2048]{1,0:T(8,128)(2,1)S(1)}, u32[]{:S(2)}, u32[]{:S(2)}) collective-permute-start(bf16[32,2048]{1,0:T(8,128)(2,1)S(1)} %get-tuple-element.24), channel_id=1, source_target_pairs={{0,192},{64,0},{128,64},{192,128},{1,193},{65,1},{129,65},{193,129... | collective-permute-start | bytes 393224 | tf_op jit(solution)/shard_map/ppermute | solution.py:242
  37.2 6.7 %collective-permute-start.8 = (bf16[32,2048]{1,0:T(8,128)(2,1)S(1)}, bf16[32,2048]{1,0:T(8,128)(2,1)S(1)}, u32[]{:S(2)}, u32[]{:S(2)}) collective-permute-start(bf16[32,2048]{1,0:T(8,128)(2,1)S(1)} %get-tuple-element.23), channel_id=1, source_target_pairs={{0,64},{64,128},{128,192},{192,0},{1,65},{65,129},{129,193},{193,1... | collective-permute-start | bytes 393224 | tf_op jit(solution)/shard_map/ppermute | solution.py:242
  45.9 17.2 %collective-permute-start.11 = (bf16[64,2048]{1,0:T(8,128)(2,1)}, bf16[64,2048]{1,0:T(8,128)(2,1)S(1)}, u32[]{:S(2)}, u32[]{:S(2)}) collective-permute-start(bf16[64,2048]{1,0:T(8,128)(2,1)} %get-tuple-element.22), channel_id=1, source_target_pairs={{0,192},{64,0},{128,64},{192,128},{1,193},{65,1},{129,65},{193,129... | collective-permute-start | bytes 786440 | tf_op jit(solution)/shard_map/ppermute | solution.py:242
  46.4 16.6 %collective-permute-start.9 = (bf16[64,2048]{1,0:T(8,128)(2,1)}, bf16[64,2048]{1,0:T(8,128)(2,1)}, u32[]{:S(2)}, u32[]{:S(2)}) collective-permute-start(bf16[64,2048]{1,0:T(8,128)(2,1)} %get-tuple-element.21), channel_id=1, source_target_pairs={{0,64},{64,128},{128,192},{192,0},{1,65},{65,129},{129,193},{193,1... | collective-permute-start | bytes 786440 | tf_op jit(solution)/shard_map/ppermute | solution.py:242
  59.0 10.0 %collective-permute-start = (bf16[256,2048]{1,0:T(8,128)(2,1)S(1)}, bf16[256,2048]{1,0:T(8,128)(2,1)S(1)}, u32[]{:S(2)}, u32[]{:S(2)}) collective-permute-start(bf16[256,2048]{1,0:T(8,128)(2,1)S(1)} %bitcast.31), channel_id=1, source_target_pairs={{0,4},{4,0},{1,5},{5,1},{2,6},{6,2},{3,7},{7,3},{8,12},{12,8},{9,1... | collective-permute-start | bytes 3145736 | tf_op jit(solution)/shard_map/ppermute | solution.py:242
  64.9 14.3 %all-to-all-start.1 = ((bf16[8,8,2048]{2,1,0:T(8,128)(2,1)}), bf16[8,8,2048]{2,1,0:T(8,128)(2,1)}, u32[]{:S(2)}, u32[]{:S(2)}) async-start(bf16[8,8,2048]{2,1,0:T(8,128)(2,1)} %fusion.4), calls=%async_computation.1 | async-start | bytes 524288 | tf_op jit(solution)/shard_map/all_to_all | solution.py:233
  69.0 1.5 %copy-start.1 = (bf16[448,2048]{1,0:T(8,128)(2,1)S(1)}, bf16[448,2048]{1,0:T(8,128)(2,1)}, u32[]{:S(2)}) copy-start(bf16[448,2048]{1,0:T(8,128)(2,1)} %copy-done) | copy-start | bytes 5505028
  70.5 10.3 %copy-start.3 = (bf16[512,448]{1,0:T(8,128)(2,1)S(1)}, bf16[512,448]{1,0:T(8,128)(2,1)}, u32[]{:S(2)}) copy-start(bf16[512,448]{1,0:T(8,128)(2,1)} %copy-done.2) | copy-start | bytes 1376260
  74.1 9.8 %collective-permute-start.4 = (bf16[448,128]{1,0:T(8,128)(2,1)}, bf16[448,128]{1,0:T(8,128)(2,1)S(1)}, u32[]{:S(2)}, u32[]{:S(2)}) collective-permute-start(bf16[448,128]{1,0:T(8,128)(2,1)} %get-tuple-element.14), channel_id=1, source_target_pairs={{0,1},{1,2},{2,3},{3,0},{4,5},{5,6},{6,7},{7,4},{8,9},{9,10},{10,1... | collective-permute-start | bytes 344072 | tf_op jit(solution)/shard_map/ppermute | solution.py:242
  74.1 9.8 %collective-permute-start.5 = (bf16[448,128]{1,0:T(8,128)(2,1)S(1)}, bf16[448,128]{1,0:T(8,128)(2,1)S(1)}, u32[]{:S(2)}, u32[]{:S(2)}) collective-permute-start(bf16[448,128]{1,0:T(8,128)(2,1)S(1)} %get-tuple-element.15), channel_id=1, source_target_pairs={{0,2},{1,3},{2,0},{3,1},{4,6},{5,7},{6,4},{7,5},{8,10},{9,11},{10,... | collective-permute-start | bytes 344072 | tf_op jit(solution)/shard_map/ppermute | solution.py:242
  75.6 8.4 %collective-permute-start.6 = (bf16[448,128]{1,0:T(8,128)(2,1)S(1)}, bf16[448,128]{1,0:T(8,128)(2,1)S(1)}, u32[]{:S(2)}, u32[]{:S(2)}) collective-permute-start(bf16[448,128]{1,0:T(8,128)(2,1)S(1)} %get-tuple-element.16), channel_id=1, source_target_pairs={{0,3},{1,0},{2,1},{3,2},{4,7},{5,4},{6,5},{7,6},{8,11},{9,8},{10,9... | collective-permute-start | bytes 344072 | tf_op jit(solution)/shard_map/ppermute | solution.py:242

commit v4 on v2

v4 whole, which is shorter than its diff:
```python
import functools

import jax
import jax.numpy as jnp
from jax import lax
from jax.experimental import pallas as pl
from jax.experimental.pallas import tpu as pltpu
from jax.sharding import Mesh
from jax.sharding import PartitionSpec as P

WIDE = ("x", "z", "core")
BF = jnp.bfloat16
F32 = jnp.float32
VMEM = pl.BlockSpec(memory_space=pltpu.VMEM)
HBM = pl.BlockSpec(memory_space=pltpu.HBM)
SMEM = pl.BlockSpec(memory_space=pltpu.SMEM)


def cost(flops, moved):
    return pl.CostEstimate(flops=flops, bytes_accessed=moved, transcendentals=0)


def grant(mib):
    return pltpu.CompilerParams(vmem_limit_bytes=mib << 20)


def in_hbm(array):
    return pltpu.with_memory_space_constraint(array, pltpu.HBM)


def shaped(*dims, kind=BF):
    return jax.ShapeDtypeStruct(dims, kind)


def spread(mask, start, tile, cols):
    cols_b = mask.shape[1]
    side = cols // cols_b
    block = lax.broadcasted_iota(jnp.int32, (cols_b, tile), 0)
    at = lax.broadcasted_iota(jnp.int32, (cols_b, tile), 1) + start
    first = block * side
    pick = jnp.logical_and(at >= first, at < first + side).astype(F32)
    return jnp.dot(mask.astype(F32), pick, preferred_element_type=F32)


def own_first(core, z, tokens):
    new = lax.broadcasted_iota(jnp.int32, (tokens, tokens), 0)
    old = lax.broadcasted_iota(jnp.int32, (tokens, tokens), 1)
    half = tokens // 2
    other = (new >= half).astype(jnp.int32)
    within = new - other * half
    group = jnp.right_shift(within, 3)
    row = within - group * 8
    low = jnp.right_shift(group, 2)
    mid = jnp.bitwise_and(group, 2)
    high = jnp.bitwise_and(group, 1) * 4
    src = jnp.bitwise_xor(low + mid + high, z) * 16 + jnp.bitwise_xor(other, core) * 8 + row
    return (src == old).astype(BF)


def mask_kernel(m_hbm, w_hbm, masked_ref, m_ref, w_ref, m_sem, sems):
    rows, cols = w_ref.shape
    rows_b = m_ref.shape[0]
    side = rows // rows_b
    spans = [pl.ds(i * side, side) for i in range(rows_b)]
    first = pltpu.make_async_copy(m_hbm, m_ref, m_sem)
    first.start()
    loads = [
        pltpu.make_async_copy(w_hbm.at[span], w_ref.at[span], sems.at[i])
        for i, span in enumerate(spans)
    ]
    for load in loads:
        load.start()
    first.wait()
    wide = spread(m_ref[...], 0, cols, cols)
    for i, span in enumerate(spans):
        loads[i].wait()
        masked_ref[span, :] = w_ref[span, :] * wide[i : i + 1, :].astype(BF)


def masked_weight(mt, wt):
    hidden, cols = wt.shape
    return pl.pallas_call(
        mask_kernel,
        out_shape=shaped(hidden, cols),
        in_specs=[HBM, HBM],
        out_specs=VMEM,
        scratch_shapes=[
            pltpu.VMEM(mt.shape, jnp.int32),
            pltpu.VMEM((hidden, cols), BF),
            pltpu.SemaphoreType.DMA,
            pltpu.SemaphoreType.DMA((mt.shape[0],)),
        ],
        cost_estimate=cost(2 * hidden * cols, 4 << 20),
        compiler_params=grant(10),
        name="mask_weight",
    )(mt, wt)


def dgrad_kernel(at_ref, d0, d1, d2, d3, w_ref, keep_ref, send_ref, dy_ref):
    x, y, core, z = (at_ref[i] for i in range(4))
    tokens = d0.shape[1]
    cols = w_ref.shape[1]
    half = tokens // 2
    order = own_first(core, z, tokens)
    for k, d in enumerate((d0, d1, d2, d3)):
        rel = lax.rem(y + k - x + 4, 4)
        dy_ref[pl.ds(pl.multiple_of(rel * tokens, tokens), tokens), :] = lax.dot_general(
            order, d[...], (((1,), (1,)), ((), ())), preferred_element_type=F32
        ).astype(BF)
    steps = 4
    tile = cols // steps
    for j in range(steps):
        span = pl.ds(j * tile, tile)
        total = jnp.dot(dy_ref[...], w_ref[:, span], preferred_element_type=F32).astype(BF)
        for p in range(4):
            first = p * tokens
            keep_ref[p, :, span] = total[first : first + half]
            send_ref[p, :, span] = total[first + half : first + tokens]


def dgrad(at, blocks, masked):
    hidden, tokens = blocks[0].shape
    cols = masked.shape[1]
    half = shaped(4, tokens // 2, cols)
    return pl.pallas_call(
        dgrad_kernel,
        out_shape=(half, half, shaped(4 * tokens, hidden)),
        in_specs=[SMEM] + [VMEM] * 5,
        out_specs=(VMEM,) * 3,
        cost_estimate=cost(8 * tokens * hidden * cols, 4 << 20),
        compiler_params=grant(12),
        name="dgrad",
    )(at, *blocks, masked)


def fwd_kernel(at_ref, *refs):
    mine, other = refs[:4], refs[4:8]
    w_ref, o0, o1, o2, o3, full_ref, acc_ref = refs[8:]
    x, y = at_ref[0], at_ref[1]
    half = mine[0].shape[0]
    tokens = 2 * half
    for p in range(4):
        full_ref[p * tokens : p * tokens + half, :] = mine[p][...]
        full_ref[p * tokens + half : (p + 1) * tokens, :] = other[p][...]
    acc_ref[...] = lax.dot_general(
        w_ref[...], full_ref[...], (((1,), (1,)), ((), ())), preferred_element_type=F32
    ).astype(BF)
    for k, out in enumerate((o0, o1, o2, o3)):
        rel = lax.rem(y + k - x + 4, 4)
        out[...] = acc_ref[:, pl.ds(pl.multiple_of(rel * tokens, tokens), tokens)]


def forward(at, mine, other, masked):
    half, cols = mine[0].shape
    hidden = masked.shape[0]
    out = shaped(hidden, 2 * half)
    return pl.pallas_call(
        fwd_kernel,
        out_shape=(out,) * 4 + (shaped(8 * half, cols),),
        in_specs=[SMEM] + [VMEM] * 9,
        out_specs=(VMEM,) * 5,
        scratch_shapes=[pltpu.VMEM((hidden, 8 * half), BF)],
        cost_estimate=cost(16 * half * hidden * cols, 6 << 20),
        compiler_params=grant(14),
        name="forward",
    )(at, *mine, *other, masked)


def wgrad_kernel(cols, dy_ref, a_ref, m_ref, o_ref, dyt_ref):
    step = pl.program_id(0)

    @pl.when(step == 0)
    def _():
        dyt_ref[...] = dy_ref[...].T

    total = jnp.dot(dyt_ref[...], a_ref[...], preferred_element_type=F32)
    rows_b = m_ref.shape[0]
    tile = a_ref.shape[1]
    wide = spread(m_ref[...], step * tile, tile, cols)
    side = total.shape[0] // rows_b
    for i in range(rows_b):
        span = slice(i * side, (i + 1) * side)
        o_ref[span, :] = (total[span] * wide[i : i + 1, :]).astype(BF)


def wgrad(dy, full, mt):
    rows, hidden = dy.shape
    cols = full.shape[1]
    steps = 4
    tile = cols // steps
    return pl.pallas_call(
        functools.partial(wgrad_kernel, cols),
        out_shape=shaped(hidden, cols),
        grid=(steps,),
        in_specs=[
            pl.BlockSpec((rows, hidden), lambda i: (0, 0)),
            pl.BlockSpec((rows, tile), lambda i: (0, i)),
            pl.BlockSpec(mt.shape, lambda i: (0, 0)),
        ],
        out_specs=pl.BlockSpec((hidden, tile), lambda i: (0, i)),
        scratch_shapes=[pltpu.VMEM((hidden, rows), BF)],
        cost_estimate=cost(2 * rows * hidden * cols, 6 << 20),
        compiler_params=grant(14),
        name="wgrad",
    )(dy, full, mt)


def finish_kernel(at_ref, r0, r1, r2, r3, o_ref):
    total = (r0[...].astype(F32) + r1[...].astype(F32)) + (
        r2[...].astype(F32) + r3[...].astype(F32)
    )
    back = own_first(at_ref[2], at_ref[3], r0.shape[1])
    o_ref[...] = jnp.dot(total.astype(BF), back, preferred_element_type=F32).astype(BF)


def finish(at, parts):
    return pl.pallas_call(
        finish_kernel,
        out_shape=shaped(*parts[0].shape),
        in_specs=[SMEM] + [VMEM] * 4,
        out_specs=VMEM,
        cost_estimate=cost(parts[0].size * 256, 1 << 20),
        compiler_params=grant(6),
        name="finish",
    )(at, *parts)


def to(array, axis, step):
    n = lax.axis_size(axis)
    return lax.ppermute(array, axis, [(i, (i + step) % n) for i in range(n)])


def with_partner(array, bit):
    return jnp.concatenate([array, across(array, bit)])


def across(array, bit):
    return lax.ppermute(array, "z", [(i, i ^ bit) for i in range(lax.axis_size("z"))])


def halved(*terms):
    half = terms[0].shape[0] // 2
    return added(*(t[:half] for t in terms)), added(*(t[half:] for t in terms))


def added(*terms):
    return sum(t.astype(F32) for t in terms).astype(BF)


def on_device(activations, up_weight, block_mask, out_grad):
    at = jnp.stack([lax.axis_index(n).astype(jnp.int32) for n in ("x", "narrow", "core", "z")])
    wt, mt, dyt = up_weight.T, block_mask.T, out_grad.T

    blocks = (dyt, to(dyt, "narrow", -1), to(dyt, "narrow", 2), to(dyt, "narrow", 1))
    masked = masked_weight(in_hbm(mt), in_hbm(wt))
    near = with_partner(activations, 4)
    keep, send, dy = dgrad(at, blocks, masked)
    got = to(send, "core", 1)
    near = with_partner(near, 2)
    near = with_partner(near, 1)
    second, first = added(keep[2], got[2]), added(keep[1], got[1])
    behind = to(second, "x", -1)
    direct = to(first, "x", 1)
    third = added(keep[3], got[3], behind)
    relayed = to(third, "x", -1)
    own, away = halved(keep[0], got[0], direct, relayed)
    came = across(away, 1)
    own, away = halved(own, came)
    came = across(away, 2)
    own, away = halved(own, came)
    came = across(away, 4)
    input_grad = added(own, came)

    before = to(near, "x", 1)
    after = to(near, "x", -1)
    far = to(before, "x", 1)
    mine = (near, after, far, before)
    other = tuple(to(m, "core", 1) for m in mine)
    o0, o1, o2, o3, full = forward(at, mine, other, masked)
    parts = (o0, to(o1, "narrow", 1), to(o2, "narrow", 2), to(o3, "narrow", -1))
    output = finish(at, parts).T
    weight_grad = wgrad(dy, full, mt).T
    return (output, input_grad, weight_grad)


def solution(mesh):
    torus = Mesh(
        mesh.devices.reshape(4, 8, 2, mesh.shape["narrow"]),
        ("x", "z", "core", "narrow"),
    )
    return jax.shard_map(
        on_device,
        mesh=torus,
        in_specs=(P(WIDE, "narrow"), P("narrow", WIDE), P("narrow", WIDE), P("narrow", WIDE)),
        out_specs=(P("narrow", WIDE), P(WIDE, "narrow"), P("narrow", WIDE)),
        check_vma=False,
    )
```

time: 77.2 us -> 72.5 us (0.939)
  local copies, waits for them, and re-layouts: 6.6 us -> 0.04 us
  starting transfers between devices: 39.6 us -> 45.3 us
  other arithmetic: 6.51 us -> 1.13 us
  waiting for transfers between devices: 12.3 us -> 13.8 us
    ppermute x0 -> x6, starting transfers between devices: none -> 14.9 us  [across(): lax.ppermute(array, 'z', [(i, i ^ bit) for i in range(lax.axis_size('z'))])]
    all_to_all x2 -> x0, starting transfers between devices: 12 us -> none  [exchange(): return lax.all_to_all(blocks, axis, split_axis=0, concat_axis=0, tiled=True)]
    all_to_all x2 -> x0, waiting for transfers between devices: 7.95 us -> none  [exchange(): return lax.all_to_all(blocks, axis, split_axis=0, concat_axis=0, tiled=True)]
    ppermute x0 -> x6, waiting for transfers between devices: none -> 6.81 us  [across(): lax.ppermute(array, 'z', [(i, i ^ bit) for i in range(lax.axis_size('z'))])]
    unnamed x16 -> x9, local copies, waits for them, and re-layouts: 3.63 us -> 0.03 us
    ppermute x20 -> x17, starting transfers between devices: 27.6 us -> 30.4 us  [to(): return lax.ppermute(array, axis, [(i, (i + step) % n) for i in range(n)])]
    ppermute x20 -> x17, waiting for transfers between devices: 4.38 us -> 6.99 us  [to(): return lax.ppermute(array, axis, [(i, (i + step) % n) for i in range(n)])]
    slice x2 -> x0, local copies, waits for them, and re-layouts: 2.23 us -> none  [on_device(): far_low, far_high = (to(before[:half], 'x', 1), to(after[half:], 'x', -1))]
  transfers between devices with their start and end apart: 22 -> 23, of which waited for: 7 -> 7; matrix products, arithmetic and copies ran while one was open for 10% -> 1% of each run, Pallas kernels for 10% -> 12%
where the time goes in v4:
time: 72.5 us; the launch traced here: 71.3 us
  starting transfers between devices  45.3 us (62%)
  waiting for transfers between devices  13.8 us (19%)
  Pallas kernels  10.3 us (14%)
  other arithmetic  1.13 us (2%)
  between operations  0.75 us (1%)
    ppermute x17, starting transfers between devices, to(): return lax.ppermute(array, axis, [(i, (i + step) % n) for i in range(n)])  30.4 us
    ppermute x6, starting transfers between devices, across(): lax.ppermute(array, 'z', [(i, i ^ bit) for i in range(lax.axis_size('z'))])  14.9 us
    ppermute x17, waiting for transfers between devices, to(): return lax.ppermute(array, axis, [(i, (i + step) % n) for i in range(n)])  6.99 us
    ppermute x6, waiting for transfers between devices, across(): lax.ppermute(array, 'z', [(i, i ^ bit) for i in range(lax.axis_size('z'))])  6.81 us
    pallas_call x1, Pallas kernels, wgrad(): pl.pallas_call(functools.partial(wgrad_kernel, cols), out_shape=shaped(hi...  3.31 us
    pallas_call x1, Pallas kernels, dgrad(): pl.pallas_call(dgrad_kernel, out_shape=(half, half, shaped(4 * tokens, hi...  2.05 us
    pallas_call x1, Pallas kernels, forward(): pl.pallas_call(fwd_kernel, out_shape=(out,) * 4 + (shaped(8 * half, cols)...  1.87 us
    pallas_call x1, Pallas kernels, masked_weight(): pl.pallas_call(mask_kernel, out_shape=shaped(hidden, cols), in_specs=[HBM...  1.67 us
  transfers between devices with their start and end apart: 23, of which 7 were waited for; matrix products, arithmetic and copies ran while one was open for 1% of the time, Pallas kernels for 12%

profile of v4, /device:TPU:1, one launch (start us, length us, event | category | flops | bytes accessed | tf_op | source)
XLA Modules:
  0.0 71.3 jit_solution(17369837026756387040)
XLA Ops:
  0.6 2.2 %collective-permute-start.15 = (bf16[448,128]{1,0:T(8,128)(2,1)}, bf16[448,128]{1,0:T(8,128)(2,1)S(1)}, u32[]{:S(2)}, u32[]{:S(2)}) collective-permute-start(bf16[448,128]{1,0:T(8,128)(2,1)} %bitcast.31), channel_id=1, source_target_pairs={{0,1},{1,2},{2,3},{3,0},{4,5},{5,6},{6,7},{7,4},{8,9},{9,10},{10,1... | collective-permute-start | bytes 344072 | tf_op jit(solution)/shard_map/ppermute | solution.py:230
  2.8 2.6 %collective-permute-start.14 = (bf16[448,128]{1,0:T(8,128)(2,1)}, bf16[448,128]{1,0:T(8,128)(2,1)S(1)}, u32[]{:S(2)}, u32[]{:S(2)}) collective-permute-start(bf16[448,128]{1,0:T(8,128)(2,1)} %bitcast.32), channel_id=1, source_target_pairs={{0,2},{1,3},{2,0},{3,1},{4,6},{5,7},{6,4},{7,5},{8,10},{9,11},{10,... | collective-permute-start | bytes 344072 | tf_op jit(solution)/shard_map/ppermute | solution.py:230
  6.5 1.7 %mask_weight.1.refs_8_.w_ref = bf16[448,2048]{1,0:T(8,128)(2,1)S(1)} custom-call(s32[7,32]{1,0:T(8,128)} %bitcast.29, bf16[448,2048]{1,0:T(8,128)(2,1)} %bitcast.36), custom_call_target="tpu_custom_call" | custom-call | flops 1835008 | bytes 4194304 | tf_op jit(solution)/shard_map/mask_weight/pallas_call | solution.py:82
  8.3 2.4 %collective-permute-done.14.d2 = bf16[448,128]{1,0:T(8,128)(2,1)S(1)} collective-permute-done((bf16[448,128]{1,0:T(8,128)(2,1)}, bf16[448,128]{1,0:T(8,128)(2,1)S(1)}, u32[]{:S(2)}, u32[]{:S(2)}) %collective-permute-start.14) | collective-permute-done | bytes 114720 | tf_op jit(solution)/shard_map/ppermute | solution.py:230
  10.7 2.1 %dgrad.1 = (bf16[4,64,2048]{2,1,0:T(8,128)(2,1)S(1)}, bf16[4,64,2048]{2,1,0:T(8,128)(2,1)S(1)}, bf16[512,448]{1,0:T(8,128)(2,1)S(1)}) custom-call(s32[4]{0:T(128)S(1)} %pad_add_fusion.at_ref, bf16[448,128]{1,0:T(8,128)(2,1)S(1)} %bitcast.34, bf16[448,128]{1,0:T(8,128)(2,1)S(1)} %collective-permute-done.13.d1, ...), custom_call_target="tpu_custom_call" | custom-call | flops 939524096 | bytes 4194304 | tf_op jit(solution)/shard_map/dgrad/pallas_call | solution.py:125
  12.7 1.9 %collective-permute-start.16 = (bf16[4,64,2048]{2,1,0:T(8,128)(2,1)S(1)}, bf16[4,64,2048]{2,1,0:T(8,128)(2,1)S(1)}, u32[]{:S(2)}, u32[]{:S(2)}) collective-permute-start(bf16[4,64,2048]{2,1,0:T(8,128)(2,1)S(1)} %get-tuple-element.16), channel_id=1, source_target_pairs={{0,4},{4,0},{1,5},{5,1},{2,6},{6,2},{3,7},{7,3},{8,12},{12,8},{9,1... | collective-permute-start | bytes 3145736 | tf_op jit(solution)/shard_map/ppermute | solution.py:230
  14.6 6.7 %collective-permute-start = (bf16[8,2048]{1,0:T(8,128)(2,1)S(1)}, bf16[8,2048]{1,0:T(8,128)(2,1)S(1)}, u32[]{:S(2)}, u32[]{:S(2)}) collective-permute-start(bf16[8,2048]{1,0:T(8,128)(2,1)S(1)} %copy-done.2), channel_id=1, source_target_pairs={{0,32},{8,40},{16,48},{24,56},{32,0},{40,8},{48,16},{56,24},{1,33}... | collective-permute-start | bytes 98312 | tf_op jit(solution)/shard_map/ppermute | solution.py:238
  21.3 1.7 %collective-permute-done = bf16[8,2048]{1,0:T(8,128)(2,1)S(1)} collective-permute-done((bf16[8,2048]{1,0:T(8,128)(2,1)S(1)}, bf16[8,2048]{1,0:T(8,128)(2,1)S(1)}, u32[]{:S(2)}, u32[]{:S(2)}) %collective-permute-start) | collective-permute-done | bytes 32800 | tf_op jit(solution)/shard_map/ppermute | solution.py:238
  24.0 4.1 %collective-permute-done.1 = bf16[16,2048]{1,0:T(8,128)(2,1)S(1)} collective-permute-done((bf16[16,2048]{1,0:T(8,128)(2,1)S(1)}, bf16[16,2048]{1,0:T(8,128)(2,1)S(1)}, u32[]{:S(2)}, u32[]{:S(2)}) %collective-permute-start.1) | collective-permute-done | bytes 65568 | tf_op jit(solution)/shard_map/ppermute | solution.py:238
  28.3 2.6 %collective-permute-start.18 = (bf16[64,2048]{1,0:T(8,128)(2,1)S(1)}, bf16[64,2048]{1,0:T(8,128)(2,1)S(1)}, u32[]{:S(2)}, u32[]{:S(2)}) collective-permute-start(bf16[64,2048]{1,0:T(8,128)(2,1)S(1)} %get-tuple-element.22), channel_id=1, source_target_pairs={{0,192},{64,0},{128,64},{192,128},{1,193},{65,1},{129,65},{193,129... | collective-permute-start | bytes 786440 | tf_op jit(solution)/shard_map/ppermute | solution.py:230
  32.0 1.3 %collective-permute-start.4 = (bf16[64,2048]{1,0:T(8,128)(2,1)S(1)}, bf16[64,2048]{1,0:T(8,128)(2,1)S(1)}, u32[]{:S(2)}, u32[]{:S(2)}) collective-permute-start(bf16[64,2048]{1,0:T(8,128)(2,1)S(1)} %constant_dynamic-update-slice_fusion.refs_0_), channel_id=1, source_target_pairs={{0,64},{64,128},{128,192},{192,0},{1,65},{65,129},{129,193},{193,1... | collective-permute-start | bytes 786440 | tf_op jit(solution)/shard_map/ppermute | solution.py:230
  33.3 1.2 %collective-permute-start.17 = (bf16[64,2048]{1,0:T(8,128)(2,1)S(1)}, bf16[64,2048]{1,0:T(8,128)(2,1)S(1)}, u32[]{:S(2)}, u32[]{:S(2)}) collective-permute-start(bf16[64,2048]{1,0:T(8,128)(2,1)S(1)} %get-tuple-element.21), channel_id=1, source_target_pairs={{0,64},{64,128},{128,192},{192,0},{1,65},{65,129},{129,193},{193,1... | collective-permute-start | bytes 786440 | tf_op jit(solution)/shard_map/ppermute | solution.py:230
  34.8 3.5 %collective-permute-start.19 = (bf16[64,2048]{1,0:T(8,128)(2,1)S(1)}, bf16[64,2048]{1,0:T(8,128)(2,1)S(1)}, u32[]{:S(2)}, u32[]{:S(2)}) collective-permute-start(bf16[64,2048]{1,0:T(8,128)(2,1)S(1)} %fusion), channel_id=1, source_target_pairs={{0,192},{64,0},{128,64},{192,128},{1,193},{65,1},{129,65},{193,129... | collective-permute-start | bytes 786440 | tf_op jit(solution)/shard_map/ppermute | solution.py:230
  38.5 1.2 %collective-permute-start.5 = (bf16[64,2048]{1,0:T(8,128)(2,1)S(1)}, bf16[64,2048]{1,0:T(8,128)(2,1)S(1)}, u32[]{:S(2)}, u32[]{:S(2)}) collective-permute-start(bf16[64,2048]{1,0:T(8,128)(2,1)S(1)} %collective-permute-done.4.refs_3_), channel_id=1, source_target_pairs={{0,64},{64,128},{128,192},{192,0},{1,65},{65,129},{129,193},{193,1... | collective-permute-start | bytes 786440 | tf_op jit(solution)/shard_map/ppermute | solution.py:230
  39.7 4.2 %collective-permute-done.17 = bf16[64,2048]{1,0:T(8,128)(2,1)S(1)} collective-permute-done((bf16[64,2048]{1,0:T(8,128)(2,1)S(1)}, bf16[64,2048]{1,0:T(8,128)(2,1)S(1)}, u32[]{:S(2)}, u32[]{:S(2)}) %collective-permute-start.17) | collective-permute-done | bytes 262176 | tf_op jit(solution)/shard_map/ppermute | solution.py:230
  45.0 6.4 %collective-permute-start.6 = (bf16[64,2048]{1,0:T(8,128)(2,1)S(1)}, bf16[64,2048]{1,0:T(8,128)(2,1)S(1)}, u32[]{:S(2)}, u32[]{:S(2)}) collective-permute-start(bf16[64,2048]{1,0:T(8,128)(2,1)S(1)} %constant_dynamic-update-slice_fusion.refs_0_), channel_id=1, source_target_pairs={{0,4},{4,0},{1,5},{5,1},{2,6},{6,2},{3,7},{7,3},{8,12},{12,8},{9,1... | collective-permute-start | bytes 786440 | tf_op jit(solution)/shard_map/ppermute | solution.py:230
  51.8 1.4 %collective-permute-start.8 = (bf16[64,2048]{1,0:T(8,128)(2,1)S(1)}, bf16[64,2048]{1,0:T(8,128)(2,1)S(1)}, u32[]{:S(2)}, u32[]{:S(2)}) collective-permute-start(bf16[64,2048]{1,0:T(8,128)(2,1)S(1)} %collective-permute-done.5.refs_2_), channel_id=1, source_target_pairs={{0,4},{4,0},{1,5},{5,1},{2,6},{6,2},{3,7},{7,3},{8,12},{12,8},{9,1... | collective-permute-start | bytes 786440 | tf_op jit(solution)/shard_map/ppermute | solution.py:230
  53.3 1.2 %collective-permute-start.21 = (bf16[16,2048]{1,0:T(8,128)(2,1)S(1)}, bf16[16,2048]{1,0:T(8,128)(2,1)S(1)}, u32[]{:S(2)}, u32[]{:S(2)}) collective-permute-start(bf16[16,2048]{1,0:T(8,128)(2,1)S(1)} %get-tuple-element.24), channel_id=1, source_target_pairs={{0,16},{8,24},{16,0},{24,8},{32,48},{40,56},{48,32},{56,40},{1,17}... | collective-permute-start | bytes 196616 | tf_op jit(solution)/shard_map/ppermute | solution.py:238
  54.6 1.9 %forward.1 = (bf16[448,128]{1,0:T(8,128)(2,1)S(1)}, bf16[448,128]{1,0:T(8,128)(2,1)S(1)}, bf16[448,128]{1,0:T(8,128)(2,1)S(1)}, bf16[448,128]{1,0:T(8,128)(2,1)S(1)}, bf16[512,2048]{1,0:T(8,128)(2,1)S(1)}) custom-call(s32[4]{0:T(128)S(1)} %pad_add_fusion.at_ref, bf16[64,2048]{1,0:T(8,128)(2,1)S(1)} %constant_dynamic-update-slice_fusion.refs_0_, ...), custom_call_target="tpu_custom_call" | custom-call | flops 939524096 | bytes 6291456 | tf_op jit(solution)/shard_map/forward/pallas_call | solution.py:157
  57.5 2.1 %collective-permute-start.11 = (bf16[448,128]{1,0:T(8,128)(2,1)S(1)}, bf16[448,128]{1,0:T(8,128)(2,1)S(1)}, u32[]{:S(2)}, u32[]{:S(2)}) collective-permute-start(bf16[448,128]{1,0:T(8,128)(2,1)S(1)} %get-tuple-element.13), channel_id=1, source_target_pairs={{0,2},{1,3},{2,0},{3,1},{4,6},{5,7},{6,4},{7,5},{8,10},{9,11},{10,... | collective-permute-start | bytes 344072 | tf_op jit(solution)/shard_map/ppermute | solution.py:230
  59.6 1.3 %collective-permute-start.12 = (bf16[448,128]{1,0:T(8,128)(2,1)S(1)}, bf16[448,128]{1,0:T(8,128)(2,1)S(1)}, u32[]{:S(2)}, u32[]{:S(2)}) collective-permute-start(bf16[448,128]{1,0:T(8,128)(2,1)S(1)} %get-tuple-element.14), channel_id=1, source_target_pairs={{0,3},{1,0},{2,1},{3,2},{4,7},{5,4},{6,5},{7,6},{8,11},{9,8},{10,9... | collective-permute-start | bytes 344072 | tf_op jit(solution)/shard_map/ppermute | solution.py:230
  60.9 5.0 %collective-permute-start.22 = (bf16[8,2048]{1,0:T(8,128)(2,1)S(1)}, bf16[8,2048]{1,0:T(8,128)(2,1)S(1)}, u32[]{:S(2)}, u32[]{:S(2)}) collective-permute-start(bf16[8,2048]{1,0:T(8,128)(2,1)S(1)} %add_convert_fusion.5), channel_id=1, source_target_pairs={{0,32},{8,40},{16,48},{24,56},{32,0},{40,8},{48,16},{56,24},{1,33}... | collective-permute-start | bytes 98312 | tf_op jit(solution)/shard_map/ppermute | solution.py:238
  65.9 3.3 %wgrad.1 = bf16[448,2048]{1,0:T(8,128)(2,1)} custom-call(bf16[512,448]{1,0:T(8,128)(2,1)S(1)} %get-tuple-element.17.dy_ref, bf16[512,2048]{1,0:T(8,128)(2,1)S(1)} %get-tuple-element.18.a_ref, s32[7,32]{1,0:T(8,128)S(1)} %bitcast.30), custom_call_target="tpu_custom_call" | custom-call | flops 939524096 | bytes 6291456 | tf_op jit(solution)/shard_map/wgrad/pallas_call | solution.py:191
  69.3 1.4 %finish.1 = bf16[448,128]{1,0:T(8,128)(2,1)} custom-call(s32[4]{0:T(128)S(1)} %pad_add_fusion.at_ref, bf16[448,128]{1,0:T(8,128)(2,1)S(1)} %get-tuple-element.11.r0, bf16[448,128]{1,0:T(8,128)(2,1)S(1)} %collective-permute-done.10.r1, bf16[448,128]{1,0:T(8,128)(2,1)S(1)} %collective-permute-done.11.r2, bf16[448,128]{1,0:T(8,128)(2,1)S(1)} %collective-permute-done.12.r3), custom_call_target="tpu_custom_call" | custom-call | flops 14680064 | bytes 1048576 | tf_op jit(solution)/shard_map/finish/pallas_call | solution.py:217
  (46 shorter events, 7.4 us)
Async XLA Ops:
  0.6 7.7 %collective-permute-start.15 = (bf16[448,128]{1,0:T(8,128)(2,1)}, bf16[448,128]{1,0:T(8,128)(2,1)S(1)}, u32[]{:S(2)}, u32[]{:S(2)}) collective-permute-start(bf16[448,128]{1,0:T(8,128)(2,1)} %bitcast.31), channel_id=1, source_target_pairs={{0,1},{1,2},{2,3},{3,0},{4,5},{5,6},{6,7},{7,4},{8,9},{9,10},{10,1... | collective-permute-start | bytes 344072 | tf_op jit(solution)/shard_map/ppermute | solution.py:230
  2.8 7.9 %collective-permute-start.14 = (bf16[448,128]{1,0:T(8,128)(2,1)}, bf16[448,128]{1,0:T(8,128)(2,1)S(1)}, u32[]{:S(2)}, u32[]{:S(2)}) collective-permute-start(bf16[448,128]{1,0:T(8,128)(2,1)} %bitcast.32), channel_id=1, source_target_pairs={{0,2},{1,3},{2,0},{3,1},{4,6},{5,7},{6,4},{7,5},{8,10},{9,11},{10,... | collective-permute-start | bytes 344072 | tf_op jit(solution)/shard_map/ppermute | solution.py:230
  5.4 5.2 %collective-permute-start.13 = (bf16[448,128]{1,0:T(8,128)(2,1)}, bf16[448,128]{1,0:T(8,128)(2,1)S(1)}, u32[]{:S(2)}, u32[]{:S(2)}) collective-permute-start(bf16[448,128]{1,0:T(8,128)(2,1)} %bitcast.33), channel_id=1, source_target_pairs={{0,3},{1,0},{2,1},{3,2},{4,7},{5,4},{6,5},{7,6},{8,11},{9,8},{10,9... | collective-permute-start | bytes 344072 | tf_op jit(solution)/shard_map/ppermute | solution.py:230
  12.7 15.5 %collective-permute-start.16 = (bf16[4,64,2048]{2,1,0:T(8,128)(2,1)S(1)}, bf16[4,64,2048]{2,1,0:T(8,128)(2,1)S(1)}, u32[]{:S(2)}, u32[]{:S(2)}) collective-permute-start(bf16[4,64,2048]{2,1,0:T(8,128)(2,1)S(1)} %get-tuple-element.16), channel_id=1, source_target_pairs={{0,4},{4,0},{1,5},{5,1},{2,6},{6,2},{3,7},{7,3},{8,12},{12,8},{9,1... | collective-permute-start | bytes 3145736 | tf_op jit(solution)/shard_map/ppermute | solution.py:230
  14.6 8.3 %collective-permute-start = (bf16[8,2048]{1,0:T(8,128)(2,1)S(1)}, bf16[8,2048]{1,0:T(8,128)(2,1)S(1)}, u32[]{:S(2)}, u32[]{:S(2)}) collective-permute-start(bf16[8,2048]{1,0:T(8,128)(2,1)S(1)} %copy-done.2), channel_id=1, source_target_pairs={{0,32},{8,40},{16,48},{24,56},{32,0},{40,8},{48,16},{56,24},{1,33}... | collective-permute-start | bytes 98312 | tf_op jit(solution)/shard_map/ppermute | solution.py:238
  22.9 5.2 %collective-permute-start.1 = (bf16[16,2048]{1,0:T(8,128)(2,1)S(1)}, bf16[16,2048]{1,0:T(8,128)(2,1)S(1)}, u32[]{:S(2)}, u32[]{:S(2)}) collective-permute-start(bf16[16,2048]{1,0:T(8,128)(2,1)S(1)} %pad_maximum_fusion.1), channel_id=1, source_target_pairs={{0,16},{8,24},{16,0},{24,8},{32,48},{40,56},{48,32},{56,40},{1,17}... | collective-permute-start | bytes 196616 | tf_op jit(solution)/shard_map/ppermute | solution.py:238
  28.1 3.9 %collective-permute-start.2 = (bf16[32,2048]{1,0:T(8,128)(2,1)S(1)}, bf16[32,2048]{1,0:T(8,128)(2,1)S(1)}, u32[]{:S(2)}, u32[]{:S(2)}) collective-permute-start(bf16[32,2048]{1,0:T(8,128)(2,1)S(1)} %pad_maximum_fusion), channel_id=1, source_target_pairs={{0,8},{8,0},{16,24},{24,16},{32,40},{40,32},{48,56},{56,48},{1,9},... | collective-permute-start | bytes 393224 | tf_op jit(solution)/shard_map/ppermute | solution.py:238
  28.3 6.3 %collective-permute-start.18 = (bf16[64,2048]{1,0:T(8,128)(2,1)S(1)}, bf16[64,2048]{1,0:T(8,128)(2,1)S(1)}, u32[]{:S(2)}, u32[]{:S(2)}) collective-permute-start(bf16[64,2048]{1,0:T(8,128)(2,1)S(1)} %get-tuple-element.22), channel_id=1, source_target_pairs={{0,192},{64,0},{128,64},{192,128},{1,193},{65,1},{129,65},{193,129... | collective-permute-start | bytes 786440 | tf_op jit(solution)/shard_map/ppermute | solution.py:230
  32.0 6.5 %collective-permute-start.4 = (bf16[64,2048]{1,0:T(8,128)(2,1)S(1)}, bf16[64,2048]{1,0:T(8,128)(2,1)S(1)}, u32[]{:S(2)}, u32[]{:S(2)}) collective-permute-start(bf16[64,2048]{1,0:T(8,128)(2,1)S(1)} %constant_dynamic-update-slice_fusion.refs_0_), channel_id=1, source_target_pairs={{0,64},{64,128},{128,192},{192,0},{1,65},{65,129},{129,193},{193,1... | collective-permute-start | bytes 786440 | tf_op jit(solution)/shard_map/ppermute | solution.py:230
  33.3 10.7 %collective-permute-start.17 = (bf16[64,2048]{1,0:T(8,128)(2,1)S(1)}, bf16[64,2048]{1,0:T(8,128)(2,1)S(1)}, u32[]{:S(2)}, u32[]{:S(2)}) collective-permute-start(bf16[64,2048]{1,0:T(8,128)(2,1)S(1)} %get-tuple-element.21), channel_id=1, source_target_pairs={{0,64},{64,128},{128,192},{192,0},{1,65},{65,129},{129,193},{193,1... | collective-permute-start | bytes 786440 | tf_op jit(solution)/shard_map/ppermute | solution.py:230
  34.8 9.2 %collective-permute-start.19 = (bf16[64,2048]{1,0:T(8,128)(2,1)S(1)}, bf16[64,2048]{1,0:T(8,128)(2,1)S(1)}, u32[]{:S(2)}, u32[]{:S(2)}) collective-permute-start(bf16[64,2048]{1,0:T(8,128)(2,1)S(1)} %fusion), channel_id=1, source_target_pairs={{0,192},{64,0},{128,64},{192,128},{1,193},{65,1},{129,65},{193,129... | collective-permute-start | bytes 786440 | tf_op jit(solution)/shard_map/ppermute | solution.py:230
  38.3 13.1 %collective-permute-start.3 = (bf16[64,2048]{1,0:T(8,128)(2,1)S(1)}, bf16[64,2048]{1,0:T(8,128)(2,1)S(1)}, u32[]{:S(2)}, u32[]{:S(2)}) collective-permute-start(bf16[64,2048]{1,0:T(8,128)(2,1)S(1)} %constant_dynamic-update-slice_fusion.refs_0_), channel_id=1, source_target_pairs={{0,192},{64,0},{128,64},{192,128},{1,193},{65,1},{129,65},{193,129... | collective-permute-start | bytes 786440 | tf_op jit(solution)/shard_map/ppermute | solution.py:230
  38.5 13.3 %collective-permute-start.5 = (bf16[64,2048]{1,0:T(8,128)(2,1)S(1)}, bf16[64,2048]{1,0:T(8,128)(2,1)S(1)}, u32[]{:S(2)}, u32[]{:S(2)}) collective-permute-start(bf16[64,2048]{1,0:T(8,128)(2,1)S(1)} %collective-permute-done.4.refs_3_), channel_id=1, source_target_pairs={{0,64},{64,128},{128,192},{192,0},{1,65},{65,129},{129,193},{193,1... | collective-permute-start | bytes 786440 | tf_op jit(solution)/shard_map/ppermute | solution.py:230
  44.1 9.1 %collective-permute-start.20 = (bf16[32,2048]{1,0:T(8,128)(2,1)S(1)}, bf16[32,2048]{1,0:T(8,128)(2,1)S(1)}, u32[]{:S(2)}, u32[]{:S(2)}) collective-permute-start(bf16[32,2048]{1,0:T(8,128)(2,1)S(1)} %get-tuple-element.20), channel_id=1, source_target_pairs={{0,8},{8,0},{16,24},{24,16},{32,40},{40,32},{48,56},{56,48},{1,9},... | collective-permute-start | bytes 393224 | tf_op jit(solution)/shard_map/ppermute | solution.py:238
  45.0 9.6 %collective-permute-start.6 = (bf16[64,2048]{1,0:T(8,128)(2,1)S(1)}, bf16[64,2048]{1,0:T(8,128)(2,1)S(1)}, u32[]{:S(2)}, u32[]{:S(2)}) collective-permute-start(bf16[64,2048]{1,0:T(8,128)(2,1)S(1)} %constant_dynamic-update-slice_fusion.refs_0_), channel_id=1, source_target_pairs={{0,4},{4,0},{1,5},{5,1},{2,6},{6,2},{3,7},{7,3},{8,12},{12,8},{9,1... | collective-permute-start | bytes 786440 | tf_op jit(solution)/shard_map/ppermute | solution.py:230
  51.3 3.2 %collective-permute-start.9 = (bf16[64,2048]{1,0:T(8,128)(2,1)S(1)}, bf16[64,2048]{1,0:T(8,128)(2,1)S(1)}, u32[]{:S(2)}, u32[]{:S(2)}) collective-permute-start(bf16[64,2048]{1,0:T(8,128)(2,1)S(1)} %collective-permute-done.4.refs_3_), channel_id=1, source_target_pairs={{0,4},{4,0},{1,5},{5,1},{2,6},{6,2},{3,7},{7,3},{8,12},{12,8},{9,1... | collective-permute-start | bytes 786440 | tf_op jit(solution)/shard_map/ppermute | solution.py:230
  51.3 3.2 %collective-permute-start.7 = (bf16[64,2048]{1,0:T(8,128)(2,1)S(1)}, bf16[64,2048]{1,0:T(8,128)(2,1)S(1)}, u32[]{:S(2)}, u32[]{:S(2)}) collective-permute-start(bf16[64,2048]{1,0:T(8,128)(2,1)S(1)} %collective-permute-done.3.refs_1_), channel_id=1, source_target_pairs={{0,4},{4,0},{1,5},{5,1},{2,6},{6,2},{3,7},{7,3},{8,12},{12,8},{9,1... | collective-permute-start | bytes 786440 | tf_op jit(solution)/shard_map/ppermute | solution.py:230
  51.8 2.7 %collective-permute-start.8 = (bf16[64,2048]{1,0:T(8,128)(2,1)S(1)}, bf16[64,2048]{1,0:T(8,128)(2,1)S(1)}, u32[]{:S(2)}, u32[]{:S(2)}) collective-permute-start(bf16[64,2048]{1,0:T(8,128)(2,1)S(1)} %collective-permute-done.5.refs_2_), channel_id=1, source_target_pairs={{0,4},{4,0},{1,5},{5,1},{2,6},{6,2},{3,7},{7,3},{8,12},{12,8},{9,1... | collective-permute-start | bytes 786440 | tf_op jit(solution)/shard_map/ppermute | solution.py:230
  53.3 12.6 %copy-start = (s32[32,7]{0,1:T(8,128)S(1)}, s32[32,7]{0,1:T(8,128)}, u32[]{:S(2)}) copy-start(s32[32,7]{0,1:T(8,128)} %param.6) | copy-start | bytes 2692
  53.3 7.6 %collective-permute-start.21 = (bf16[16,2048]{1,0:T(8,128)(2,1)S(1)}, bf16[16,2048]{1,0:T(8,128)(2,1)S(1)}, u32[]{:S(2)}, u32[]{:S(2)}) collective-permute-start(bf16[16,2048]{1,0:T(8,128)(2,1)S(1)} %get-tuple-element.24), channel_id=1, source_target_pairs={{0,16},{8,24},{16,0},{24,8},{32,48},{40,56},{48,32},{56,40},{1,17}... | collective-permute-start | bytes 196616 | tf_op jit(solution)/shard_map/ppermute | solution.py:238
  56.4 12.8 %collective-permute-start.10 = (bf16[448,128]{1,0:T(8,128)(2,1)S(1)}, bf16[448,128]{1,0:T(8,128)(2,1)S(1)}, u32[]{:S(2)}, u32[]{:S(2)}) collective-permute-start(bf16[448,128]{1,0:T(8,128)(2,1)S(1)} %get-tuple-element.12), channel_id=1, source_target_pairs={{0,1},{1,2},{2,3},{3,0},{4,5},{5,6},{6,7},{7,4},{8,9},{9,10},{10,1... | collective-permute-start | bytes 344072 | tf_op jit(solution)/shard_map/ppermute | solution.py:230
  57.5 11.8 %collective-permute-start.11 = (bf16[448,128]{1,0:T(8,128)(2,1)S(1)}, bf16[448,128]{1,0:T(8,128)(2,1)S(1)}, u32[]{:S(2)}, u32[]{:S(2)}) collective-permute-start(bf16[448,128]{1,0:T(8,128)(2,1)S(1)} %get-tuple-element.13), channel_id=1, source_target_pairs={{0,2},{1,3},{2,0},{3,1},{4,6},{5,7},{6,4},{7,5},{8,10},{9,11},{10,... | collective-permute-start | bytes 344072 | tf_op jit(solution)/shard_map/ppermute | solution.py:230
  59.6 9.6 %collective-permute-start.12 = (bf16[448,128]{1,0:T(8,128)(2,1)S(1)}, bf16[448,128]{1,0:T(8,128)(2,1)S(1)}, u32[]{:S(2)}, u32[]{:S(2)}) collective-permute-start(bf16[448,128]{1,0:T(8,128)(2,1)S(1)} %get-tuple-element.14), channel_id=1, source_target_pairs={{0,3},{1,0},{2,1},{3,2},{4,7},{5,4},{6,5},{7,6},{8,11},{9,8},{10,9... | collective-permute-start | bytes 344072 | tf_op jit(solution)/shard_map/ppermute | solution.py:230
  60.9 9.8 %collective-permute-start.22 = (bf16[8,2048]{1,0:T(8,128)(2,1)S(1)}, bf16[8,2048]{1,0:T(8,128)(2,1)S(1)}, u32[]{:S(2)}, u32[]{:S(2)}) collective-permute-start(bf16[8,2048]{1,0:T(8,128)(2,1)S(1)} %add_convert_fusion.5), channel_id=1, source_target_pairs={{0,32},{8,40},{16,48},{24,56},{32,0},{40,8},{48,16},{56,24},{1,33}... | collective-permute-start | bytes 98312 | tf_op jit(solution)/shard_map/ppermute | solution.py:238
  (2 other events, 10.6 us)

commit v5 on v4

--- a/solution.py
+++ b/solution.py
@@ -1,5 +1,3 @@
-import functools
-
 import jax
 import jax.numpy as jnp
 from jax import lax
@@ -9,6 +7,7 @@
 from jax.sharding import PartitionSpec as P
 
 WIDE = ("x", "z", "core")
+STEPS = (3, -1, 1)
 BF = jnp.bfloat16
 F32 = jnp.float32
 VMEM = pl.BlockSpec(memory_space=pltpu.VMEM)
@@ -32,11 +31,11 @@
     return jax.ShapeDtypeStruct(dims, kind)
 
 
-def spread(mask, start, tile, cols):
+def spread(mask, cols):
     cols_b = mask.shape[1]
     side = cols // cols_b
-    block = lax.broadcasted_iota(jnp.int32, (cols_b, tile), 0)
-    at = lax.broadcasted_iota(jnp.int32, (cols_b, tile), 1) + start
+    block = lax.broadcasted_iota(jnp.int32, (cols_b, cols), 0)
+    at = lax.broadcasted_iota(jnp.int32, (cols_b, cols), 1)
     first = block * side
     pick = jnp.logical_and(at >= first, at < first + side).astype(F32)
     return jnp.dot(mask.astype(F32), pick, preferred_element_type=F32)
@@ -50,10 +49,11 @@
     within = new - other * half
     group = jnp.right_shift(within, 3)
     row = within - group * 8
-    low = jnp.right_shift(group, 2)
-    mid = jnp.bitwise_and(group, 2)
-    high = jnp.bitwise_and(group, 1) * 4
-    src = jnp.bitwise_xor(low + mid + high, z) * 16 + jnp.bitwise_xor(other, core) * 8 + row
+    at = jnp.zeros_like(group) + z
+    for bit, step in zip((2, 1, 0), reversed(STEPS)):
+        moved = jnp.bitwise_and(jnp.right_shift(group, bit), 1) * step
+        at = at + moved * (1 - 2 * jnp.bitwise_and(at, 1))
+    src = jnp.bitwise_and(at, 7) * 16 + jnp.bitwise_xor(other, core) * 8 + row
     return (src == old).astype(BF)
 
 
@@ -71,7 +71,7 @@
     for load in loads:
         load.start()
     first.wait()
-    wide = spread(m_ref[...], 0, cols, cols)
+    wide = spread(m_ref[...], cols)
     for i, span in enumerate(spans):
         loads[i].wait()
         masked_ref[span, :] = w_ref[span, :] * wide[i : i + 1, :].astype(BF)
@@ -134,14 +134,15 @@
 
 
 def fwd_kernel(at_ref, *refs):
-    mine, other = refs[:4], refs[4:8]
-    w_ref, o0, o1, o2, o3, full_ref, acc_ref = refs[8:]
+    mine, other = refs[:5], refs[5:10]
+    w_ref, o0, o1, o2, o3, full_ref, acc_ref = refs[10:]
     x, y = at_ref[0], at_ref[1]
     half = mine[0].shape[0]
     tokens = 2 * half
-    for p in range(4):
-        full_ref[p * tokens : p * tokens + half, :] = mine[p][...]
-        full_ref[p * tokens + half : (p + 1) * tokens, :] = other[p][...]
+    for h, group in enumerate((mine, other)):
+        for piece, first in zip(group, (0, 2 * half, 4 * half, 4 * half + half // 2, 6 * half)):
+            start = first + h * half
+            full_ref[start : start + piece.shape[0], :] = piece[...]
     acc_ref[...] = lax.dot_general(
         w_ref[...], full_ref[...], (((1,), (1,)), ((), ())), preferred_element_type=F32
     ).astype(BF)
@@ -157,7 +158,7 @@
     return pl.pallas_call(
         fwd_kernel,
         out_shape=(out,) * 4 + (shaped(8 * half, cols),),
-        in_specs=[SMEM] + [VMEM] * 9,
+        in_specs=[SMEM] + [VMEM] * 11,
         out_specs=(VMEM,) * 5,
         scratch_shapes=[pltpu.VMEM((hidden, 8 * half), BF)],
         cost_estimate=cost(16 * half * hidden * cols, 6 << 20),
@@ -166,39 +167,37 @@
     )(at, *mine, *other, masked)
 
 
-def wgrad_kernel(cols, dy_ref, a_ref, m_ref, o_ref, dyt_ref):
-    step = pl.program_id(0)
-
-    @pl.when(step == 0)
-    def _():
-        dyt_ref[...] = dy_ref[...].T
-
-    total = jnp.dot(dyt_ref[...], a_ref[...], preferred_element_type=F32)
+def wgrad_kernel(dy_ref, a_ref, m_ref, o_hbm, o_ref, sems):
+    chunks = sems.shape[0]
+    cols = o_ref.shape[1]
+    tile = cols // chunks
     rows_b = m_ref.shape[0]
-    tile = a_ref.shape[1]
-    wide = spread(m_ref[...], step * tile, tile, cols)
-    side = total.shape[0] // rows_b
-    for i in range(rows_b):
-        span = slice(i * side, (i + 1) * side)
-        o_ref[span, :] = (total[span] * wide[i : i + 1, :]).astype(BF)
+    side = o_ref.shape[0] // rows_b
+    left = dy_ref[...].T
+    wide = spread(m_ref[...], cols)
+    out = []
+    for j in range(chunks):
+        here = slice(j * tile, (j + 1) * tile)
+        total = jnp.dot(left, a_ref[:, here], preferred_element_type=F32)
+        for i in range(rows_b):
+            span = slice(i * side, (i + 1) * side)
+            o_ref[span, here] = (total[span] * wide[i : i + 1, here]).astype(BF)
+        part = pl.ds(j * tile, tile)
+        out.append(pltpu.make_async_copy(o_ref.at[:, part], o_hbm.at[:, part], sems.at[j]))
+        out[-1].start()
+    for copy in out:
+        copy.wait()
 
 
 def wgrad(dy, full, mt):
     rows, hidden = dy.shape
     cols = full.shape[1]
-    steps = 4
-    tile = cols // steps
-    return pl.pallas_call(
-        functools.partial(wgrad_kernel, cols),
+    return pl.pallas_call(
+        wgrad_kernel,
         out_shape=shaped(hidden, cols),
-        grid=(steps,),
-        in_specs=[
-            pl.BlockSpec((rows, hidden), lambda i: (0, 0)),
-            pl.BlockSpec((rows, tile), lambda i: (0, i)),
-            pl.BlockSpec(mt.shape, lambda i: (0, 0)),
-        ],
-        out_specs=pl.BlockSpec((hidden, tile), lambda i: (0, i)),
-        scratch_shapes=[pltpu.VMEM((hidden, rows), BF)],
+        in_specs=[VMEM] * 3,
+        out_specs=HBM,
+        scratch_shapes=[pltpu.VMEM((hidden, cols), BF), pltpu.SemaphoreType.DMA((4,))],
         cost_estimate=cost(2 * rows * hidden * cols, 6 << 20),
         compiler_params=grant(14),
         name="wgrad",
@@ -230,12 +229,13 @@
     return lax.ppermute(array, axis, [(i, (i + step) % n) for i in range(n)])
 
 
-def with_partner(array, bit):
-    return jnp.concatenate([array, across(array, bit)])
-
-
-def across(array, bit):
-    return lax.ppermute(array, "z", [(i, i ^ bit) for i in range(lax.axis_size("z"))])
+def across(array, step):
+    n = lax.axis_size("z")
+    return lax.ppermute(array, "z", [(i, (i - step if i % 2 else i + step) % n) for i in range(n)])
+
+
+def with_partner(array, step):
+    return jnp.concatenate([array, across(array, step)])
 
 
 def halved(*terms):
@@ -253,29 +253,36 @@
 
     blocks = (dyt, to(dyt, "narrow", -1), to(dyt, "narrow", 2), to(dyt, "narrow", 1))
     masked = masked_weight(in_hbm(mt), in_hbm(wt))
-    near = with_partner(activations, 4)
+    near = with_partner(activations, STEPS[0])
     keep, send, dy = dgrad(at, blocks, masked)
     got = to(send, "core", 1)
-    near = with_partner(near, 2)
-    near = with_partner(near, 1)
-    second, first = added(keep[2], got[2]), added(keep[1], got[1])
-    behind = to(second, "x", -1)
-    direct = to(first, "x", 1)
-    third = added(keep[3], got[3], behind)
-    relayed = to(third, "x", -1)
-    own, away = halved(keep[0], got[0], direct, relayed)
-    came = across(away, 1)
+    near = with_partner(near, STEPS[1])
+    near = with_partner(near, STEPS[2])
+    half = keep.shape[1] // 2
+    low, high = halved(keep[2], got[2])
+    ahead = to(low, "x", 1)
+    behind = to(high, "x", -1)
+    none = jnp.zeros_like(ahead)
+    right = added(keep[1], got[1], jnp.concatenate([ahead, none]))
+    left = added(keep[3], got[3], jnp.concatenate([none, behind]))
+    right = to(right, "x", 1)
+    left = to(left, "x", -1)
+    own, away = halved(keep[0], got[0], right, left)
+    came = across(away, STEPS[2])
     own, away = halved(own, came)
-    came = across(away, 2)
+    came = across(away, STEPS[1])
     own, away = halved(own, came)
-    came = across(away, 4)
+    came = across(away, STEPS[0])
     input_grad = added(own, came)
 
     before = to(near, "x", 1)
     after = to(near, "x", -1)
-    far = to(before, "x", 1)
-    mine = (near, after, far, before)
-    other = tuple(to(m, "core", 1) for m in mine)
+    far_low = to(before[:half], "x", 1)
+    far_high = to(after[half:], "x", -1)
+    mine = (near, after, far_low, far_high, before)
+    near, after, before = (to(m, "core", 1) for m in (near, after, before))
+    far_low, far_high = to(far_low, "core", 1), to(far_high, "core", 1)
+    other = (near, after, far_low, far_high, before)
     o0, o1, o2, o3, full = forward(at, mine, other, masked)
     parts = (o0, to(o1, "narrow", 1), to(o2, "narrow", 2), to(o3, "narrow", -1))
     output = finish(at, parts).T

time: 72.5 us -> 64.4 us (0.89); the launches traced: 71.3 us -> 64.1 us
  waiting for transfers between devices: 13.8 us -> 8.39 us
  Pallas kernels: 10.3 us -> 9.01 us
    ppermute x6, waiting for transfers between devices: 6.81 us -> 3.35 us  [across(): lax.ppermute(array, 'z', [(i, (i - step if i % 2 else i + step) % n) for...]
    ppermute x6, starting transfers between devices: 14.9 us -> 12.7 us  [across(): lax.ppermute(array, 'z', [(i, (i - step if i % 2 else i + step) % n) for...]
    ppermute x17 -> x20, waiting for transfers between devices: 6.99 us -> 5.04 us  [to(): return lax.ppermute(array, axis, [(i, (i + step) % n) for i in range(n)])]
    ppermute x17 -> x20, starting transfers between devices: 30.4 us -> 32 us  [to(): return lax.ppermute(array, axis, [(i, (i + step) % n) for i in range(n)])]
    pallas_call x1, Pallas kernels: 3.31 us -> 1.97 us  [wgrad(): pl.pallas_call(wgrad_kernel, out_shape=shaped(hidden, cols), in_specs=[VM...]
  transfers between devices with their start and end apart: 23 -> 26, of which waited for: 7 -> 5; matrix products, arithmetic and copies ran while one was open for 1% -> 1% of each run, Pallas kernels for 12% -> 14%
where the time goes in v5:
time: 64.4 us; the launch traced here: 64.1 us
  starting transfers between devices  44.7 us (69%)
  Pallas kernels  9.01 us (14%)
  waiting for transfers between devices  8.39 us (13%)
  other arithmetic  1.16 us (2%)
  between operations  0.81 us (1%)
    ppermute x20, starting transfers between devices, to(): return lax.ppermute(array, axis, [(i, (i + step) % n) for i in range(n)])  32 us
    ppermute x6, starting transfers between devices, across(): lax.ppermute(array, 'z', [(i, (i - step if i % 2 else i + step) % n) for...  12.7 us
    ppermute x20, waiting for transfers between devices, to(): return lax.ppermute(array, axis, [(i, (i + step) % n) for i in range(n)])  5.04 us
    ppermute x6, waiting for transfers between devices, across(): lax.ppermute(array, 'z', [(i, (i - step if i % 2 else i + step) % n) for...  3.35 us
    pallas_call x1, Pallas kernels, dgrad(): pl.pallas_call(dgrad_kernel, out_shape=(half, half, shaped(4 * tokens, hi...  2.06 us
    pallas_call x1, Pallas kernels, wgrad(): pl.pallas_call(wgrad_kernel, out_shape=shaped(hidden, cols), in_specs=[VM...  1.97 us
    pallas_call x1, Pallas kernels, forward(): pl.pallas_call(fwd_kernel, out_shape=(out,) * 4 + (shaped(8 * half, cols)...  1.87 us
    pallas_call x1, Pallas kernels, masked_weight(): pl.pallas_call(mask_kernel, out_shape=shaped(hidden, cols), in_specs=[HBM...  1.67 us
  transfers between devices with their start and end apart: 26, of which 5 were waited for; matrix products, arithmetic and copies ran while one was open for 1% of the time, Pallas kernels for 14%

profile of v5, /device:TPU:1, one launch (start us, length us, event | category | flops | bytes accessed | tf_op | source)
XLA Modules:
  0.0 64.1 jit_solution(16678761835904693991)
XLA Ops:
  0.6 2.2 %collective-permute-start.17 = (bf16[448,128]{1,0:T(8,128)(2,1)}, bf16[448,128]{1,0:T(8,128)(2,1)S(1)}, u32[]{:S(2)}, u32[]{:S(2)}) collective-permute-start(bf16[448,128]{1,0:T(8,128)(2,1)} %bitcast.35), channel_id=1, source_target_pairs={{0,1},{1,2},{2,3},{3,0},{4,5},{5,6},{6,7},{7,4},{8,9},{9,10},{10,1... | collective-permute-start | bytes 344072 | tf_op jit(solution)/shard_map/ppermute | solution.py:229
  2.8 2.6 %collective-permute-start.16 = (bf16[448,128]{1,0:T(8,128)(2,1)}, bf16[448,128]{1,0:T(8,128)(2,1)S(1)}, u32[]{:S(2)}, u32[]{:S(2)}) collective-permute-start(bf16[448,128]{1,0:T(8,128)(2,1)} %bitcast.36), channel_id=1, source_target_pairs={{0,2},{1,3},{2,0},{3,1},{4,6},{5,7},{6,4},{7,5},{8,10},{9,11},{10,... | collective-permute-start | bytes 344072 | tf_op jit(solution)/shard_map/ppermute | solution.py:229
  6.5 4.3 %collective-permute-start = (bf16[8,2048]{1,0:T(8,128)(2,1)}, bf16[8,2048]{1,0:T(8,128)(2,1)S(1)}, u32[]{:S(2)}, u32[]{:S(2)}) collective-permute-start(bf16[8,2048]{1,0:T(8,128)(2,1)} %param.4), channel_id=1, source_target_pairs={{0,24},{8,48},{16,40},{24,0},{32,56},{40,16},{48,8},{56,32},{1,25}... | collective-permute-start | bytes 98312 | tf_op jit(solution)/shard_map/ppermute | solution.py:234
  10.9 1.7 %mask_weight.1.refs_10_.w_ref = bf16[448,2048]{1,0:T(8,128)(2,1)S(1)} custom-call(s32[7,32]{1,0:T(8,128)} %bitcast.33, bf16[448,2048]{1,0:T(8,128)(2,1)} %bitcast.40), custom_call_target="tpu_custom_call" | custom-call | flops 1835008 | bytes 4194304 | tf_op jit(solution)/shard_map/mask_weight/pallas_call | solution.py:82
  12.7 2.1 %dgrad.1 = (bf16[4,64,2048]{2,1,0:T(8,128)(2,1)S(1)}, bf16[4,64,2048]{2,1,0:T(8,128)(2,1)S(1)}, bf16[512,448]{1,0:T(8,128)(2,1)S(1)}) custom-call(s32[4]{0:T(128)S(1)} %pad_add_fusion.at_ref, bf16[448,128]{1,0:T(8,128)(2,1)S(1)} %bitcast.38, bf16[448,128]{1,0:T(8,128)(2,1)S(1)} %collective-permute-done.15.d1, ...), custom_call_target="tpu_custom_call" | custom-call | flops 939524096 | bytes 4194304 | tf_op jit(solution)/shard_map/dgrad/pallas_call | solution.py:125
  14.7 1.9 %collective-permute-start.18 = (bf16[4,64,2048]{2,1,0:T(8,128)(2,1)S(1)}, bf16[4,64,2048]{2,1,0:T(8,128)(2,1)S(1)}, u32[]{:S(2)}, u32[]{:S(2)}) collective-permute-start(bf16[4,64,2048]{2,1,0:T(8,128)(2,1)S(1)} %get-tuple-element.16), channel_id=1, source_target_pairs={{0,4},{4,0},{1,5},{5,1},{2,6},{6,2},{3,7},{7,3},{8,12},{12,8},{9,1... | collective-permute-start | bytes 3145736 | tf_op jit(solution)/shard_map/ppermute | solution.py:229
  16.6 3.4 %collective-permute-start.1 = (bf16[16,2048]{1,0:T(8,128)(2,1)S(1)}, bf16[16,2048]{1,0:T(8,128)(2,1)S(1)}, u32[]{:S(2)}, u32[]{:S(2)}) collective-permute-start(bf16[16,2048]{1,0:T(8,128)(2,1)S(1)} %pad_maximum_fusion.1), channel_id=1, source_target_pairs={{0,56},{8,16},{16,8},{24,32},{32,24},{40,48},{48,40},{56,0},{1,57}... | collective-permute-start | bytes 196616 | tf_op jit(solution)/shard_map/ppermute | solution.py:234
  20.1 2.4 %collective-permute-done.1 = bf16[16,2048]{1,0:T(8,128)(2,1)S(1)} collective-permute-done((bf16[16,2048]{1,0:T(8,128)(2,1)S(1)}, bf16[16,2048]{1,0:T(8,128)(2,1)S(1)}, u32[]{:S(2)}, u32[]{:S(2)}) %collective-permute-start.1) | collective-permute-done | bytes 65568 | tf_op jit(solution)/shard_map/ppermute | solution.py:234
  23.4 1.3 %collective-permute-start.19 = (bf16[32,2048]{1,0:T(8,128)(2,1)S(1)}, bf16[32,2048]{1,0:T(8,128)(2,1)S(1)}, u32[]{:S(2)}, u32[]{:S(2)}) collective-permute-start(bf16[32,2048]{1,0:T(8,128)(2,1)S(1)} %get-tuple-element.23), channel_id=1, source_target_pairs={{0,64},{64,128},{128,192},{192,0},{1,65},{65,129},{129,193},{193,1... | collective-permute-start | bytes 393224 | tf_op jit(solution)/shard_map/ppermute | solution.py:229
  24.7 1.5 %collective-permute-start.21 = (bf16[32,2048]{1,0:T(8,128)(2,1)S(1)}, bf16[32,2048]{1,0:T(8,128)(2,1)S(1)}, u32[]{:S(2)}, u32[]{:S(2)}) collective-permute-start(bf16[32,2048]{1,0:T(8,128)(2,1)S(1)} %get-tuple-element.24), channel_id=1, source_target_pairs={{0,192},{64,0},{128,64},{192,128},{1,193},{65,1},{129,65},{193,129... | collective-permute-start | bytes 393224 | tf_op jit(solution)/shard_map/ppermute | solution.py:229
  27.1 1.3 %collective-permute-start.4 = (bf16[64,2048]{1,0:T(8,128)(2,1)S(1)}, bf16[64,2048]{1,0:T(8,128)(2,1)S(1)}, u32[]{:S(2)}, u32[]{:S(2)}) collective-permute-start(bf16[64,2048]{1,0:T(8,128)(2,1)S(1)} %constant_dynamic-update-slice_fusion.refs_0_), channel_id=1, source_target_pairs={{0,64},{64,128},{128,192},{192,0},{1,65},{65,129},{129,193},{193,1... | collective-permute-start | bytes 786440 | tf_op jit(solution)/shard_map/ppermute | solution.py:229
  28.3 1.5 %collective-permute-start.3 = (bf16[64,2048]{1,0:T(8,128)(2,1)S(1)}, bf16[64,2048]{1,0:T(8,128)(2,1)S(1)}, u32[]{:S(2)}, u32[]{:S(2)}) collective-permute-start(bf16[64,2048]{1,0:T(8,128)(2,1)S(1)} %constant_dynamic-update-slice_fusion.refs_0_), channel_id=1, source_target_pairs={{0,192},{64,0},{128,64},{192,128},{1,193},{65,1},{129,65},{193,129... | collective-permute-start | bytes 786440 | tf_op jit(solution)/shard_map/ppermute | solution.py:229
  30.3 2.5 %collective-permute-start.22 = (bf16[64,2048]{1,0:T(8,128)(2,1)S(1)}, bf16[64,2048]{1,0:T(8,128)(2,1)S(1)}, u32[]{:S(2)}, u32[]{:S(2)}) collective-permute-start(bf16[64,2048]{1,0:T(8,128)(2,1)S(1)} %get-tuple-element.22), channel_id=1, source_target_pairs={{0,192},{64,0},{128,64},{192,128},{1,193},{65,1},{129,65},{193,129... | collective-permute-start | bytes 786440 | tf_op jit(solution)/shard_map/ppermute | solution.py:229
  32.8 2.0 %collective-permute-done.4.refs_4_ = bf16[64,2048]{1,0:T(8,128)(2,1)S(1)} collective-permute-done((bf16[64,2048]{1,0:T(8,128)(2,1)S(1)}, bf16[64,2048]{1,0:T(8,128)(2,1)S(1)}, u32[]{:S(2)}, u32[]{:S(2)}) %collective-permute-start.4) | collective-permute-done | bytes 262176 | tf_op jit(solution)/shard_map/ppermute | solution.py:229
  34.9 2.9 %collective-permute-start.6 = (bf16[32,2048]{1,0:T(8,128)(2,1)S(1)}, bf16[32,2048]{1,0:T(8,128)(2,1)S(1)}, u32[]{:S(2)}, u32[]{:S(2)}) collective-permute-start(bf16[32,2048]{1,0:T(8,128)(2,1)S(1)} %slice.125), channel_id=1, source_target_pairs={{0,192},{64,0},{128,64},{192,128},{1,193},{65,1},{129,65},{193,129... | collective-permute-start | bytes 393224 | tf_op jit(solution)/shard_map/ppermute | solution.py:229
  37.8 2.6 %collective-permute-done.20 = bf16[64,2048]{1,0:T(8,128)(2,1)S(1)} collective-permute-done((bf16[64,2048]{1,0:T(8,128)(2,1)S(1)}, bf16[64,2048]{1,0:T(8,128)(2,1)S(1)}, u32[]{:S(2)}, u32[]{:S(2)}) %collective-permute-start.20) | collective-permute-done | bytes 262176 | tf_op jit(solution)/shard_map/ppermute | solution.py:229
  40.7 4.3 %collective-permute-start.7 = (bf16[64,2048]{1,0:T(8,128)(2,1)S(1)}, bf16[64,2048]{1,0:T(8,128)(2,1)S(1)}, u32[]{:S(2)}, u32[]{:S(2)}) collective-permute-start(bf16[64,2048]{1,0:T(8,128)(2,1)S(1)} %constant_dynamic-update-slice_fusion.refs_0_), channel_id=1, source_target_pairs={{0,4},{4,0},{1,5},{5,1},{2,6},{6,2},{3,7},{7,3},{8,12},{12,8},{9,1... | collective-permute-start | bytes 786440 | tf_op jit(solution)/shard_map/ppermute | solution.py:229
  45.6 3.7 %collective-permute-start.10 = (bf16[32,2048]{1,0:T(8,128)(2,1)S(1)}, bf16[32,2048]{1,0:T(8,128)(2,1)S(1)}, u32[]{:S(2)}, u32[]{:S(2)}) collective-permute-start(bf16[32,2048]{1,0:T(8,128)(2,1)S(1)} %collective-permute-done.6.refs_3_), channel_id=1, source_target_pairs={{0,4},{4,0},{1,5},{5,1},{2,6},{6,2},{3,7},{7,3},{8,12},{12,8},{9,1... | collective-permute-start | bytes 393224 | tf_op jit(solution)/shard_map/ppermute | solution.py:229
  49.4 2.2 %collective-permute-start.24 = (bf16[16,2048]{1,0:T(8,128)(2,1)S(1)}, bf16[16,2048]{1,0:T(8,128)(2,1)S(1)}, u32[]{:S(2)}, u32[]{:S(2)}) collective-permute-start(bf16[16,2048]{1,0:T(8,128)(2,1)S(1)} %get-tuple-element.26), channel_id=1, source_target_pairs={{0,56},{8,16},{16,8},{24,32},{32,24},{40,48},{48,40},{56,0},{1,57}... | collective-permute-start | bytes 196616 | tf_op jit(solution)/shard_map/ppermute | solution.py:234
  51.6 1.9 %forward.1 = (bf16[448,128]{1,0:T(8,128)(2,1)S(1)}, bf16[448,128]{1,0:T(8,128)(2,1)S(1)}, bf16[448,128]{1,0:T(8,128)(2,1)S(1)}, bf16[448,128]{1,0:T(8,128)(2,1)S(1)}, bf16[512,2048]{1,0:T(8,128)(2,1)S(1)}) custom-call(s32[4]{0:T(128)S(1)} %pad_add_fusion.at_ref, bf16[64,2048]{1,0:T(8,128)(2,1)S(1)} %constant_dynamic-update-slice_fusion.refs_0_, ...), custom_call_target="tpu_custom_call" | custom-call | flops 939524096 | bytes 6291456 | tf_op jit(solution)/shard_map/forward/pallas_call | solution.py:158
  54.5 2.1 %collective-permute-start.13 = (bf16[448,128]{1,0:T(8,128)(2,1)S(1)}, bf16[448,128]{1,0:T(8,128)(2,1)S(1)}, u32[]{:S(2)}, u32[]{:S(2)}) collective-permute-start(bf16[448,128]{1,0:T(8,128)(2,1)S(1)} %get-tuple-element.13), channel_id=1, source_target_pairs={{0,2},{1,3},{2,0},{3,1},{4,6},{5,7},{6,4},{7,5},{8,10},{9,11},{10,... | collective-permute-start | bytes 344072 | tf_op jit(solution)/shard_map/ppermute | solution.py:229
  57.9 1.7 %collective-permute-start.25 = (bf16[8,2048]{1,0:T(8,128)(2,1)S(1)}, bf16[8,2048]{1,0:T(8,128)(2,1)S(1)}, u32[]{:S(2)}, u32[]{:S(2)}) collective-permute-start(bf16[8,2048]{1,0:T(8,128)(2,1)S(1)} %add_convert_fusion.5), channel_id=1, source_target_pairs={{0,24},{8,48},{16,40},{24,0},{32,56},{40,16},{48,8},{56,32},{1,25}... | collective-permute-start | bytes 98312 | tf_op jit(solution)/shard_map/ppermute | solution.py:234
  59.6 2.0 %wgrad.1 = bf16[448,2048]{1,0:T(8,128)(2,1)} custom-call(bf16[512,448]{1,0:T(8,128)(2,1)S(1)} %get-tuple-element.17.dy_ref, bf16[512,2048]{1,0:T(8,128)(2,1)S(1)} %get-tuple-element.18.a_ref, s32[7,32]{1,0:T(8,128)S(1)} %bitcast.34), custom_call_target="tpu_custom_call" | custom-call | flops 939524096 | bytes 6291456 | tf_op jit(solution)/shard_map/wgrad/pallas_call | solution.py:195
  62.0 1.4 %finish.1 = bf16[448,128]{1,0:T(8,128)(2,1)} custom-call(s32[4]{0:T(128)S(1)} %pad_add_fusion.at_ref, bf16[448,128]{1,0:T(8,128)(2,1)S(1)} %get-tuple-element.11.r0, bf16[448,128]{1,0:T(8,128)(2,1)S(1)} %collective-permute-done.12.r1, bf16[448,128]{1,0:T(8,128)(2,1)S(1)} %collective-permute-done.13.r2, bf16[448,128]{1,0:T(8,128)(2,1)S(1)} %collective-permute-done.14.r3), custom_call_target="tpu_custom_call" | custom-call | flops 14680064 | bytes 1048576 | tf_op jit(solution)/shard_map/finish/pallas_call | solution.py:216
  (54 shorter events, 7.9 us)
Async XLA Ops:
  0.6 12.0 %collective-permute-start.17 = (bf16[448,128]{1,0:T(8,128)(2,1)}, bf16[448,128]{1,0:T(8,128)(2,1)S(1)}, u32[]{:S(2)}, u32[]{:S(2)}) collective-permute-start(bf16[448,128]{1,0:T(8,128)(2,1)} %bitcast.35), channel_id=1, source_target_pairs={{0,1},{1,2},{2,3},{3,0},{4,5},{5,6},{6,7},{7,4},{8,9},{9,10},{10,1... | collective-permute-start | bytes 344072 | tf_op jit(solution)/shard_map/ppermute | solution.py:229
  2.8 9.8 %collective-permute-start.16 = (bf16[448,128]{1,0:T(8,128)(2,1)}, bf16[448,128]{1,0:T(8,128)(2,1)S(1)}, u32[]{:S(2)}, u32[]{:S(2)}) collective-permute-start(bf16[448,128]{1,0:T(8,128)(2,1)} %bitcast.36), channel_id=1, source_target_pairs={{0,2},{1,3},{2,0},{3,1},{4,6},{5,7},{6,4},{7,5},{8,10},{9,11},{10,... | collective-permute-start | bytes 344072 | tf_op jit(solution)/shard_map/ppermute | solution.py:229
  5.4 7.2 %collective-permute-start.15 = (bf16[448,128]{1,0:T(8,128)(2,1)}, bf16[448,128]{1,0:T(8,128)(2,1)S(1)}, u32[]{:S(2)}, u32[]{:S(2)}) collective-permute-start(bf16[448,128]{1,0:T(8,128)(2,1)} %bitcast.37), channel_id=1, source_target_pairs={{0,3},{1,0},{2,1},{3,2},{4,7},{5,4},{6,5},{7,6},{8,11},{9,8},{10,9... | collective-permute-start | bytes 344072 | tf_op jit(solution)/shard_map/ppermute | solution.py:229
  6.5 10.1 %collective-permute-start = (bf16[8,2048]{1,0:T(8,128)(2,1)}, bf16[8,2048]{1,0:T(8,128)(2,1)S(1)}, u32[]{:S(2)}, u32[]{:S(2)}) collective-permute-start(bf16[8,2048]{1,0:T(8,128)(2,1)} %param.4), channel_id=1, source_target_pairs={{0,24},{8,48},{16,40},{24,0},{32,56},{40,16},{48,8},{56,32},{1,25}... | collective-permute-start | bytes 98312 | tf_op jit(solution)/shard_map/ppermute | solution.py:234
  14.7 8.6 %collective-permute-start.18 = (bf16[4,64,2048]{2,1,0:T(8,128)(2,1)S(1)}, bf16[4,64,2048]{2,1,0:T(8,128)(2,1)S(1)}, u32[]{:S(2)}, u32[]{:S(2)}) collective-permute-start(bf16[4,64,2048]{2,1,0:T(8,128)(2,1)S(1)} %get-tuple-element.16), channel_id=1, source_target_pairs={{0,4},{4,0},{1,5},{5,1},{2,6},{6,2},{3,7},{7,3},{8,12},{12,8},{9,1... | collective-permute-start | bytes 3145736 | tf_op jit(solution)/shard_map/ppermute | solution.py:229
  16.6 5.9 %collective-permute-start.1 = (bf16[16,2048]{1,0:T(8,128)(2,1)S(1)}, bf16[16,2048]{1,0:T(8,128)(2,1)S(1)}, u32[]{:S(2)}, u32[]{:S(2)}) collective-permute-start(bf16[16,2048]{1,0:T(8,128)(2,1)S(1)} %pad_maximum_fusion.1), channel_id=1, source_target_pairs={{0,56},{8,16},{16,8},{24,32},{32,24},{40,48},{48,40},{56,0},{1,57}... | collective-permute-start | bytes 196616 | tf_op jit(solution)/shard_map/ppermute | solution.py:234
  23.4 6.4 %collective-permute-start.19 = (bf16[32,2048]{1,0:T(8,128)(2,1)S(1)}, bf16[32,2048]{1,0:T(8,128)(2,1)S(1)}, u32[]{:S(2)}, u32[]{:S(2)}) collective-permute-start(bf16[32,2048]{1,0:T(8,128)(2,1)S(1)} %get-tuple-element.23), channel_id=1, source_target_pairs={{0,64},{64,128},{128,192},{192,0},{1,65},{65,129},{129,193},{193,1... | collective-permute-start | bytes 393224 | tf_op jit(solution)/shard_map/ppermute | solution.py:229
  24.7 5.1 %collective-permute-start.21 = (bf16[32,2048]{1,0:T(8,128)(2,1)S(1)}, bf16[32,2048]{1,0:T(8,128)(2,1)S(1)}, u32[]{:S(2)}, u32[]{:S(2)}) collective-permute-start(bf16[32,2048]{1,0:T(8,128)(2,1)S(1)} %get-tuple-element.24), channel_id=1, source_target_pairs={{0,192},{64,0},{128,64},{192,128},{1,193},{65,1},{129,65},{193,129... | collective-permute-start | bytes 393224 | tf_op jit(solution)/shard_map/ppermute | solution.py:229
  27.1 7.7 %collective-permute-start.4 = (bf16[64,2048]{1,0:T(8,128)(2,1)S(1)}, bf16[64,2048]{1,0:T(8,128)(2,1)S(1)}, u32[]{:S(2)}, u32[]{:S(2)}) collective-permute-start(bf16[64,2048]{1,0:T(8,128)(2,1)S(1)} %constant_dynamic-update-slice_fusion.refs_0_), channel_id=1, source_target_pairs={{0,64},{64,128},{128,192},{192,0},{1,65},{65,129},{129,193},{193,1... | collective-permute-start | bytes 786440 | tf_op jit(solution)/shard_map/ppermute | solution.py:229
  28.3 6.5 %collective-permute-start.3 = (bf16[64,2048]{1,0:T(8,128)(2,1)S(1)}, bf16[64,2048]{1,0:T(8,128)(2,1)S(1)}, u32[]{:S(2)}, u32[]{:S(2)}) collective-permute-start(bf16[64,2048]{1,0:T(8,128)(2,1)S(1)} %constant_dynamic-update-slice_fusion.refs_0_), channel_id=1, source_target_pairs={{0,192},{64,0},{128,64},{192,128},{1,193},{65,1},{129,65},{193,129... | collective-permute-start | bytes 786440 | tf_op jit(solution)/shard_map/ppermute | solution.py:229
  30.0 10.4 %collective-permute-start.20 = (bf16[64,2048]{1,0:T(8,128)(2,1)S(1)}, bf16[64,2048]{1,0:T(8,128)(2,1)S(1)}, u32[]{:S(2)}, u32[]{:S(2)}) collective-permute-start(bf16[64,2048]{1,0:T(8,128)(2,1)S(1)} %get-tuple-element.21), channel_id=1, source_target_pairs={{0,64},{64,128},{128,192},{192,0},{1,65},{65,129},{129,193},{193,1... | collective-permute-start | bytes 786440 | tf_op jit(solution)/shard_map/ppermute | solution.py:229
  30.3 10.1 %collective-permute-start.22 = (bf16[64,2048]{1,0:T(8,128)(2,1)S(1)}, bf16[64,2048]{1,0:T(8,128)(2,1)S(1)}, u32[]{:S(2)}, u32[]{:S(2)}) collective-permute-start(bf16[64,2048]{1,0:T(8,128)(2,1)S(1)} %get-tuple-element.22), channel_id=1, source_target_pairs={{0,192},{64,0},{128,64},{192,128},{1,193},{65,1},{129,65},{193,129... | collective-permute-start | bytes 786440 | tf_op jit(solution)/shard_map/ppermute | solution.py:229
  34.8 10.3 %collective-permute-start.5 = (bf16[32,2048]{1,0:T(8,128)(2,1)S(1)}, bf16[32,2048]{1,0:T(8,128)(2,1)S(1)}, u32[]{:S(2)}, u32[]{:S(2)}) collective-permute-start(bf16[32,2048]{1,0:T(8,128)(2,1)S(1)} %slice.124), channel_id=1, source_target_pairs={{0,64},{64,128},{128,192},{192,0},{1,65},{65,129},{129,193},{193,1... | collective-permute-start | bytes 393224 | tf_op jit(solution)/shard_map/ppermute | solution.py:229
  34.9 10.7 %collective-permute-start.6 = (bf16[32,2048]{1,0:T(8,128)(2,1)S(1)}, bf16[32,2048]{1,0:T(8,128)(2,1)S(1)}, u32[]{:S(2)}, u32[]{:S(2)}) collective-permute-start(bf16[32,2048]{1,0:T(8,128)(2,1)S(1)} %slice.125), channel_id=1, source_target_pairs={{0,192},{64,0},{128,64},{192,128},{1,193},{65,1},{129,65},{193,129... | collective-permute-start | bytes 393224 | tf_op jit(solution)/shard_map/ppermute | solution.py:229
  40.7 8.6 %collective-permute-start.7 = (bf16[64,2048]{1,0:T(8,128)(2,1)S(1)}, bf16[64,2048]{1,0:T(8,128)(2,1)S(1)}, u32[]{:S(2)}, u32[]{:S(2)}) collective-permute-start(bf16[64,2048]{1,0:T(8,128)(2,1)S(1)} %constant_dynamic-update-slice_fusion.refs_0_), channel_id=1, source_target_pairs={{0,4},{4,0},{1,5},{5,1},{2,6},{6,2},{3,7},{7,3},{8,12},{12,8},{9,1... | collective-permute-start | bytes 786440 | tf_op jit(solution)/shard_map/ppermute | solution.py:229
  45.0 6.5 %collective-permute-start.11 = (bf16[64,2048]{1,0:T(8,128)(2,1)S(1)}, bf16[64,2048]{1,0:T(8,128)(2,1)S(1)}, u32[]{:S(2)}, u32[]{:S(2)}) collective-permute-start(bf16[64,2048]{1,0:T(8,128)(2,1)S(1)} %collective-permute-done.4.refs_4_), channel_id=1, source_target_pairs={{0,4},{4,0},{1,5},{5,1},{2,6},{6,2},{3,7},{7,3},{8,12},{12,8},{9,1... | collective-permute-start | bytes 786440 | tf_op jit(solution)/shard_map/ppermute | solution.py:229
  45.0 6.5 %collective-permute-start.8 = (bf16[64,2048]{1,0:T(8,128)(2,1)S(1)}, bf16[64,2048]{1,0:T(8,128)(2,1)S(1)}, u32[]{:S(2)}, u32[]{:S(2)}) collective-permute-start(bf16[64,2048]{1,0:T(8,128)(2,1)S(1)} %collective-permute-done.3.refs_1_), channel_id=1, source_target_pairs={{0,4},{4,0},{1,5},{5,1},{2,6},{6,2},{3,7},{7,3},{8,12},{12,8},{9,1... | collective-permute-start | bytes 786440 | tf_op jit(solution)/shard_map/ppermute | solution.py:229
  45.5 6.0 %collective-permute-start.9 = (bf16[32,2048]{1,0:T(8,128)(2,1)S(1)}, bf16[32,2048]{1,0:T(8,128)(2,1)S(1)}, u32[]{:S(2)}, u32[]{:S(2)}) collective-permute-start(bf16[32,2048]{1,0:T(8,128)(2,1)S(1)} %collective-permute-done.5.refs_2_), channel_id=1, source_target_pairs={{0,4},{4,0},{1,5},{5,1},{2,6},{6,2},{3,7},{7,3},{8,12},{12,8},{9,1... | collective-permute-start | bytes 393224 | tf_op jit(solution)/shard_map/ppermute | solution.py:229
  45.6 5.9 %collective-permute-start.10 = (bf16[32,2048]{1,0:T(8,128)(2,1)S(1)}, bf16[32,2048]{1,0:T(8,128)(2,1)S(1)}, u32[]{:S(2)}, u32[]{:S(2)}) collective-permute-start(bf16[32,2048]{1,0:T(8,128)(2,1)S(1)} %collective-permute-done.6.refs_3_), channel_id=1, source_target_pairs={{0,4},{4,0},{1,5},{5,1},{2,6},{6,2},{3,7},{7,3},{8,12},{12,8},{9,1... | collective-permute-start | bytes 393224 | tf_op jit(solution)/shard_map/ppermute | solution.py:229
  49.4 8.6 %collective-permute-start.24 = (bf16[16,2048]{1,0:T(8,128)(2,1)S(1)}, bf16[16,2048]{1,0:T(8,128)(2,1)S(1)}, u32[]{:S(2)}, u32[]{:S(2)}) collective-permute-start(bf16[16,2048]{1,0:T(8,128)(2,1)S(1)} %get-tuple-element.26), channel_id=1, source_target_pairs={{0,56},{8,16},{16,8},{24,32},{32,24},{40,48},{48,40},{56,0},{1,57}... | collective-permute-start | bytes 196616 | tf_op jit(solution)/shard_map/ppermute | solution.py:234
  53.4 8.2 %collective-permute-start.12 = (bf16[448,128]{1,0:T(8,128)(2,1)S(1)}, bf16[448,128]{1,0:T(8,128)(2,1)S(1)}, u32[]{:S(2)}, u32[]{:S(2)}) collective-permute-start(bf16[448,128]{1,0:T(8,128)(2,1)S(1)} %get-tuple-element.12), channel_id=1, source_target_pairs={{0,1},{1,2},{2,3},{3,0},{4,5},{5,6},{6,7},{7,4},{8,9},{9,10},{10,1... | collective-permute-start | bytes 344072 | tf_op jit(solution)/shard_map/ppermute | solution.py:229
  54.5 7.6 %collective-permute-start.13 = (bf16[448,128]{1,0:T(8,128)(2,1)S(1)}, bf16[448,128]{1,0:T(8,128)(2,1)S(1)}, u32[]{:S(2)}, u32[]{:S(2)}) collective-permute-start(bf16[448,128]{1,0:T(8,128)(2,1)S(1)} %get-tuple-element.13), channel_id=1, source_target_pairs={{0,2},{1,3},{2,0},{3,1},{4,6},{5,7},{6,4},{7,5},{8,10},{9,11},{10,... | collective-permute-start | bytes 344072 | tf_op jit(solution)/shard_map/ppermute | solution.py:229
  56.6 5.4 %collective-permute-start.14 = (bf16[448,128]{1,0:T(8,128)(2,1)S(1)}, bf16[448,128]{1,0:T(8,128)(2,1)S(1)}, u32[]{:S(2)}, u32[]{:S(2)}) collective-permute-start(bf16[448,128]{1,0:T(8,128)(2,1)S(1)} %get-tuple-element.14), channel_id=1, source_target_pairs={{0,3},{1,0},{2,1},{3,2},{4,7},{5,4},{6,5},{7,6},{8,11},{9,8},{10,9... | collective-permute-start | bytes 344072 | tf_op jit(solution)/shard_map/ppermute | solution.py:229
  57.9 5.6 %collective-permute-start.25 = (bf16[8,2048]{1,0:T(8,128)(2,1)S(1)}, bf16[8,2048]{1,0:T(8,128)(2,1)S(1)}, u32[]{:S(2)}, u32[]{:S(2)}) collective-permute-start(bf16[8,2048]{1,0:T(8,128)(2,1)S(1)} %add_convert_fusion.5), channel_id=1, source_target_pairs={{0,24},{8,48},{16,40},{24,0},{32,56},{40,16},{48,8},{56,32},{1,25}... | collective-permute-start | bytes 98312 | tf_op jit(solution)/shard_map/ppermute | solution.py:234
  (5 other events, 25.8 us)

commit v6 on v5

--- a/solution.py
+++ b/solution.py
@@ -96,7 +96,7 @@
     )(mt, wt)
 
 
-def dgrad_kernel(at_ref, d0, d1, d2, d3, w_ref, keep_ref, send_ref, dy_ref):
+def dgrad_kernel(at_ref, d0, d1, d2, d3, w_ref, keep_ref, far_ref, send_ref, dy_ref):
     x, y, core, z = (at_ref[i] for i in range(4))
     tokens = d0.shape[1]
     cols = w_ref.shape[1]
@@ -115,34 +115,62 @@
         for p in range(4):
             first = p * tokens
             keep_ref[p, :, span] = total[first : first + half]
-            send_ref[p, :, span] = total[first + half : first + tokens]
+            other = total[first + half : first + tokens]
+            if p == 2:
+                far_ref[:, span] = other
+            else:
+                send_ref[min(p, 2), :, span] = other
 
 
 def dgrad(at, blocks, masked):
     hidden, tokens = blocks[0].shape
     cols = masked.shape[1]
-    half = shaped(4, tokens // 2, cols)
+    half = tokens // 2
     return pl.pallas_call(
         dgrad_kernel,
-        out_shape=(half, half, shaped(4 * tokens, hidden)),
+        out_shape=(
+            shaped(4, half, cols),
+            shaped(half, cols),
+            shaped(3, half, cols),
+            shaped(4 * tokens, hidden),
+        ),
         in_specs=[SMEM] + [VMEM] * 5,
-        out_specs=(VMEM,) * 3,
+        out_specs=(VMEM,) * 4,
         cost_estimate=cost(8 * tokens * hidden * cols, 4 << 20),
         compiler_params=grant(12),
         name="dgrad",
     )(at, *blocks, masked)
 
 
+def join_kernel(*refs):
+    rows = refs[0].shape[0]
+    for i, ref in enumerate(refs[:-1]):
+        refs[-1][i * rows : (i + 1) * rows, :] = ref[...]
+
+
+def join(parts):
+    rows, cols = parts[0].shape
+    return pl.pallas_call(
+        join_kernel,
+        out_shape=shaped(len(parts) * rows, cols),
+        in_specs=[VMEM] * len(parts),
+        out_specs=VMEM,
+        cost_estimate=cost(0, 4 * len(parts) * rows * cols),
+        compiler_params=grant(4),
+        name="join",
+    )(*parts)
+
+
 def fwd_kernel(at_ref, *refs):
-    mine, other = refs[:5], refs[5:10]
-    w_ref, o0, o1, o2, o3, full_ref, acc_ref = refs[10:]
+    pieces = refs[:8]
+    w_ref, o0, o1, o2, o3, full_ref, acc_ref = refs[8:]
     x, y = at_ref[0], at_ref[1]
-    half = mine[0].shape[0]
-    tokens = 2 * half
-    for h, group in enumerate((mine, other)):
-        for piece, first in zip(group, (0, 2 * half, 4 * half, 4 * half + half // 2, 6 * half)):
-            start = first + h * half
-            full_ref[start : start + piece.shape[0], :] = piece[...]
+    rows = pieces[0].shape[0] // 4
+    tokens = 8 * rows
+    for i, piece in enumerate(pieces):
+        for p in range(4):
+            start = p * tokens + i * rows
+            full_ref[start : start + rows, :] = piece[p * rows : (p + 1) * rows, :]
     acc_ref[...] = lax.dot_general(
         w_ref[...], full_ref[...], (((1,), (1,)), ((), ())), preferred_element_type=F32
     ).astype(BF)
@@ -151,20 +179,20 @@
         out[...] = acc_ref[:, pl.ds(pl.multiple_of(rel * tokens, tokens), tokens)]
 
 
-def forward(at, mine, other, masked):
-    half, cols = mine[0].shape
+def forward(at, pieces, masked):
+    rows, cols = pieces[0].shape
     hidden = masked.shape[0]
-    out = shaped(hidden, 2 * half)
+    out = shaped(hidden, 2 * rows)
     return pl.pallas_call(
         fwd_kernel,
-        out_shape=(out,) * 4 + (shaped(8 * half, cols),),
-        in_specs=[SMEM] + [VMEM] * 11,
+        out_shape=(out,) * 4 + (shaped(8 * rows, cols),),
+        in_specs=[SMEM] + [VMEM] * 9,
         out_specs=(VMEM,) * 5,
-        scratch_shapes=[pltpu.VMEM((hidden, 8 * half), BF)],
-        cost_estimate=cost(16 * half * hidden * cols, 6 << 20),
+        scratch_shapes=[pltpu.VMEM((hidden, 8 * rows), BF)],
+        cost_estimate=cost(16 * rows * hidden * cols, 6 << 20),
         compiler_params=grant(14),
         name="forward",
-    )(at, *mine, *other, masked)
+    )(at, *pieces, masked)
 
 
 def wgrad_kernel(dy_ref, a_ref, m_ref, o_hbm, o_ref, sems):
@@ -235,7 +263,7 @@
 
 
 def with_partner(array, step):
-    return jnp.concatenate([array, across(array, step)])
+    return join((array, across(array, step)))
 
 
 def halved(*terms):
@@ -252,38 +280,37 @@
     wt, mt, dyt = up_weight.T, block_mask.T, out_grad.T
 
     blocks = (dyt, to(dyt, "narrow", -1), to(dyt, "narrow", 2), to(dyt, "narrow", 1))
+    near = with_partner(activations, STEPS[0])
+    far = to(near, "x", 2)
+    before, after = to(near, "x", 1), to(near, "x", -1)
     masked = masked_weight(in_hbm(mt), in_hbm(wt))
-    near = with_partner(activations, STEPS[0])
-    keep, send, dy = dgrad(at, blocks, masked)
+    keep, send_far, send, dy = dgrad(at, blocks, masked)
+    got_far = to(send_far, "core", 1)
     got = to(send, "core", 1)
-    near = with_partner(near, STEPS[1])
-    near = with_partner(near, STEPS[2])
-    half = keep.shape[1] // 2
-    low, high = halved(keep[2], got[2])
+    own = join((near, after, far, before))
+    side = across(own, STEPS[1])
+    up_own = across(own, STEPS[2])
+    up_side = across(side, STEPS[2])
+    pieces = own, side, up_own, up_side
+    swapped = [to(piece, "core", 1) for piece in pieces[:3]]
+    swapped.append(to(up_side, "core", 1))
+    low, high = halved(keep[2], got_far)
     ahead = to(low, "x", 1)
     behind = to(high, "x", -1)
     none = jnp.zeros_like(ahead)
     right = added(keep[1], got[1], jnp.concatenate([ahead, none]))
-    left = added(keep[3], got[3], jnp.concatenate([none, behind]))
+    left = added(keep[3], got[2], jnp.concatenate([none, behind]))
     right = to(right, "x", 1)
     left = to(left, "x", -1)
-    own, away = halved(keep[0], got[0], right, left)
+    rest, away = halved(keep[0], got[0], right, left)
     came = across(away, STEPS[2])
-    own, away = halved(own, came)
+    rest, away = halved(rest, came)
     came = across(away, STEPS[1])
-    own, away = halved(own, came)
+    rest, away = halved(rest, came)
     came = across(away, STEPS[0])
-    input_grad = added(own, came)
-
-    before = to(near, "x", 1)
-    after = to(near, "x", -1)
-    far_low = to(before[:half], "x", 1)
-    far_high = to(after[half:], "x", -1)
-    mine = (near, after, far_low, far_high, before)
-    near, after, before = (to(m, "core", 1) for m in (near, after, before))
-    far_low, far_high = to(far_low, "core", 1), to(far_high, "core", 1)
-    other = (near, after, far_low, far_high, before)
-    o0, o1, o2, o3, full = forward(at, mine, other, masked)
+    input_grad = added(rest, came)
+
+    o0, o1, o2, o3, full = forward(at, (*pieces, *swapped), masked)
     parts = (o0, to(o1, "narrow", 1), to(o2, "narrow", 2), to(o3, "narrow", -1))
     output = finish(at, parts).T
     weight_grad = wgrad(dy, full, mt).T

time: 64.4 us -> 67.6 us (1.050); the launches traced: 64.1 us -> 66.3 us
  waiting for transfers between devices: 8.39 us -> 10.1 us
    ppermute x20 -> x19, waiting for transfers between devices: 5.04 us -> 7.97 us  [to(): return lax.ppermute(array, axis, [(i, (i + step) % n) for i in range(n)])]
    ppermute x6 -> x7, waiting for transfers between devices: 3.35 us -> 2.13 us  [across(): lax.ppermute(array, 'z', [(i, (i - step if i % 2 else i + step) % n) for...]
    ppermute x20 -> x19, starting transfers between devices: 32 us -> 32.8 us  [to(): return lax.ppermute(array, axis, [(i, (i + step) % n) for i in range(n)])]
    ppermute x6 -> x7, starting transfers between devices: 12.7 us -> 12.4 us  [across(): lax.ppermute(array, 'z', [(i, (i - step if i % 2 else i + step) % n) for...]
    pallas_call x2 -> x4, Pallas kernels: 3.93 us -> 3.95 us  [the longest x1 2.06 us: dgrad(): pl.pallas_call(dgrad_kernel, out_shape=(shaped(4, half, cols), shaped(hal...]
  transfers between devices with their start and end apart: 26 -> 26, of which waited for: 5 -> 5; matrix products, arithmetic and copies ran while one was open for 1% -> 1% of each run, Pallas kernels for 14% -> 10%
where the time goes in v6:
time: 67.6 us; the launch traced here: 66.3 us
  starting transfers between devices  45.3 us (67%)
  waiting for transfers between devices  10.1 us (15%)
  Pallas kernels  9.03 us (13%)
  other arithmetic  1.13 us (2%)
  between operations  0.77 us (1%)
    ppermute x19, starting transfers between devices, to(): return lax.ppermute(array, axis, [(i, (i + step) % n) for i in range(n)])  32.8 us
    ppermute x7, starting transfers between devices, across(): lax.ppermute(array, 'z', [(i, (i - step if i % 2 else i + step) % n) for...  12.4 us
    ppermute x19, waiting for transfers between devices, to(): return lax.ppermute(array, axis, [(i, (i + step) % n) for i in range(n)])  7.97 us
    ppermute x7, waiting for transfers between devices, across(): lax.ppermute(array, 'z', [(i, (i - step if i % 2 else i + step) % n) for...  2.13 us
    pallas_call x1, Pallas kernels, dgrad(): pl.pallas_call(dgrad_kernel, out_shape=(shaped(4, half, cols), shaped(hal...  2.06 us
    pallas_call x1, Pallas kernels, wgrad(): pl.pallas_call(wgrad_kernel, out_shape=shaped(hidden, cols), in_specs=[VM...  1.97 us
    pallas_call x1, Pallas kernels, forward(): pl.pallas_call(fwd_kernel, out_shape=(out,) * 4 + (shaped(8 * rows, cols)...  1.87 us
    pallas_call x1, Pallas kernels, masked_weight(): pl.pallas_call(mask_kernel, out_shape=shaped(hidden, cols), in_specs=[HBM...  1.67 us
  transfers between devices with their start and end apart: 26, of which 5 were waited for; matrix products, arithmetic and copies ran while one was open for 1% of the time, Pallas kernels for 10%

profile of v6, /device:TPU:1, one launch (start us, length us, event | category | flops | bytes accessed | tf_op | source)
XLA Modules:
  0.0 66.3 jit_solution(1151093315224376579)
XLA Ops:
  0.6 2.2 %collective-permute-start.16 = (bf16[448,128]{1,0:T(8,128)(2,1)}, bf16[448,128]{1,0:T(8,128)(2,1)S(1)}, u32[]{:S(2)}, u32[]{:S(2)}) collective-permute-start(bf16[448,128]{1,0:T(8,128)(2,1)} %bitcast.37), channel_id=1, source_target_pairs={{0,1},{1,2},{2,3},{3,0},{4,5},{5,6},{6,7},{7,4},{8,9},{9,10},{10,1... | collective-permute-start | bytes 344072 | tf_op jit(solution)/shard_map/ppermute | solution.py:257
  2.8 2.6 %collective-permute-start.15 = (bf16[448,128]{1,0:T(8,128)(2,1)}, bf16[448,128]{1,0:T(8,128)(2,1)S(1)}, u32[]{:S(2)}, u32[]{:S(2)}) collective-permute-start(bf16[448,128]{1,0:T(8,128)(2,1)} %bitcast.38), channel_id=1, source_target_pairs={{0,2},{1,3},{2,0},{3,1},{4,6},{5,7},{6,4},{7,5},{8,10},{9,11},{10,... | collective-permute-start | bytes 344072 | tf_op jit(solution)/shard_map/ppermute | solution.py:257
  6.5 1.7 %mask_weight.1.refs_8_.w_ref = bf16[448,2048]{1,0:T(8,128)(2,1)S(1)} custom-call(s32[7,32]{1,0:T(8,128)} %bitcast.35, bf16[448,2048]{1,0:T(8,128)(2,1)} %bitcast.42), custom_call_target="tpu_custom_call" | custom-call | flops 1835008 | bytes 4194304 | tf_op jit(solution)/shard_map/mask_weight/pallas_call | solution.py:82
  8.3 2.4 %collective-permute-done.15.d2 = bf16[448,128]{1,0:T(8,128)(2,1)S(1)} collective-permute-done((bf16[448,128]{1,0:T(8,128)(2,1)}, bf16[448,128]{1,0:T(8,128)(2,1)S(1)}, u32[]{:S(2)}, u32[]{:S(2)}) %collective-permute-start.15) | collective-permute-done | bytes 114720 | tf_op jit(solution)/shard_map/ppermute | solution.py:257
  10.7 2.1 %dgrad.1 = (bf16[4,64,2048]{2,1,0:T(8,128)(2,1)S(1)}, bf16[64,2048]{1,0:T(8,128)(2,1)S(1)}, bf16[3,64,2048]{2,1,0:T(8,128)(2,1)S(1)}, bf16[512,448]{1,0:T(8,128)(2,1)S(1)}) custom-call(s32[4]{0:T(128)S(1)} %pad_add_fusion.at_ref, bf16[448,128]{1,0:T(8,128)(2,1)S(1)} %bitcast.40, bf16[448,128]{1,0:T(8,128)(2,1)S(1)} %collective-permute-done.14.d1, ...), custom_call_target="tpu_custom_call" | custom-call | flops 939524096 | bytes 4194304 | tf_op jit(solution)/shard_map/dgrad/pallas_call | solution.py:129
  12.8 1.9 %collective-permute-start.18 = (bf16[64,2048]{1,0:T(8,128)(2,1)S(1)}, bf16[64,2048]{1,0:T(8,128)(2,1)S(1)}, u32[]{:S(2)}, u32[]{:S(2)}) collective-permute-start(bf16[64,2048]{1,0:T(8,128)(2,1)S(1)} %get-tuple-element.18), channel_id=1, source_target_pairs={{0,4},{4,0},{1,5},{5,1},{2,6},{6,2},{3,7},{7,3},{8,12},{12,8},{9,1... | collective-permute-start | bytes 786440 | tf_op jit(solution)/shard_map/ppermute | solution.py:257
  14.7 4.1 %collective-permute-start = (bf16[8,2048]{1,0:T(8,128)(2,1)S(1)}, bf16[8,2048]{1,0:T(8,128)(2,1)S(1)}, u32[]{:S(2)}, u32[]{:S(2)}) collective-permute-start(bf16[8,2048]{1,0:T(8,128)(2,1)S(1)} %copy-done), channel_id=1, source_target_pairs={{0,24},{8,48},{16,40},{24,0},{32,56},{40,16},{48,8},{56,32},{1,25}... | collective-permute-start | bytes 98312 | tf_op jit(solution)/shard_map/ppermute | solution.py:262
  18.8 1.3 %collective-permute-done.refs_1_ = bf16[8,2048]{1,0:T(8,128)(2,1)S(1)} collective-permute-done((bf16[8,2048]{1,0:T(8,128)(2,1)S(1)}, bf16[8,2048]{1,0:T(8,128)(2,1)S(1)}, u32[]{:S(2)}, u32[]{:S(2)}) %collective-permute-start) | collective-permute-done | bytes 32800 | tf_op jit(solution)/shard_map/ppermute | solution.py:262
  21.4 1.3 %collective-permute-start.19 = (bf16[32,2048]{1,0:T(8,128)(2,1)S(1)}, bf16[32,2048]{1,0:T(8,128)(2,1)S(1)}, u32[]{:S(2)}, u32[]{:S(2)}) collective-permute-start(bf16[32,2048]{1,0:T(8,128)(2,1)S(1)} %get-tuple-element.25), channel_id=1, source_target_pairs={{0,64},{64,128},{128,192},{192,0},{1,65},{65,129},{129,193},{193,1... | collective-permute-start | bytes 393224 | tf_op jit(solution)/shard_map/ppermute | solution.py:257
  22.7 1.5 %collective-permute-start.21 = (bf16[32,2048]{1,0:T(8,128)(2,1)S(1)}, bf16[32,2048]{1,0:T(8,128)(2,1)S(1)}, u32[]{:S(2)}, u32[]{:S(2)}) collective-permute-start(bf16[32,2048]{1,0:T(8,128)(2,1)S(1)} %get-tuple-element.26), channel_id=1, source_target_pairs={{0,192},{64,0},{128,64},{192,128},{1,193},{65,1},{129,65},{193,129... | collective-permute-start | bytes 393224 | tf_op jit(solution)/shard_map/ppermute | solution.py:257
  26.6 2.9 %collective-permute-done.2.refs_2_ = bf16[16,2048]{1,0:T(8,128)(2,1)S(1)} collective-permute-done((bf16[16,2048]{1,0:T(8,128)(2,1)S(1)}, bf16[16,2048]{1,0:T(8,128)(2,1)S(1)}, u32[]{:S(2)}, u32[]{:S(2)}) %collective-permute-start.2) | collective-permute-done | bytes 65568 | tf_op jit(solution)/shard_map/ppermute | solution.py:257
  29.5 4.6 %collective-permute-start.4 = (bf16[64,2048]{1,0:T(8,128)(2,1)S(1)}, bf16[64,2048]{1,0:T(8,128)(2,1)S(1)}, u32[]{:S(2)}, u32[]{:S(2)}) collective-permute-start(bf16[64,2048]{1,0:T(8,128)(2,1)S(1)} %join.3.refs_0_), channel_id=1, source_target_pairs={{0,56},{8,16},{16,8},{24,32},{32,24},{40,48},{48,40},{56,0},{1,57}... | collective-permute-start | bytes 786440 | tf_op jit(solution)/shard_map/ppermute | solution.py:262
  34.6 2.4 %collective-permute-start.22 = (bf16[64,2048]{1,0:T(8,128)(2,1)S(1)}, bf16[64,2048]{1,0:T(8,128)(2,1)S(1)}, u32[]{:S(2)}, u32[]{:S(2)}) collective-permute-start(bf16[64,2048]{1,0:T(8,128)(2,1)S(1)} %get-tuple-element.24), channel_id=1, source_target_pairs={{0,192},{64,0},{128,64},{192,128},{1,193},{65,1},{129,65},{193,129... | collective-permute-start | bytes 786440 | tf_op jit(solution)/shard_map/ppermute | solution.py:257
  38.5 2.6 %collective-permute-done.20 = bf16[64,2048]{1,0:T(8,128)(2,1)S(1)} collective-permute-done((bf16[64,2048]{1,0:T(8,128)(2,1)S(1)}, bf16[64,2048]{1,0:T(8,128)(2,1)S(1)}, u32[]{:S(2)}, u32[]{:S(2)}) %collective-permute-start.20) | collective-permute-done | bytes 262176 | tf_op jit(solution)/shard_map/ppermute | solution.py:257
  41.4 4.1 %collective-permute-start.7 = (bf16[64,2048]{1,0:T(8,128)(2,1)S(1)}, bf16[64,2048]{1,0:T(8,128)(2,1)S(1)}, u32[]{:S(2)}, u32[]{:S(2)}) collective-permute-start(bf16[64,2048]{1,0:T(8,128)(2,1)S(1)} %join.3.refs_0_), channel_id=1, source_target_pairs={{0,4},{4,0},{1,5},{5,1},{2,6},{6,2},{3,7},{7,3},{8,12},{12,8},{9,1... | collective-permute-start | bytes 786440 | tf_op jit(solution)/shard_map/ppermute | solution.py:257
  45.5 4.4 %collective-permute-start.9 = (bf16[64,2048]{1,0:T(8,128)(2,1)S(1)}, bf16[64,2048]{1,0:T(8,128)(2,1)S(1)}, u32[]{:S(2)}, u32[]{:S(2)}) collective-permute-start(bf16[64,2048]{1,0:T(8,128)(2,1)S(1)} %collective-permute-done.5.refs_2_), channel_id=1, source_target_pairs={{0,4},{4,0},{1,5},{5,1},{2,6},{6,2},{3,7},{7,3},{8,12},{12,8},{9,1... | collective-permute-start | bytes 786440 | tf_op jit(solution)/shard_map/ppermute | solution.py:257
  49.9 2.9 %collective-permute-start.10 = (bf16[64,2048]{1,0:T(8,128)(2,1)S(1)}, bf16[64,2048]{1,0:T(8,128)(2,1)S(1)}, u32[]{:S(2)}, u32[]{:S(2)}) collective-permute-start(bf16[64,2048]{1,0:T(8,128)(2,1)S(1)} %collective-permute-done.6.refs_3_), channel_id=1, source_target_pairs={{0,4},{4,0},{1,5},{5,1},{2,6},{6,2},{3,7},{7,3},{8,12},{12,8},{9,1... | collective-permute-start | bytes 786440 | tf_op jit(solution)/shard_map/ppermute | solution.py:257
  52.9 1.3 %collective-permute-start.24 = (bf16[16,2048]{1,0:T(8,128)(2,1)S(1)}, bf16[16,2048]{1,0:T(8,128)(2,1)S(1)}, u32[]{:S(2)}, u32[]{:S(2)}) collective-permute-start(bf16[16,2048]{1,0:T(8,128)(2,1)S(1)} %get-tuple-element.28), channel_id=1, source_target_pairs={{0,56},{8,16},{16,8},{24,32},{32,24},{40,48},{48,40},{56,0},{1,57}... | collective-permute-start | bytes 196616 | tf_op jit(solution)/shard_map/ppermute | solution.py:262
  54.2 1.9 %forward.1 = (bf16[448,128]{1,0:T(8,128)(2,1)S(1)}, bf16[448,128]{1,0:T(8,128)(2,1)S(1)}, bf16[448,128]{1,0:T(8,128)(2,1)S(1)}, bf16[448,128]{1,0:T(8,128)(2,1)S(1)}, bf16[512,2048]{1,0:T(8,128)(2,1)S(1)}) custom-call(s32[4]{0:T(128)S(1)} %pad_add_fusion.at_ref, bf16[64,2048]{1,0:T(8,128)(2,1)S(1)} %join.3.refs_0_, ...), custom_call_target="tpu_custom_call" | custom-call | flops 939524096 | bytes 6291456 | tf_op jit(solution)/shard_map/forward/pallas_call | solution.py:186
  57.1 2.2 %collective-permute-start.12 = (bf16[448,128]{1,0:T(8,128)(2,1)S(1)}, bf16[448,128]{1,0:T(8,128)(2,1)S(1)}, u32[]{:S(2)}, u32[]{:S(2)}) collective-permute-start(bf16[448,128]{1,0:T(8,128)(2,1)S(1)} %get-tuple-element.14), channel_id=1, source_target_pairs={{0,2},{1,3},{2,0},{3,1},{4,6},{5,7},{6,4},{7,5},{8,10},{9,11},{10,... | collective-permute-start | bytes 344072 | tf_op jit(solution)/shard_map/ppermute | solution.py:257
  59.2 1.3 %collective-permute-start.13 = (bf16[448,128]{1,0:T(8,128)(2,1)S(1)}, bf16[448,128]{1,0:T(8,128)(2,1)S(1)}, u32[]{:S(2)}, u32[]{:S(2)}) collective-permute-start(bf16[448,128]{1,0:T(8,128)(2,1)S(1)} %get-tuple-element.15), channel_id=1, source_target_pairs={{0,3},{1,0},{2,1},{3,2},{4,7},{5,4},{6,5},{7,6},{8,11},{9,8},{10,9... | collective-permute-start | bytes 344072 | tf_op jit(solution)/shard_map/ppermute | solution.py:257
  60.5 1.7 %collective-permute-start.25 = (bf16[8,2048]{1,0:T(8,128)(2,1)S(1)}, bf16[8,2048]{1,0:T(8,128)(2,1)S(1)}, u32[]{:S(2)}, u32[]{:S(2)}) collective-permute-start(bf16[8,2048]{1,0:T(8,128)(2,1)S(1)} %add_convert_fusion.3), channel_id=1, source_target_pairs={{0,24},{8,48},{16,40},{24,0},{32,56},{40,16},{48,8},{56,32},{1,25}... | collective-permute-start | bytes 98312 | tf_op jit(solution)/shard_map/ppermute | solution.py:262
  62.2 2.0 %wgrad.1 = bf16[448,2048]{1,0:T(8,128)(2,1)} custom-call(bf16[512,448]{1,0:T(8,128)(2,1)S(1)} %get-tuple-element.19.dy_ref, bf16[512,2048]{1,0:T(8,128)(2,1)S(1)} %get-tuple-element.20.a_ref, s32[7,32]{1,0:T(8,128)S(1)} %bitcast.36), custom_call_target="tpu_custom_call" | custom-call | flops 939524096 | bytes 6291456 | tf_op jit(solution)/shard_map/wgrad/pallas_call | solution.py:223
  64.3 1.4 %finish.1 = bf16[448,128]{1,0:T(8,128)(2,1)} custom-call(s32[4]{0:T(128)S(1)} %pad_add_fusion.at_ref, bf16[448,128]{1,0:T(8,128)(2,1)S(1)} %get-tuple-element.12.r0, bf16[448,128]{1,0:T(8,128)(2,1)S(1)} %collective-permute-done.11.r1, bf16[448,128]{1,0:T(8,128)(2,1)S(1)} %collective-permute-done.12.r2, bf16[448,128]{1,0:T(8,128)(2,1)S(1)} %collective-permute-done.13.r3), custom_call_target="tpu_custom_call" | custom-call | flops 14680064 | bytes 1048576 | tf_op jit(solution)/shard_map/finish/pallas_call | solution.py:244
  (48 shorter events, 9.0 us)
Async XLA Ops:
  0.6 7.7 %collective-permute-start.16 = (bf16[448,128]{1,0:T(8,128)(2,1)}, bf16[448,128]{1,0:T(8,128)(2,1)S(1)}, u32[]{:S(2)}, u32[]{:S(2)}) collective-permute-start(bf16[448,128]{1,0:T(8,128)(2,1)} %bitcast.37), channel_id=1, source_target_pairs={{0,1},{1,2},{2,3},{3,0},{4,5},{5,6},{6,7},{7,4},{8,9},{9,10},{10,1... | collective-permute-start | bytes 344072 | tf_op jit(solution)/shard_map/ppermute | solution.py:257
  2.8 7.9 %collective-permute-start.15 = (bf16[448,128]{1,0:T(8,128)(2,1)}, bf16[448,128]{1,0:T(8,128)(2,1)S(1)}, u32[]{:S(2)}, u32[]{:S(2)}) collective-permute-start(bf16[448,128]{1,0:T(8,128)(2,1)} %bitcast.38), channel_id=1, source_target_pairs={{0,2},{1,3},{2,0},{3,1},{4,6},{5,7},{6,4},{7,5},{8,10},{9,11},{10,... | collective-permute-start | bytes 344072 | tf_op jit(solution)/shard_map/ppermute | solution.py:257
  5.4 5.2 %collective-permute-start.14 = (bf16[448,128]{1,0:T(8,128)(2,1)}, bf16[448,128]{1,0:T(8,128)(2,1)S(1)}, u32[]{:S(2)}, u32[]{:S(2)}) collective-permute-start(bf16[448,128]{1,0:T(8,128)(2,1)} %bitcast.39), channel_id=1, source_target_pairs={{0,3},{1,0},{2,1},{3,2},{4,7},{5,4},{6,5},{7,6},{8,11},{9,8},{10,9... | collective-permute-start | bytes 344072 | tf_op jit(solution)/shard_map/ppermute | solution.py:257
  12.8 8.6 %collective-permute-start.18 = (bf16[64,2048]{1,0:T(8,128)(2,1)S(1)}, bf16[64,2048]{1,0:T(8,128)(2,1)S(1)}, u32[]{:S(2)}, u32[]{:S(2)}) collective-permute-start(bf16[64,2048]{1,0:T(8,128)(2,1)S(1)} %get-tuple-element.18), channel_id=1, source_target_pairs={{0,4},{4,0},{1,5},{5,1},{2,6},{6,2},{3,7},{7,3},{8,12},{12,8},{9,1... | collective-permute-start | bytes 786440 | tf_op jit(solution)/shard_map/ppermute | solution.py:257
  14.6 19.5 %collective-permute-start.17 = (bf16[3,64,2048]{2,1,0:T(8,128)(2,1)S(1)}, bf16[3,64,2048]{2,1,0:T(8,128)(2,1)S(1)}, u32[]{:S(2)}, u32[]{:S(2)}) collective-permute-start(bf16[3,64,2048]{2,1,0:T(8,128)(2,1)S(1)} %get-tuple-element.17), channel_id=1, source_target_pairs={{0,4},{4,0},{1,5},{5,1},{2,6},{6,2},{3,7},{7,3},{8,12},{12,8},{9,1... | collective-permute-start | bytes 2359304 | tf_op jit(solution)/shard_map/ppermute | solution.py:257
  14.7 5.4 %collective-permute-start = (bf16[8,2048]{1,0:T(8,128)(2,1)S(1)}, bf16[8,2048]{1,0:T(8,128)(2,1)S(1)}, u32[]{:S(2)}, u32[]{:S(2)}) collective-permute-start(bf16[8,2048]{1,0:T(8,128)(2,1)S(1)} %copy-done), channel_id=1, source_target_pairs={{0,24},{8,48},{16,40},{24,0},{32,56},{40,16},{48,8},{56,32},{1,25}... | collective-permute-start | bytes 98312 | tf_op jit(solution)/shard_map/ppermute | solution.py:262
  20.1 5.3 %collective-permute-start.3 = (bf16[16,2048]{1,0:T(8,128)(2,1)S(1)}, bf16[16,2048]{1,0:T(8,128)(2,1)S(1)}, u32[]{:S(2)}, u32[]{:S(2)}) collective-permute-start(bf16[16,2048]{1,0:T(8,128)(2,1)S(1)} %join.2.refs_0_), channel_id=1, source_target_pairs={{0,64},{64,128},{128,192},{192,0},{1,65},{65,129},{129,193},{193,1... | collective-permute-start | bytes 196616 | tf_op jit(solution)/shard_map/ppermute | solution.py:257
  21.4 12.7 %collective-permute-start.19 = (bf16[32,2048]{1,0:T(8,128)(2,1)S(1)}, bf16[32,2048]{1,0:T(8,128)(2,1)S(1)}, u32[]{:S(2)}, u32[]{:S(2)}) collective-permute-start(bf16[32,2048]{1,0:T(8,128)(2,1)S(1)} %get-tuple-element.25), channel_id=1, source_target_pairs={{0,64},{64,128},{128,192},{192,0},{1,65},{65,129},{129,193},{193,1... | collective-permute-start | bytes 393224 | tf_op jit(solution)/shard_map/ppermute | solution.py:257
  22.7 11.4 %collective-permute-start.21 = (bf16[32,2048]{1,0:T(8,128)(2,1)S(1)}, bf16[32,2048]{1,0:T(8,128)(2,1)S(1)}, u32[]{:S(2)}, u32[]{:S(2)}) collective-permute-start(bf16[32,2048]{1,0:T(8,128)(2,1)S(1)} %get-tuple-element.26), channel_id=1, source_target_pairs={{0,192},{64,0},{128,64},{192,128},{1,193},{65,1},{129,65},{193,129... | collective-permute-start | bytes 393224 | tf_op jit(solution)/shard_map/ppermute | solution.py:257
  24.2 5.3 %collective-permute-start.2 = (bf16[16,2048]{1,0:T(8,128)(2,1)S(1)}, bf16[16,2048]{1,0:T(8,128)(2,1)S(1)}, u32[]{:S(2)}, u32[]{:S(2)}) collective-permute-start(bf16[16,2048]{1,0:T(8,128)(2,1)S(1)} %join.2.refs_0_), channel_id=1, source_target_pairs={{0,128},{64,192},{128,0},{192,64},{1,129},{65,193},{129,1},{193,65... | collective-permute-start | bytes 196616 | tf_op jit(solution)/shard_map/ppermute | solution.py:257
  29.5 8.3 %collective-permute-start.4 = (bf16[64,2048]{1,0:T(8,128)(2,1)S(1)}, bf16[64,2048]{1,0:T(8,128)(2,1)S(1)}, u32[]{:S(2)}, u32[]{:S(2)}) collective-permute-start(bf16[64,2048]{1,0:T(8,128)(2,1)S(1)} %join.3.refs_0_), channel_id=1, source_target_pairs={{0,56},{8,16},{16,8},{24,32},{32,24},{40,48},{48,40},{56,0},{1,57}... | collective-permute-start | bytes 786440 | tf_op jit(solution)/shard_map/ppermute | solution.py:262
  34.3 6.8 %collective-permute-start.20 = (bf16[64,2048]{1,0:T(8,128)(2,1)S(1)}, bf16[64,2048]{1,0:T(8,128)(2,1)S(1)}, u32[]{:S(2)}, u32[]{:S(2)}) collective-permute-start(bf16[64,2048]{1,0:T(8,128)(2,1)S(1)} %get-tuple-element.23), channel_id=1, source_target_pairs={{0,64},{64,128},{128,192},{192,0},{1,65},{65,129},{129,193},{193,1... | collective-permute-start | bytes 786440 | tf_op jit(solution)/shard_map/ppermute | solution.py:257
  34.6 6.5 %collective-permute-start.22 = (bf16[64,2048]{1,0:T(8,128)(2,1)S(1)}, bf16[64,2048]{1,0:T(8,128)(2,1)S(1)}, u32[]{:S(2)}, u32[]{:S(2)}) collective-permute-start(bf16[64,2048]{1,0:T(8,128)(2,1)S(1)} %get-tuple-element.24), channel_id=1, source_target_pairs={{0,192},{64,0},{128,64},{192,128},{1,193},{65,1},{129,65},{193,129... | collective-permute-start | bytes 786440 | tf_op jit(solution)/shard_map/ppermute | solution.py:257
  37.1 8.5 %collective-permute-start.5 = (bf16[64,2048]{1,0:T(8,128)(2,1)S(1)}, bf16[64,2048]{1,0:T(8,128)(2,1)S(1)}, u32[]{:S(2)}, u32[]{:S(2)}) collective-permute-start(bf16[64,2048]{1,0:T(8,128)(2,1)S(1)} %join.3.refs_0_), channel_id=1, source_target_pairs={{0,8},{8,0},{16,24},{24,16},{32,40},{40,32},{48,56},{56,48},{1,9},... | collective-permute-start | bytes 786440 | tf_op jit(solution)/shard_map/ppermute | solution.py:262
  37.9 12.0 %collective-permute-start.6 = (bf16[64,2048]{1,0:T(8,128)(2,1)S(1)}, bf16[64,2048]{1,0:T(8,128)(2,1)S(1)}, u32[]{:S(2)}, u32[]{:S(2)}) collective-permute-start(bf16[64,2048]{1,0:T(8,128)(2,1)S(1)} %collective-permute-done.4.refs_1_), channel_id=1, source_target_pairs={{0,8},{8,0},{16,24},{24,16},{32,40},{40,32},{48,56},{56,48},{1,9},... | collective-permute-start | bytes 786440 | tf_op jit(solution)/shard_map/ppermute | solution.py:262
  41.3 11.6 %collective-permute-start.23 = (bf16[32,2048]{1,0:T(8,128)(2,1)S(1)}, bf16[32,2048]{1,0:T(8,128)(2,1)S(1)}, u32[]{:S(2)}, u32[]{:S(2)}) collective-permute-start(bf16[32,2048]{1,0:T(8,128)(2,1)S(1)} %get-tuple-element.22), channel_id=1, source_target_pairs={{0,8},{8,0},{16,24},{24,16},{32,40},{40,32},{48,56},{56,48},{1,9},... | collective-permute-start | bytes 393224 | tf_op jit(solution)/shard_map/ppermute | solution.py:262
  41.4 12.8 %collective-permute-start.7 = (bf16[64,2048]{1,0:T(8,128)(2,1)S(1)}, bf16[64,2048]{1,0:T(8,128)(2,1)S(1)}, u32[]{:S(2)}, u32[]{:S(2)}) collective-permute-start(bf16[64,2048]{1,0:T(8,128)(2,1)S(1)} %join.3.refs_0_), channel_id=1, source_target_pairs={{0,4},{4,0},{1,5},{5,1},{2,6},{6,2},{3,7},{7,3},{8,12},{12,8},{9,1... | collective-permute-start | bytes 786440 | tf_op jit(solution)/shard_map/ppermute | solution.py:257
  45.4 8.7 %collective-permute-start.8 = (bf16[64,2048]{1,0:T(8,128)(2,1)S(1)}, bf16[64,2048]{1,0:T(8,128)(2,1)S(1)}, u32[]{:S(2)}, u32[]{:S(2)}) collective-permute-start(bf16[64,2048]{1,0:T(8,128)(2,1)S(1)} %collective-permute-done.4.refs_1_), channel_id=1, source_target_pairs={{0,4},{4,0},{1,5},{5,1},{2,6},{6,2},{3,7},{7,3},{8,12},{12,8},{9,1... | collective-permute-start | bytes 786440 | tf_op jit(solution)/shard_map/ppermute | solution.py:257
  45.5 8.6 %collective-permute-start.9 = (bf16[64,2048]{1,0:T(8,128)(2,1)S(1)}, bf16[64,2048]{1,0:T(8,128)(2,1)S(1)}, u32[]{:S(2)}, u32[]{:S(2)}) collective-permute-start(bf16[64,2048]{1,0:T(8,128)(2,1)S(1)} %collective-permute-done.5.refs_2_), channel_id=1, source_target_pairs={{0,4},{4,0},{1,5},{5,1},{2,6},{6,2},{3,7},{7,3},{8,12},{12,8},{9,1... | collective-permute-start | bytes 786440 | tf_op jit(solution)/shard_map/ppermute | solution.py:257
  52.9 7.6 %collective-permute-start.24 = (bf16[16,2048]{1,0:T(8,128)(2,1)S(1)}, bf16[16,2048]{1,0:T(8,128)(2,1)S(1)}, u32[]{:S(2)}, u32[]{:S(2)}) collective-permute-start(bf16[16,2048]{1,0:T(8,128)(2,1)S(1)} %get-tuple-element.28), channel_id=1, source_target_pairs={{0,56},{8,16},{16,8},{24,32},{32,24},{40,48},{48,40},{56,0},{1,57}... | collective-permute-start | bytes 196616 | tf_op jit(solution)/shard_map/ppermute | solution.py:262
  56.0 8.2 %collective-permute-start.11 = (bf16[448,128]{1,0:T(8,128)(2,1)S(1)}, bf16[448,128]{1,0:T(8,128)(2,1)S(1)}, u32[]{:S(2)}, u32[]{:S(2)}) collective-permute-start(bf16[448,128]{1,0:T(8,128)(2,1)S(1)} %get-tuple-element.13), channel_id=1, source_target_pairs={{0,1},{1,2},{2,3},{3,0},{4,5},{5,6},{6,7},{7,4},{8,9},{9,10},{10,1... | collective-permute-start | bytes 344072 | tf_op jit(solution)/shard_map/ppermute | solution.py:257
  57.1 7.2 %collective-permute-start.12 = (bf16[448,128]{1,0:T(8,128)(2,1)S(1)}, bf16[448,128]{1,0:T(8,128)(2,1)S(1)}, u32[]{:S(2)}, u32[]{:S(2)}) collective-permute-start(bf16[448,128]{1,0:T(8,128)(2,1)S(1)} %get-tuple-element.14), channel_id=1, source_target_pairs={{0,2},{1,3},{2,0},{3,1},{4,6},{5,7},{6,4},{7,5},{8,10},{9,11},{10,... | collective-permute-start | bytes 344072 | tf_op jit(solution)/shard_map/ppermute | solution.py:257
  59.2 5.0 %collective-permute-start.13 = (bf16[448,128]{1,0:T(8,128)(2,1)S(1)}, bf16[448,128]{1,0:T(8,128)(2,1)S(1)}, u32[]{:S(2)}, u32[]{:S(2)}) collective-permute-start(bf16[448,128]{1,0:T(8,128)(2,1)S(1)} %get-tuple-element.15), channel_id=1, source_target_pairs={{0,3},{1,0},{2,1},{3,2},{4,7},{5,4},{6,5},{7,6},{8,11},{9,8},{10,9... | collective-permute-start | bytes 344072 | tf_op jit(solution)/shard_map/ppermute | solution.py:257
  60.5 5.2 %collective-permute-start.25 = (bf16[8,2048]{1,0:T(8,128)(2,1)S(1)}, bf16[8,2048]{1,0:T(8,128)(2,1)S(1)}, u32[]{:S(2)}, u32[]{:S(2)}) collective-permute-start(bf16[8,2048]{1,0:T(8,128)(2,1)S(1)} %add_convert_fusion.3), channel_id=1, source_target_pairs={{0,24},{8,48},{16,40},{24,0},{32,56},{40,16},{48,8},{56,32},{1,25}... | collective-permute-start | bytes 98312 | tf_op jit(solution)/shard_map/ppermute | solution.py:262
  (5 other events, 28.4 us)

commit v7 on v6

--- a/solution.py
+++ b/solution.py
@@ -292,17 +292,16 @@
     up_own = across(own, STEPS[2])
     up_side = across(side, STEPS[2])
     pieces = own, side, up_own, up_side
-    swapped = [to(piece, "core", 1) for piece in pieces[:3]]
+    swapped = [to(own, "core", 1)]
+    swapped += [to(piece, "core", 1) for piece in pieces[1:3]]
     swapped.append(to(up_side, "core", 1))
-    low, high = halved(keep[2], got_far)
-    ahead = to(low, "x", 1)
-    behind = to(high, "x", -1)
-    none = jnp.zeros_like(ahead)
-    right = added(keep[1], got[1], jnp.concatenate([ahead, none]))
-    left = added(keep[3], got[2], jnp.concatenate([none, behind]))
-    right = to(right, "x", 1)
-    left = to(left, "x", -1)
-    rest, away = halved(keep[0], got[0], right, left)
+    second = added(keep[2], got_far)
+    behind = to(second, "x", -1)
+    first = added(keep[1], got[1])
+    direct = to(first, "x", 1)
+    third = added(keep[3], got[2], behind)
+    relayed = to(third, "x", -1)
+    rest, away = halved(keep[0], got[0], direct, relayed)
     came = across(away, STEPS[2])
     rest, away = halved(rest, came)
     came = across(away, STEPS[1])
@@ -311,7 +310,8 @@
     input_grad = added(rest, came)
 
     o0, o1, o2, o3, full = forward(at, (*pieces, *swapped), masked)
-    parts = (o0, to(o1, "narrow", 1), to(o2, "narrow", 2), to(o3, "narrow", -1))
+    far_out = to(o2, "narrow", 2)
+    parts = (o0, to(o1, "narrow", 1), far_out, to(o3, "narrow", -1))
     output = finish(at, parts).T
     weight_grad = wgrad(dy, full, mt).T
     return (output, input_grad, weight_grad)

time: 67.6 us -> 71.6 us (1.059)
  starting transfers between devices: 45.3 us -> 47.9 us
  waiting for transfers between devices: 10.1 us -> 11.6 us
    ppermute x19 -> x18, starting transfers between devices: 32.8 us -> 35.4 us  [to(): return lax.ppermute(array, axis, [(i, (i + step) % n) for i in range(n)])]
    ppermute x19 -> x18, waiting for transfers between devices: 7.97 us -> 10.3 us  [to(): return lax.ppermute(array, axis, [(i, (i + step) % n) for i in range(n)])]
    ppermute x7, waiting for transfers between devices: 2.13 us -> 1.32 us  [across(): lax.ppermute(array, 'z', [(i, (i - step if i % 2 else i + step) % n) for...]
  transfers between devices with their start and end apart: 26 -> 25, of which waited for: 5 -> 7; matrix products, arithmetic and copies ran while one was open for 1% -> 1% of each run, Pallas kernels for 10% -> 10%
where the time goes in v7:
time: 71.6 us; the launch traced here: 70.5 us
  starting transfers between devices  47.9 us (67%)
  waiting for transfers between devices  11.6 us (16%)
  Pallas kernels  9.01 us (13%)
  other arithmetic  1.12 us (2%)
  between operations  0.77 us (1%)
    ppermute x18, starting transfers between devices, to(): return lax.ppermute(array, axis, [(i, (i + step) % n) for i in range(n)])  35.4 us
    ppermute x7, starting transfers between devices, across(): lax.ppermute(array, 'z', [(i, (i - step if i % 2 else i + step) % n) for...  12.6 us
    ppermute x18, waiting for transfers between devices, to(): return lax.ppermute(array, axis, [(i, (i + step) % n) for i in range(n)])  10.3 us
    pallas_call x1, Pallas kernels, dgrad(): pl.pallas_call(dgrad_kernel, out_shape=(shaped(4, half, cols), shaped(hal...  2.06 us
    pallas_call x1, Pallas kernels, wgrad(): pl.pallas_call(wgrad_kernel, out_shape=shaped(hidden, cols), in_specs=[VM...  1.97 us
    pallas_call x1, Pallas kernels, forward(): pl.pallas_call(fwd_kernel, out_shape=(out,) * 4 + (shaped(8 * rows, cols)...  1.86 us
    pallas_call x1, Pallas kernels, masked_weight(): pl.pallas_call(mask_kernel, out_shape=shaped(hidden, cols), in_specs=[HBM...  1.67 us
  transfers between devices with their start and end apart: 25, of which 7 were waited for; matrix products, arithmetic and copies ran while one was open for 1% of the time, Pallas kernels for 10%

profile of v7, /device:TPU:1, one launch (start us, length us, event | category | flops | bytes accessed | tf_op | source)
XLA Modules:
  0.0 70.5 jit_solution(3481675038580885190)
XLA Ops:
  0.6 2.2 %collective-permute-start.16 = (bf16[448,128]{1,0:T(8,128)(2,1)}, bf16[448,128]{1,0:T(8,128)(2,1)S(1)}, u32[]{:S(2)}, u32[]{:S(2)}) collective-permute-start(bf16[448,128]{1,0:T(8,128)(2,1)} %bitcast.32), channel_id=1, source_target_pairs={{0,1},{1,2},{2,3},{3,0},{4,5},{5,6},{6,7},{7,4},{8,9},{9,10},{10,1... | collective-permute-start | bytes 344072 | tf_op jit(solution)/shard_map/ppermute | solution.py:257
  2.8 2.6 %collective-permute-start.15 = (bf16[448,128]{1,0:T(8,128)(2,1)}, bf16[448,128]{1,0:T(8,128)(2,1)S(1)}, u32[]{:S(2)}, u32[]{:S(2)}) collective-permute-start(bf16[448,128]{1,0:T(8,128)(2,1)} %bitcast.33), channel_id=1, source_target_pairs={{0,2},{1,3},{2,0},{3,1},{4,6},{5,7},{6,4},{7,5},{8,10},{9,11},{10,... | collective-permute-start | bytes 344072 | tf_op jit(solution)/shard_map/ppermute | solution.py:257
  6.5 1.7 %mask_weight.1.refs_8_.w_ref = bf16[448,2048]{1,0:T(8,128)(2,1)S(1)} custom-call(s32[7,32]{1,0:T(8,128)} %bitcast.30, bf16[448,2048]{1,0:T(8,128)(2,1)} %bitcast.37), custom_call_target="tpu_custom_call" | custom-call | flops 1835008 | bytes 4194304 | tf_op jit(solution)/shard_map/mask_weight/pallas_call | solution.py:82
  8.3 2.4 %collective-permute-done.15.d2 = bf16[448,128]{1,0:T(8,128)(2,1)S(1)} collective-permute-done((bf16[448,128]{1,0:T(8,128)(2,1)}, bf16[448,128]{1,0:T(8,128)(2,1)S(1)}, u32[]{:S(2)}, u32[]{:S(2)}) %collective-permute-start.15) | collective-permute-done | bytes 114720 | tf_op jit(solution)/shard_map/ppermute | solution.py:257
  10.7 2.1 %dgrad.1 = (bf16[4,64,2048]{2,1,0:T(8,128)(2,1)S(1)}, bf16[64,2048]{1,0:T(8,128)(2,1)S(1)}, bf16[3,64,2048]{2,1,0:T(8,128)(2,1)S(1)}, bf16[512,448]{1,0:T(8,128)(2,1)S(1)}) custom-call(s32[4]{0:T(128)S(1)} %pad_add_fusion.at_ref, bf16[448,128]{1,0:T(8,128)(2,1)S(1)} %bitcast.35, bf16[448,128]{1,0:T(8,128)(2,1)S(1)} %collective-permute-done.14.d1, ...), custom_call_target="tpu_custom_call" | custom-call | flops 939524096 | bytes 4194304 | tf_op jit(solution)/shard_map/dgrad/pallas_call | solution.py:129
  12.8 1.9 %collective-permute-start.17 = (bf16[3,64,2048]{2,1,0:T(8,128)(2,1)S(1)}, bf16[3,64,2048]{2,1,0:T(8,128)(2,1)S(1)}, u32[]{:S(2)}, u32[]{:S(2)}) collective-permute-start(bf16[3,64,2048]{2,1,0:T(8,128)(2,1)S(1)} %get-tuple-element.17), channel_id=1, source_target_pairs={{0,4},{4,0},{1,5},{5,1},{2,6},{6,2},{3,7},{7,3},{8,12},{12,8},{9,1... | collective-permute-start | bytes 2359304 | tf_op jit(solution)/shard_map/ppermute | solution.py:257
  14.7 4.1 %collective-permute-start = (bf16[8,2048]{1,0:T(8,128)(2,1)S(1)}, bf16[8,2048]{1,0:T(8,128)(2,1)S(1)}, u32[]{:S(2)}, u32[]{:S(2)}) collective-permute-start(bf16[8,2048]{1,0:T(8,128)(2,1)S(1)} %copy-done), channel_id=1, source_target_pairs={{0,24},{8,48},{16,40},{24,0},{32,56},{40,16},{48,8},{56,32},{1,25}... | collective-permute-start | bytes 98312 | tf_op jit(solution)/shard_map/ppermute | solution.py:262
  18.8 1.3 %collective-permute-done.refs_1_ = bf16[8,2048]{1,0:T(8,128)(2,1)S(1)} collective-permute-done((bf16[8,2048]{1,0:T(8,128)(2,1)S(1)}, bf16[8,2048]{1,0:T(8,128)(2,1)S(1)}, u32[]{:S(2)}, u32[]{:S(2)}) %collective-permute-start) | collective-permute-done | bytes 32800 | tf_op jit(solution)/shard_map/ppermute | solution.py:262
  21.3 2.5 %collective-permute-start.2 = (bf16[16,2048]{1,0:T(8,128)(2,1)S(1)}, bf16[16,2048]{1,0:T(8,128)(2,1)S(1)}, u32[]{:S(2)}, u32[]{:S(2)}) collective-permute-start(bf16[16,2048]{1,0:T(8,128)(2,1)S(1)} %join.2.refs_0_), channel_id=1, source_target_pairs={{0,128},{64,192},{128,0},{192,64},{1,129},{65,193},{129,1},{193,65... | collective-permute-start | bytes 196616 | tf_op jit(solution)/shard_map/ppermute | solution.py:257
  26.2 1.5 %collective-permute-done.1.refs_1_ = bf16[16,2048]{1,0:T(8,128)(2,1)S(1)} collective-permute-done((bf16[16,2048]{1,0:T(8,128)(2,1)S(1)}, bf16[16,2048]{1,0:T(8,128)(2,1)S(1)}, u32[]{:S(2)}, u32[]{:S(2)}) %collective-permute-start.1) | collective-permute-done | bytes 65568 | tf_op jit(solution)/shard_map/ppermute | solution.py:257
  27.8 4.0 %collective-permute-start.4 = (bf16[64,2048]{1,0:T(8,128)(2,1)S(1)}, bf16[64,2048]{1,0:T(8,128)(2,1)S(1)}, u32[]{:S(2)}, u32[]{:S(2)}) collective-permute-start(bf16[64,2048]{1,0:T(8,128)(2,1)S(1)} %join.3.refs_0_), channel_id=1, source_target_pairs={{0,56},{8,16},{16,8},{24,32},{32,24},{40,48},{48,40},{56,0},{1,57}... | collective-permute-start | bytes 786440 | tf_op jit(solution)/shard_map/ppermute | solution.py:262
  31.9 2.7 %collective-permute-start.20 = (bf16[64,2048]{1,0:T(8,128)(2,1)S(1)}, bf16[64,2048]{1,0:T(8,128)(2,1)S(1)}, u32[]{:S(2)}, u32[]{:S(2)}) collective-permute-start(bf16[64,2048]{1,0:T(8,128)(2,1)S(1)} %fusion), channel_id=1, source_target_pairs={{0,192},{64,0},{128,64},{192,128},{1,193},{65,1},{129,65},{193,129... | collective-permute-start | bytes 786440 | tf_op jit(solution)/shard_map/ppermute | solution.py:257
  34.7 3.2 %collective-permute-done.20 = bf16[64,2048]{1,0:T(8,128)(2,1)S(1)} collective-permute-done((bf16[64,2048]{1,0:T(8,128)(2,1)S(1)}, bf16[64,2048]{1,0:T(8,128)(2,1)S(1)}, u32[]{:S(2)}, u32[]{:S(2)}) %collective-permute-start.20) | collective-permute-done | bytes 262176 | tf_op jit(solution)/shard_map/ppermute | solution.py:257
  38.0 3.5 %collective-permute-start.21 = (bf16[64,2048]{1,0:T(8,128)(2,1)S(1)}, bf16[64,2048]{1,0:T(8,128)(2,1)S(1)}, u32[]{:S(2)}, u32[]{:S(2)}) collective-permute-start(bf16[64,2048]{1,0:T(8,128)(2,1)S(1)} %fusion.1), channel_id=1, source_target_pairs={{0,192},{64,0},{128,64},{192,128},{1,193},{65,1},{129,65},{193,129... | collective-permute-start | bytes 786440 | tf_op jit(solution)/shard_map/ppermute | solution.py:257
  41.5 1.5 %collective-permute-start.6 = (bf16[64,2048]{1,0:T(8,128)(2,1)S(1)}, bf16[64,2048]{1,0:T(8,128)(2,1)S(1)}, u32[]{:S(2)}, u32[]{:S(2)}) collective-permute-start(bf16[64,2048]{1,0:T(8,128)(2,1)S(1)} %collective-permute-done.4.refs_1_), channel_id=1, source_target_pairs={{0,8},{8,0},{16,24},{24,16},{32,40},{40,32},{48,56},{56,48},{1,9},... | collective-permute-start | bytes 786440 | tf_op jit(solution)/shard_map/ppermute | solution.py:262
  42.9 1.8 %collective-permute-done.21 = bf16[64,2048]{1,0:T(8,128)(2,1)S(1)} collective-permute-done((bf16[64,2048]{1,0:T(8,128)(2,1)S(1)}, bf16[64,2048]{1,0:T(8,128)(2,1)S(1)}, u32[]{:S(2)}, u32[]{:S(2)}) %collective-permute-start.21) | collective-permute-done | bytes 262176 | tf_op jit(solution)/shard_map/ppermute | solution.py:257
  45.2 4.8 %collective-permute-start.7 = (bf16[64,2048]{1,0:T(8,128)(2,1)S(1)}, bf16[64,2048]{1,0:T(8,128)(2,1)S(1)}, u32[]{:S(2)}, u32[]{:S(2)}) collective-permute-start(bf16[64,2048]{1,0:T(8,128)(2,1)S(1)} %join.3.refs_0_), channel_id=1, source_target_pairs={{0,4},{4,0},{1,5},{5,1},{2,6},{6,2},{3,7},{7,3},{8,12},{12,8},{9,1... | collective-permute-start | bytes 786440 | tf_op jit(solution)/shard_map/ppermute | solution.py:257
  50.1 4.3 %collective-permute-start.9 = (bf16[64,2048]{1,0:T(8,128)(2,1)S(1)}, bf16[64,2048]{1,0:T(8,128)(2,1)S(1)}, u32[]{:S(2)}, u32[]{:S(2)}) collective-permute-start(bf16[64,2048]{1,0:T(8,128)(2,1)S(1)} %collective-permute-done.5.refs_2_), channel_id=1, source_target_pairs={{0,4},{4,0},{1,5},{5,1},{2,6},{6,2},{3,7},{7,3},{8,12},{12,8},{9,1... | collective-permute-start | bytes 786440 | tf_op jit(solution)/shard_map/ppermute | solution.py:257
  54.4 2.8 %collective-permute-start.10 = (bf16[64,2048]{1,0:T(8,128)(2,1)S(1)}, bf16[64,2048]{1,0:T(8,128)(2,1)S(1)}, u32[]{:S(2)}, u32[]{:S(2)}) collective-permute-start(bf16[64,2048]{1,0:T(8,128)(2,1)S(1)} %collective-permute-done.6.refs_3_), channel_id=1, source_target_pairs={{0,4},{4,0},{1,5},{5,1},{2,6},{6,2},{3,7},{7,3},{8,12},{12,8},{9,1... | collective-permute-start | bytes 786440 | tf_op jit(solution)/shard_map/ppermute | solution.py:257
  58.4 1.9 %forward.1 = (bf16[448,128]{1,0:T(8,128)(2,1)S(1)}, bf16[448,128]{1,0:T(8,128)(2,1)S(1)}, bf16[448,128]{1,0:T(8,128)(2,1)S(1)}, bf16[448,128]{1,0:T(8,128)(2,1)S(1)}, bf16[512,2048]{1,0:T(8,128)(2,1)S(1)}) custom-call(s32[4]{0:T(128)S(1)} %pad_add_fusion.at_ref, bf16[64,2048]{1,0:T(8,128)(2,1)S(1)} %join.3.refs_0_, ...), custom_call_target="tpu_custom_call" | custom-call | flops 939524096 | bytes 6291456 | tf_op jit(solution)/shard_map/forward/pallas_call | solution.py:186
  61.3 2.2 %collective-permute-start.12 = (bf16[448,128]{1,0:T(8,128)(2,1)S(1)}, bf16[448,128]{1,0:T(8,128)(2,1)S(1)}, u32[]{:S(2)}, u32[]{:S(2)}) collective-permute-start(bf16[448,128]{1,0:T(8,128)(2,1)S(1)} %get-tuple-element.14), channel_id=1, source_target_pairs={{0,2},{1,3},{2,0},{3,1},{4,6},{5,7},{6,4},{7,5},{8,10},{9,11},{10,... | collective-permute-start | bytes 344072 | tf_op jit(solution)/shard_map/ppermute | solution.py:257
  64.7 1.7 %collective-permute-start.24 = (bf16[8,2048]{1,0:T(8,128)(2,1)S(1)}, bf16[8,2048]{1,0:T(8,128)(2,1)S(1)}, u32[]{:S(2)}, u32[]{:S(2)}) collective-permute-start(bf16[8,2048]{1,0:T(8,128)(2,1)S(1)} %add_convert_fusion.4), channel_id=1, source_target_pairs={{0,24},{8,48},{16,40},{24,0},{32,56},{40,16},{48,8},{56,32},{1,25}... | collective-permute-start | bytes 98312 | tf_op jit(solution)/shard_map/ppermute | solution.py:262
  66.4 2.0 %wgrad.1 = bf16[448,2048]{1,0:T(8,128)(2,1)} custom-call(bf16[512,448]{1,0:T(8,128)(2,1)S(1)} %get-tuple-element.19.dy_ref, bf16[512,2048]{1,0:T(8,128)(2,1)S(1)} %get-tuple-element.20.a_ref, s32[7,32]{1,0:T(8,128)S(1)} %bitcast.31), custom_call_target="tpu_custom_call" | custom-call | flops 939524096 | bytes 6291456 | tf_op jit(solution)/shard_map/wgrad/pallas_call | solution.py:223
  68.4 1.4 %finish.1 = bf16[448,128]{1,0:T(8,128)(2,1)} custom-call(s32[4]{0:T(128)S(1)} %pad_add_fusion.at_ref, bf16[448,128]{1,0:T(8,128)(2,1)S(1)} %get-tuple-element.12.r0, bf16[448,128]{1,0:T(8,128)(2,1)S(1)} %collective-permute-done.11.r1, bf16[448,128]{1,0:T(8,128)(2,1)S(1)} %collective-permute-done.12.r2, bf16[448,128]{1,0:T(8,128)(2,1)S(1)} %collective-permute-done.13.r3), custom_call_target="tpu_custom_call" | custom-call | flops 14680064 | bytes 1048576 | tf_op jit(solution)/shard_map/finish/pallas_call | solution.py:244
  (47 shorter events, 9.8 us)
Async XLA Ops:
  0.6 7.7 %collective-permute-start.16 = (bf16[448,128]{1,0:T(8,128)(2,1)}, bf16[448,128]{1,0:T(8,128)(2,1)S(1)}, u32[]{:S(2)}, u32[]{:S(2)}) collective-permute-start(bf16[448,128]{1,0:T(8,128)(2,1)} %bitcast.32), channel_id=1, source_target_pairs={{0,1},{1,2},{2,3},{3,0},{4,5},{5,6},{6,7},{7,4},{8,9},{9,10},{10,1... | collective-permute-start | bytes 344072 | tf_op jit(solution)/shard_map/ppermute | solution.py:257
  2.8 7.9 %collective-permute-start.15 = (bf16[448,128]{1,0:T(8,128)(2,1)}, bf16[448,128]{1,0:T(8,128)(2,1)S(1)}, u32[]{:S(2)}, u32[]{:S(2)}) collective-permute-start(bf16[448,128]{1,0:T(8,128)(2,1)} %bitcast.33), channel_id=1, source_target_pairs={{0,2},{1,3},{2,0},{3,1},{4,6},{5,7},{6,4},{7,5},{8,10},{9,11},{10,... | collective-permute-start | bytes 344072 | tf_op jit(solution)/shard_map/ppermute | solution.py:257
  5.4 5.2 %collective-permute-start.14 = (bf16[448,128]{1,0:T(8,128)(2,1)}, bf16[448,128]{1,0:T(8,128)(2,1)S(1)}, u32[]{:S(2)}, u32[]{:S(2)}) collective-permute-start(bf16[448,128]{1,0:T(8,128)(2,1)} %bitcast.34), channel_id=1, source_target_pairs={{0,3},{1,0},{2,1},{3,2},{4,7},{5,4},{6,5},{7,6},{8,11},{9,8},{10,9... | collective-permute-start | bytes 344072 | tf_op jit(solution)/shard_map/ppermute | solution.py:257
  12.8 21.8 %collective-permute-start.17 = (bf16[3,64,2048]{2,1,0:T(8,128)(2,1)S(1)}, bf16[3,64,2048]{2,1,0:T(8,128)(2,1)S(1)}, u32[]{:S(2)}, u32[]{:S(2)}) collective-permute-start(bf16[3,64,2048]{2,1,0:T(8,128)(2,1)S(1)} %get-tuple-element.17), channel_id=1, source_target_pairs={{0,4},{4,0},{1,5},{5,1},{2,6},{6,2},{3,7},{7,3},{8,12},{12,8},{9,1... | collective-permute-start | bytes 2359304 | tf_op jit(solution)/shard_map/ppermute | solution.py:257
  14.6 17.2 %collective-permute-start.19 = (bf16[64,2048]{1,0:T(8,128)(2,1)S(1)}, bf16[64,2048]{1,0:T(8,128)(2,1)S(1)}, u32[]{:S(2)}, u32[]{:S(2)}) collective-permute-start(bf16[64,2048]{1,0:T(8,128)(2,1)S(1)} %get-tuple-element.18), channel_id=1, source_target_pairs={{0,4},{4,0},{1,5},{5,1},{2,6},{6,2},{3,7},{7,3},{8,12},{12,8},{9,1... | collective-permute-start | bytes 786440 | tf_op jit(solution)/shard_map/ppermute | solution.py:257
  14.7 5.4 %collective-permute-start = (bf16[8,2048]{1,0:T(8,128)(2,1)S(1)}, bf16[8,2048]{1,0:T(8,128)(2,1)S(1)}, u32[]{:S(2)}, u32[]{:S(2)}) collective-permute-start(bf16[8,2048]{1,0:T(8,128)(2,1)S(1)} %copy-done), channel_id=1, source_target_pairs={{0,24},{8,48},{16,40},{24,0},{32,56},{40,16},{48,8},{56,32},{1,25}... | collective-permute-start | bytes 98312 | tf_op jit(solution)/shard_map/ppermute | solution.py:262
  20.1 4.8 %collective-permute-start.3 = (bf16[16,2048]{1,0:T(8,128)(2,1)S(1)}, bf16[16,2048]{1,0:T(8,128)(2,1)S(1)}, u32[]{:S(2)}, u32[]{:S(2)}) collective-permute-start(bf16[16,2048]{1,0:T(8,128)(2,1)S(1)} %join.2.refs_0_), channel_id=1, source_target_pairs={{0,64},{64,128},{128,192},{192,0},{1,65},{65,129},{129,193},{193,1... | collective-permute-start | bytes 196616 | tf_op jit(solution)/shard_map/ppermute | solution.py:257
  21.3 4.9 %collective-permute-start.2 = (bf16[16,2048]{1,0:T(8,128)(2,1)S(1)}, bf16[16,2048]{1,0:T(8,128)(2,1)S(1)}, u32[]{:S(2)}, u32[]{:S(2)}) collective-permute-start(bf16[16,2048]{1,0:T(8,128)(2,1)S(1)} %join.2.refs_0_), channel_id=1, source_target_pairs={{0,128},{64,192},{128,0},{192,64},{1,129},{65,193},{129,1},{193,65... | collective-permute-start | bytes 196616 | tf_op jit(solution)/shard_map/ppermute | solution.py:257
  23.8 4.0 %collective-permute-start.1 = (bf16[16,2048]{1,0:T(8,128)(2,1)S(1)}, bf16[16,2048]{1,0:T(8,128)(2,1)S(1)}, u32[]{:S(2)}, u32[]{:S(2)}) collective-permute-start(bf16[16,2048]{1,0:T(8,128)(2,1)S(1)} %join.2.refs_0_), channel_id=1, source_target_pairs={{0,192},{64,0},{128,64},{192,128},{1,193},{65,1},{129,65},{193,129... | collective-permute-start | bytes 196616 | tf_op jit(solution)/shard_map/ppermute | solution.py:257
  27.8 13.7 %collective-permute-start.4 = (bf16[64,2048]{1,0:T(8,128)(2,1)S(1)}, bf16[64,2048]{1,0:T(8,128)(2,1)S(1)}, u32[]{:S(2)}, u32[]{:S(2)}) collective-permute-start(bf16[64,2048]{1,0:T(8,128)(2,1)S(1)} %join.3.refs_0_), channel_id=1, source_target_pairs={{0,56},{8,16},{16,8},{24,32},{32,24},{40,48},{48,40},{56,0},{1,57}... | collective-permute-start | bytes 786440 | tf_op jit(solution)/shard_map/ppermute | solution.py:262
  31.9 6.0 %collective-permute-start.20 = (bf16[64,2048]{1,0:T(8,128)(2,1)S(1)}, bf16[64,2048]{1,0:T(8,128)(2,1)S(1)}, u32[]{:S(2)}, u32[]{:S(2)}) collective-permute-start(bf16[64,2048]{1,0:T(8,128)(2,1)S(1)} %fusion), channel_id=1, source_target_pairs={{0,192},{64,0},{128,64},{192,128},{1,193},{65,1},{129,65},{193,129... | collective-permute-start | bytes 786440 | tf_op jit(solution)/shard_map/ppermute | solution.py:257
  34.6 8.3 %collective-permute-start.18 = (bf16[64,2048]{1,0:T(8,128)(2,1)S(1)}, bf16[64,2048]{1,0:T(8,128)(2,1)S(1)}, u32[]{:S(2)}, u32[]{:S(2)}) collective-permute-start(bf16[64,2048]{1,0:T(8,128)(2,1)S(1)} %fusion.2), channel_id=1, source_target_pairs={{0,64},{64,128},{128,192},{192,0},{1,65},{65,129},{129,193},{193,1... | collective-permute-start | bytes 786440 | tf_op jit(solution)/shard_map/ppermute | solution.py:257
  38.0 6.8 %collective-permute-start.21 = (bf16[64,2048]{1,0:T(8,128)(2,1)S(1)}, bf16[64,2048]{1,0:T(8,128)(2,1)S(1)}, u32[]{:S(2)}, u32[]{:S(2)}) collective-permute-start(bf16[64,2048]{1,0:T(8,128)(2,1)S(1)} %fusion.1), channel_id=1, source_target_pairs={{0,192},{64,0},{128,64},{192,128},{1,193},{65,1},{129,65},{193,129... | collective-permute-start | bytes 786440 | tf_op jit(solution)/shard_map/ppermute | solution.py:257
  41.5 8.6 %collective-permute-start.5 = (bf16[64,2048]{1,0:T(8,128)(2,1)S(1)}, bf16[64,2048]{1,0:T(8,128)(2,1)S(1)}, u32[]{:S(2)}, u32[]{:S(2)}) collective-permute-start(bf16[64,2048]{1,0:T(8,128)(2,1)S(1)} %join.3.refs_0_), channel_id=1, source_target_pairs={{0,8},{8,0},{16,24},{24,16},{32,40},{40,32},{48,56},{56,48},{1,9},... | collective-permute-start | bytes 786440 | tf_op jit(solution)/shard_map/ppermute | solution.py:262
  41.5 12.9 %collective-permute-start.6 = (bf16[64,2048]{1,0:T(8,128)(2,1)S(1)}, bf16[64,2048]{1,0:T(8,128)(2,1)S(1)}, u32[]{:S(2)}, u32[]{:S(2)}) collective-permute-start(bf16[64,2048]{1,0:T(8,128)(2,1)S(1)} %collective-permute-done.4.refs_1_), channel_id=1, source_target_pairs={{0,8},{8,0},{16,24},{24,16},{32,40},{40,32},{48,56},{56,48},{1,9},... | collective-permute-start | bytes 786440 | tf_op jit(solution)/shard_map/ppermute | solution.py:262
  44.9 12.3 %collective-permute-start.22 = (bf16[32,2048]{1,0:T(8,128)(2,1)S(1)}, bf16[32,2048]{1,0:T(8,128)(2,1)S(1)}, u32[]{:S(2)}, u32[]{:S(2)}) collective-permute-start(bf16[32,2048]{1,0:T(8,128)(2,1)S(1)} %get-tuple-element.22), channel_id=1, source_target_pairs={{0,8},{8,0},{16,24},{24,16},{32,40},{40,32},{48,56},{56,48},{1,9},... | collective-permute-start | bytes 393224 | tf_op jit(solution)/shard_map/ppermute | solution.py:262
  45.2 13.1 %collective-permute-start.7 = (bf16[64,2048]{1,0:T(8,128)(2,1)S(1)}, bf16[64,2048]{1,0:T(8,128)(2,1)S(1)}, u32[]{:S(2)}, u32[]{:S(2)}) collective-permute-start(bf16[64,2048]{1,0:T(8,128)(2,1)S(1)} %join.3.refs_0_), channel_id=1, source_target_pairs={{0,4},{4,0},{1,5},{5,1},{2,6},{6,2},{3,7},{7,3},{8,12},{12,8},{9,1... | collective-permute-start | bytes 786440 | tf_op jit(solution)/shard_map/ppermute | solution.py:257
  50.0 8.3 %collective-permute-start.8 = (bf16[64,2048]{1,0:T(8,128)(2,1)S(1)}, bf16[64,2048]{1,0:T(8,128)(2,1)S(1)}, u32[]{:S(2)}, u32[]{:S(2)}) collective-permute-start(bf16[64,2048]{1,0:T(8,128)(2,1)S(1)} %collective-permute-done.4.refs_1_), channel_id=1, source_target_pairs={{0,4},{4,0},{1,5},{5,1},{2,6},{6,2},{3,7},{7,3},{8,12},{12,8},{9,1... | collective-permute-start | bytes 786440 | tf_op jit(solution)/shard_map/ppermute | solution.py:257
  50.1 8.2 %collective-permute-start.9 = (bf16[64,2048]{1,0:T(8,128)(2,1)S(1)}, bf16[64,2048]{1,0:T(8,128)(2,1)S(1)}, u32[]{:S(2)}, u32[]{:S(2)}) collective-permute-start(bf16[64,2048]{1,0:T(8,128)(2,1)S(1)} %collective-permute-done.5.refs_2_), channel_id=1, source_target_pairs={{0,4},{4,0},{1,5},{5,1},{2,6},{6,2},{3,7},{7,3},{8,12},{12,8},{9,1... | collective-permute-start | bytes 786440 | tf_op jit(solution)/shard_map/ppermute | solution.py:257
  57.3 7.4 %collective-permute-start.23 = (bf16[16,2048]{1,0:T(8,128)(2,1)S(1)}, bf16[16,2048]{1,0:T(8,128)(2,1)S(1)}, u32[]{:S(2)}, u32[]{:S(2)}) collective-permute-start(bf16[16,2048]{1,0:T(8,128)(2,1)S(1)} %get-tuple-element.24), channel_id=1, source_target_pairs={{0,56},{8,16},{16,8},{24,32},{32,24},{40,48},{48,40},{56,0},{1,57}... | collective-permute-start | bytes 196616 | tf_op jit(solution)/shard_map/ppermute | solution.py:262
  60.2 8.2 %collective-permute-start.11 = (bf16[448,128]{1,0:T(8,128)(2,1)S(1)}, bf16[448,128]{1,0:T(8,128)(2,1)S(1)}, u32[]{:S(2)}, u32[]{:S(2)}) collective-permute-start(bf16[448,128]{1,0:T(8,128)(2,1)S(1)} %get-tuple-element.13), channel_id=1, source_target_pairs={{0,1},{1,2},{2,3},{3,0},{4,5},{5,6},{6,7},{7,4},{8,9},{9,10},{10,1... | collective-permute-start | bytes 344072 | tf_op jit(solution)/shard_map/ppermute | solution.py:257
  61.3 7.1 %collective-permute-start.12 = (bf16[448,128]{1,0:T(8,128)(2,1)S(1)}, bf16[448,128]{1,0:T(8,128)(2,1)S(1)}, u32[]{:S(2)}, u32[]{:S(2)}) collective-permute-start(bf16[448,128]{1,0:T(8,128)(2,1)S(1)} %get-tuple-element.14), channel_id=1, source_target_pairs={{0,2},{1,3},{2,0},{3,1},{4,6},{5,7},{6,4},{7,5},{8,10},{9,11},{10,... | collective-permute-start | bytes 344072 | tf_op jit(solution)/shard_map/ppermute | solution.py:257
  63.4 5.0 %collective-permute-start.13 = (bf16[448,128]{1,0:T(8,128)(2,1)S(1)}, bf16[448,128]{1,0:T(8,128)(2,1)S(1)}, u32[]{:S(2)}, u32[]{:S(2)}) collective-permute-start(bf16[448,128]{1,0:T(8,128)(2,1)S(1)} %get-tuple-element.15), channel_id=1, source_target_pairs={{0,3},{1,0},{2,1},{3,2},{4,7},{5,4},{6,5},{7,6},{8,11},{9,8},{10,9... | collective-permute-start | bytes 344072 | tf_op jit(solution)/shard_map/ppermute | solution.py:257
  64.7 5.1 %collective-permute-start.24 = (bf16[8,2048]{1,0:T(8,128)(2,1)S(1)}, bf16[8,2048]{1,0:T(8,128)(2,1)S(1)}, u32[]{:S(2)}, u32[]{:S(2)}) collective-permute-start(bf16[8,2048]{1,0:T(8,128)(2,1)S(1)} %add_convert_fusion.4), channel_id=1, source_target_pairs={{0,24},{8,48},{16,40},{24,0},{32,56},{40,16},{48,8},{56,32},{1,25}... | collective-permute-start | bytes 98312 | tf_op jit(solution)/shard_map/ppermute | solution.py:262
  (4 other events, 23.8 us)
